TPU v7x, 32 devices: a whole 2x2x4 slice. The times are simulated.
32 devices in a mesh: region: 4 (over x, core), dom: 8 (over z, y).
Axes of the slice: x: 2, y: 2, z: 4, core: 2. Of those that a mesh axis runs over, the one named last changes fastest.
Arguments:
- params: float32 [59, 32768], P(None, ('region', 'dom')), may hold values from -6.4 to 6.4, as said below
- first_moment: float32 [59, 32768], P(None, ('region', 'dom')), may hold values from -0.3 to 0.3
- second_moment: float32 [59, 32768], P(None, ('region', 'dom')), may hold values from 0.0001 to 0.01
- piece_blocks: int32 [32, 32, 2], P(('region', 'dom')), may hold values from 0 to 9, all different within a row
- piece_live: int32 [32, 32], P(('region', 'dom')), may hold values from 1 to 2
- piece_owner: int32 [32, 32], P(('region', 'dom')), may hold values from 0 to 7, as said below
- piece_cell: int32 [32, 32], P(('region', 'dom')), may hold values from 0 to 63, as said below
- target: float32 [32, 8, 3, 256], P(('region', 'dom')), may hold values from 0 to 1
- background: float32 [3], replicated, may hold values from 0 to 1
Outputs:
- gradient: float32 [59, 32768], P(None, ('region', 'dom'))
- new_params: float32 [59, 32768], P(None, ('region', 'dom'))
- new_first: float32 [59, 32768], P(None, ('region', 'dom'))
- new_second: float32 [59, 32768], P(None, ('region', 'dom'))
Inputs may be any that keep to these rules, and one draw needn't show every extreme that they name: `params`: rows 0 to 2: z in [2, 4], x / z and y / z in [-1.6, 1.6]; rows 3 to 5 in [-0.9, 0.2]; row 6 in [0.5, 1.5]; rows 7 to 9 in [-1, 1]; row 10 in [-5.5, -1.8]; rows 11 to 58 in [-2, 2]. `piece_blocks`: the entries of one list are different pool blocks. `piece_owner`: each part sends at most 8 pieces to one owner; in every region some owner receives exactly 8 pieces from every part. `piece_cell`: the pieces that one owner receives have different cells.
All inputs are finite; a program needn't handle non-finite values.
Results may differ from a plain program's by a relative error of at most 0.0003.
Values sent between devices are 32-bit elements; how exact they have to be, the bound alone decides.
No kernel may reach another device: no remote copies, remote signals or barrier semaphores. Data moves between devices by JAX's collectives and lax.ppermute only.
A program may use at most 64 MiB of HBM per device.

v0:
```python
import jax
import jax.numpy as jnp
from jax import lax
from jax.sharding import PartitionSpec as P

PARAMS = 59
TSIDE = 16
WIN = 8
BLOCK = 128
MAXD = 8
PIECES = 32
PIX = 256
TILE_DEV = 8
CELLS = 64


harmonic_zero = 0.28209479177387814
harmonic_one = 0.4886025119029199
harmonic_two = (
    1.0925484305920792,
    -1.0925484305920792,
    0.31539156525252005,
    -1.0925484305920792,
    0.5462742152960396,
)
harmonic_three = (
    -0.5900435899266435,
    2.890611442640554,
    -0.4570457994644658,
    0.3731763325901154,
    -0.4570457994644658,
    1.445305721320277,
    -0.5900435899266435,
)
beta_one = 0.9
beta_two = 0.999
rate = 0.001
adam_step = 100
tiny = 1e-08
group_pieces = 8


def extended(block, sides, width):
    for axis, dim in sides:
        count = lax.axis_size(axis)
        forward = [(i, i + 1) for i in range(count - 1)]
        backward = [(target, source) for source, target in forward]
        low = lax.ppermute(
            lax.slice_in_dim(block, block.shape[dim] - width, None, axis=dim), axis, forward
        )
        high = lax.ppermute(lax.slice_in_dim(block, 0, width, axis=dim), axis, backward)
        block = jnp.concatenate([low, block, high], axis=dim)
    return block


def splat_table(block, screen_px):
    mean_x, mean_y, mean_z = (block[0], block[1], block[2])
    scales = jnp.exp(block[3:6])
    quat_raw = block[6:10]
    quat_norm = quat_raw / jnp.sqrt(jnp.sum(quat_raw * quat_raw, axis=0))
    quat_w, quat_x, quat_y, quat_z = (quat_norm[0], quat_norm[1], quat_norm[2], quat_norm[3])
    rotation = [
        [
            1 - 2 * (quat_y * quat_y + quat_z * quat_z),
            2 * (quat_x * quat_y - quat_w * quat_z),
            2 * (quat_x * quat_z + quat_w * quat_y),
        ],
        [
            2 * (quat_x * quat_y + quat_w * quat_z),
            1 - 2 * (quat_x * quat_x + quat_z * quat_z),
            2 * (quat_y * quat_z - quat_w * quat_x),
        ],
        [
            2 * (quat_x * quat_z - quat_w * quat_y),
            2 * (quat_y * quat_z + quat_w * quat_x),
            1 - 2 * (quat_x * quat_x + quat_y * quat_y),
        ],
    ]
    focal_px = 0.3125 * screen_px
    inv_z = 1.0 / mean_z
    jac_rows = [
        [focal_px * inv_z, 0.0 * inv_z, -focal_px * mean_x * inv_z * inv_z],
        [0.0 * inv_z, focal_px * inv_z, -focal_px * mean_y * inv_z * inv_z],
    ]
    projected = []
    for out_row in range(2):
        entries = []
        for out_col in range(3):
            acc_term = jac_rows[out_row][0] * rotation[0][out_col]
            acc_term = acc_term + jac_rows[out_row][1] * rotation[1][out_col]
            acc_term = acc_term + jac_rows[out_row][2] * rotation[2][out_col]
            entries.append(acc_term * scales[out_col])
        projected.append(entries)
    sigma_xx = (
        projected[0][0] * projected[0][0]
        + projected[0][1] * projected[0][1]
        + projected[0][2] * projected[0][2]
        + 0.3
    )
    sigma_xy = (
        projected[0][0] * projected[1][0]
        + projected[0][1] * projected[1][1]
        + projected[0][2] * projected[1][2]
    )
    sigma_yy = (
        projected[1][0] * projected[1][0]
        + projected[1][1] * projected[1][1]
        + projected[1][2] * projected[1][2]
        + 0.3
    )
    determinant = sigma_xx * sigma_yy - sigma_xy * sigma_xy
    conic_xx = sigma_yy / determinant
    conic_xy = -sigma_xy / determinant
    conic_yy = sigma_xx / determinant
    centre_u = 0.5 * screen_px + focal_px * mean_x * inv_z
    centre_v = 0.5 * screen_px + focal_px * mean_y * inv_z
    opacity = jax.nn.sigmoid(block[10])
    length = jnp.sqrt(mean_x * mean_x + mean_y * mean_y + mean_z * mean_z)
    dir_x, dir_y, dir_z = (mean_x / length, mean_y / length, mean_z / length)
    sq_x, sq_y, sq_z = (dir_x * dir_x, dir_y * dir_y, dir_z * dir_z)
    harmonics = [
        harmonic_zero + 0.0 * dir_x,
        -harmonic_one * dir_y,
        harmonic_one * dir_z,
        -harmonic_one * dir_x,
        harmonic_two[0] * dir_x * dir_y,
        harmonic_two[1] * dir_y * dir_z,
        harmonic_two[2] * (2 * sq_z - sq_x - sq_y),
        harmonic_two[3] * dir_x * dir_z,
        harmonic_two[4] * (sq_x - sq_y),
        harmonic_three[0] * dir_y * (3 * sq_x - sq_y),
        harmonic_three[1] * dir_x * dir_y * dir_z,
        harmonic_three[2] * dir_y * (4 * sq_z - sq_x - sq_y),
        harmonic_three[3] * dir_z * (2 * sq_z - 3 * sq_x - 3 * sq_y),
        harmonic_three[4] * dir_x * (4 * sq_z - sq_x - sq_y),
        harmonic_three[5] * dir_z * (sq_x - sq_y),
        harmonic_three[6] * dir_x * (sq_x - 3 * sq_y),
    ]
    basis = jnp.stack(harmonics, axis=0)
    coeffs = block[11:59].reshape(3, 16, block.shape[1])
    colour = jnp.maximum(jnp.sum(coeffs * basis[None], axis=1) + 0.5, 0.0)
    return jnp.stack(
        [
            centre_u,
            centre_v,
            conic_xx,
            conic_xy,
            conic_yy,
            opacity,
            colour[0],
            colour[1],
            colour[2],
        ],
        axis=0,
    )


def render_piece(chosen, slot_flags, tile_index):
    pixels = jnp.arange(TSIDE * TSIDE, dtype=jnp.int32)
    column = tile_index % WIN
    tile_row = tile_index // WIN
    pixel_x = (TSIDE * column + pixels % TSIDE).astype(chosen.dtype) + 0.5
    pixel_y = (TSIDE * tile_row + pixels // TSIDE).astype(chosen.dtype) + 0.5
    carry_log = jnp.zeros((TSIDE * TSIDE,), chosen.dtype)
    colour_sum = jnp.zeros((3, TSIDE * TSIDE), chosen.dtype)
    for slot_no in range(chosen.shape[1]):
        terms = chosen[:, slot_no]
        centre_u, centre_v, conic_xx, conic_xy, conic_yy, opacity = (
            terms[0],
            terms[1],
            terms[2],
            terms[3],
            terms[4],
            terms[5],
        )
        colour = terms[6:9]
        offset_x = pixel_x[None, :] - centre_u[:, None]
        offset_y = pixel_y[None, :] - centre_v[:, None]
        quadratic = (
            conic_xx[:, None] * offset_x * offset_x
            + 2.0 * conic_xy[:, None] * offset_x * offset_y
            + conic_yy[:, None] * offset_y * offset_y
        )
        alphas = (opacity * slot_flags[slot_no])[:, None] * jnp.exp(-0.5 * quadratic)
        log_keep = jnp.log1p(-alphas)
        before = carry_log[None, :] + jnp.cumsum(log_keep, axis=0) - log_keep
        weight = alphas * jnp.exp(before)
        colour_sum = colour_sum + jnp.dot(colour, weight, precision=lax.Precision.HIGHEST)
        carry_log = carry_log + jnp.sum(log_keep, axis=0)
    return jnp.concatenate([colour_sum, jnp.exp(carry_log)[None, :]], axis=0)


def render_listed(terms, present, blocks_row, live_row, tile_index):
    chosen = terms[:, blocks_row]
    slot_ids = jnp.arange(blocks_row.shape[0], dtype=jnp.int32)
    slot_flags = present[blocks_row] * (slot_ids < live_row).astype(present.dtype)
    return render_piece(chosen, slot_flags, tile_index)


def composite_grads(cell_grid, target_tiles, background):
    cell_grid = cell_grid.reshape(TILE_DEV, MAXD, 4, PIX)
    colours = cell_grid[:, :, :3]
    transmit = 1.0 - cell_grid[:, :, 3]
    in_front = jnp.ones((TILE_DEV, PIX), jnp.float32)
    composite = jnp.zeros((TILE_DEV, 3, PIX), jnp.float32)
    fronts = []
    for depth_slot in range(MAXD):
        fronts.append(in_front)
        composite = composite + in_front[:, None, :] * colours[:, depth_slot]
        in_front = in_front * transmit[:, depth_slot]
    composite = composite + in_front[:, None, :] * background[:, None]
    residual = composite - target_tiles
    behind = jnp.broadcast_to(background[None, :, None], (TILE_DEV, 3, PIX))
    cell_grads = [None] * MAXD
    for depth_slot in reversed(range(MAXD)):
        grad_trans = fronts[depth_slot] * jnp.sum(residual * behind, axis=1)
        grad_colour = fronts[depth_slot][:, None, :] * residual
        cell_grads[depth_slot] = jnp.concatenate([grad_colour, grad_trans[:, None, :]], axis=1)
        behind = colours[:, depth_slot] + transmit[:, depth_slot][:, None, :] * behind
    return jnp.stack(cell_grads, axis=1).reshape(CELLS, 4 * PIX)


def on_device(
    params,
    first_moment,
    second_moment,
    piece_blocks,
    piece_live,
    piece_owner,
    piece_cell,
    target,
    background,
):
    region_idx = lax.axis_index("region")
    regions = lax.axis_size("region")
    own_blocks = params.shape[1] // BLOCK
    screen_px = float(WIN * TSIDE)
    present = jnp.concatenate(
        [
            (region_idx > 0).astype(jnp.float32)[None],
            jnp.ones((own_blocks,), jnp.float32),
            (region_idx < regions - 1).astype(jnp.float32)[None],
        ]
    )

    def masked_terms(columns):
        terms = splat_table(columns, screen_px).reshape(9, own_blocks + 2, BLOCK)
        return jnp.where(present[None, :, None] > 0, terms, jnp.zeros_like(terms))

    pool_cols = extended(params, (("region", 1),), BLOCK)
    pool_terms, terms_pull = jax.vjp(masked_terms, pool_cols)
    group_count = PIECES // group_pieces
    grouped_blocks = piece_blocks[0].reshape(group_count, group_pieces, piece_blocks.shape[2])
    grouped_live = piece_live[0].reshape(group_count, group_pieces)
    grouped_tiles = jnp.arange(PIECES, dtype=jnp.int32).reshape(group_count, group_pieces)

    def render_group(terms, group_blocks, group_live, group_tiles):
        return jax.vmap(render_listed, in_axes=(None, None, 0, 0, 0))(
            terms, present, group_blocks, group_live, group_tiles
        )

    def forward_group(items):
        return render_group(pool_terms, items[0], items[1], items[2])

    rendered = lax.map(forward_group, (grouped_blocks, grouped_live, grouped_tiles)).reshape(
        PIECES, 4, PIX
    )
    outbound = jnp.concatenate([rendered[:, :3], 1.0 - rendered[:, 3:]], axis=1).reshape(
        PIECES, 4 * PIX
    )
    owner_ids = piece_owner[0]
    cell_ids = piece_cell[0]
    doms = lax.axis_size("dom")
    cell_range = jnp.arange(CELLS, dtype=jnp.int32)
    capacity = 2 * PIECES // doms
    dest_onehot = (owner_ids[:, None] == jnp.arange(doms, dtype=jnp.int32)[None, :]).astype(
        jnp.int32
    )
    earlier = jnp.cumsum(dest_onehot, axis=0) - dest_onehot
    position = jnp.sum(earlier * dest_onehot, axis=1)
    slot_index = owner_ids * capacity + position
    slot_onehot = (
        slot_index[:, None] == jnp.arange(doms * capacity, dtype=jnp.int32)[None, :]
    ).astype(jnp.float32)
    slot_rows = jnp.dot(slot_onehot.T, outbound, precision=lax.Precision.HIGHEST)
    slot_labels = (
        jnp.dot(slot_onehot.T, (cell_ids + 1).astype(jnp.float32), precision=lax.Precision.HIGHEST)
        - 1.0
    )
    arrived, arrived_labels = (
        lax.all_to_all(
            slot_rows.reshape(doms, capacity, 4 * PIX),
            "dom",
            split_axis=0,
            concat_axis=0,
            tiled=True,
        ),
        lax.all_to_all(
            slot_labels.reshape(doms, capacity), "dom", split_axis=0, concat_axis=0, tiled=True
        ),
    )
    arrived = arrived.reshape(doms * capacity, 4 * PIX)
    cell_onehot = (
        arrived_labels.reshape(doms * capacity)[:, None] == cell_range.astype(jnp.float32)[None, :]
    ).astype(jnp.float32)
    cell_grid = jnp.dot(cell_onehot.T, arrived, precision=lax.Precision.HIGHEST)
    grid_grads = composite_grads(cell_grid, target[0], background)
    slot_back = jnp.dot(cell_onehot, grid_grads, precision=lax.Precision.HIGHEST)
    returned = lax.all_to_all(
        slot_back.reshape(doms, capacity, 4 * PIX), "dom", split_axis=0, concat_axis=0, tiled=True
    )
    piece_grads = jnp.dot(
        slot_onehot, returned.reshape(doms * capacity, 4 * PIX), precision=lax.Precision.HIGHEST
    )
    cotangent = piece_grads.reshape(group_count, group_pieces, 4, PIX)

    def backward_group(running, items):
        group_blocks, group_live, group_tiles, group_cot = items
        _, pull_back = jax.vjp(
            lambda terms: render_group(terms, group_blocks, group_live, group_tiles), pool_terms
        )
        return (running + pull_back(group_cot)[0], None)

    term_grads, _ = lax.scan(
        backward_group,
        jnp.zeros_like(pool_terms),
        (grouped_blocks, grouped_live, grouped_tiles, cotangent),
    )
    inner_zero = jnp.zeros((PARAMS, (own_blocks - 2) * BLOCK), jnp.float32)
    pool_grads = terms_pull(term_grads)[0]
    rims = jnp.concatenate([pool_grads[:, :BLOCK], pool_grads[:, -BLOCK:]], axis=1)
    crossed = extended(rims, (("region", 1),), BLOCK)
    incoming = jnp.concatenate([crossed[:, :BLOCK], inner_zero, crossed[:, 3 * BLOCK :]], axis=1)
    gradient = pool_grads[:, BLOCK:-BLOCK] + incoming
    new_first = beta_one * first_moment + (1 - beta_one) * gradient
    new_second = beta_two * second_moment + (1 - beta_two) * gradient * gradient
    update = (
        new_first
        / (1 - beta_one**adam_step)
        / (jnp.sqrt(new_second / (1 - beta_two**adam_step)) + tiny)
    )
    new_params = params - rate * update
    return (gradient, new_params, new_first, new_second)


def solution(mesh):
    in_specs = (
        P(None, ("region", "dom")),
        P(None, ("region", "dom")),
        P(None, ("region", "dom")),
        P(("region", "dom"), None, None),
        P(("region", "dom"), None),
        P(("region", "dom"), None),
        P(("region", "dom"), None),
        P(("region", "dom"), None, None, None),
        P(),
    )
    out_specs = (
        P(None, ("region", "dom")),
        P(None, ("region", "dom")),
        P(None, ("region", "dom")),
        P(None, ("region", "dom")),
    )
    return jax.shard_map(
        on_device, mesh=mesh, in_specs=in_specs, out_specs=out_specs, check_vma=False
    )
```

profile of v0, /device:TPU:1, one launch (start us, length us, event | category | flops | bytes accessed | tf_op | source)
XLA Modules:
  0.0 230.2 jit_solution(16530438478424017581)
XLA Ops:
  4.5 6.4 %all-to-all-start = ((f32[8,1,8]{2,1,0:T(1,128)}), f32[8,1,8]{2,1,0:T(1,128)S(1)}, u32[]{:S(2)}, u32[]{:S(2)}) async-start(f32[8,1,8]{2,1,0:T(1,128)} %bitcast.65), calls=%async_computation | async-start | bytes 8192 | tf_op jit(solution)/shard_map/all_to_all | solution.py:298
  11.6 2.9 %collective-permute-start.1 = (f32[59,128]{1,0:T(8,128)S(1)}, f32[59,128]{1,0:T(8,128)S(1)}, u32[]{:S(2)}, u32[]{:S(2)}) collective-permute-start(f32[59,128]{1,0:T(8,128)S(1)} %get-tuple-element.668), channel_id=1, source_target_pairs={{8,0},{16,8},{24,16},{9,1},{17,9},{25,17},{10,2},{18,10},{26,18},{... | collective-permute-start | bytes 90632 | tf_op jit(solution)/shard_map/ppermute | solution.py:51
  14.5 3.0 %collective-permute-start = (f32[59,128]{1,0:T(8,128)S(1)}, f32[59,128]{1,0:T(8,128)S(1)}, u32[]{:S(2)}, u32[]{:S(2)}) collective-permute-start(f32[59,128]{1,0:T(8,128)S(1)} %get-tuple-element.669), channel_id=1, source_target_pairs={{0,8},{8,16},{16,24},{1,9},{9,17},{17,25},{2,10},{10,18},{18,26},{... | collective-permute-start | bytes 90632 | tf_op jit(solution)/shard_map/ppermute | solution.py:48
  20.8 46.0 %while.26 = (s32[]{:T(128)}, f32[4,8,4,256]{3,2,1,0:T(4,128)S(1)}, s32[4,8,2]{1,2,0:T(2,128)S(1)}, f32[9,10,128]{2,0,1:T(8,128)S(1)}, s32[4,8]{1,0:T(4,128)S(1)}...) while((s32[]{:T(128)}, f32[4,8,4,256]{3,2,1,0:T(4,128)S(1)}, s32[4,8,2]{1,2,0:T(2,128)S(1)}, ...), condition=%wide.region_9.10_spmd, body=%wide.region_4.9_spmd.sunk | while | flops 107774232 | bytes 5277265 | solution.py:265
  68.0 5.7 %all-to-all-start.1 = ((f32[8,8,1024]{2,1,0:T(8,128)}), f32[8,8,1024]{2,1,0:T(8,128)S(1)}, u32[]{:S(2)}, u32[]{:S(2)}) async-start(f32[8,8,1024]{2,1,0:T(8,128)} %fusion.129), calls=%async_computation.1 | async-start | bytes 524288 | tf_op jit(solution)/shard_map/all_to_all | solution.py:291
  75.0 8.0 %all-to-all-done.1 = f32[8,8,1024]{2,1,0:T(8,128)S(1)} async-done(((f32[8,8,1024]{2,1,0:T(8,128)}), f32[8,8,1024]{2,1,0:T(8,128)S(1)}, u32[]{:S(2)}, u32[]{:S(2)}) %all-to-all-start.1) | async-done | bytes 262176 | tf_op jit(solution)/shard_map/all_to_all | solution.py:291
  86.3 3.6 %all-to-all-start.2 = ((f32[8,8,1024]{2,1,0:T(8,128)}), f32[8,8,1024]{2,1,0:T(8,128)S(1)}, u32[]{:S(2)}, u32[]{:S(2)}) async-start(f32[8,8,1024]{2,1,0:T(8,128)} %fusion.132), calls=%async_computation.2 | async-start | bytes 524288 | tf_op jit(solution)/shard_map/all_to_all | solution.py:309
  90.7 6.8 %all-to-all-done.2 = f32[8,8,1024]{2,1,0:T(8,128)S(1)} async-done(((f32[8,8,1024]{2,1,0:T(8,128)}), f32[8,8,1024]{2,1,0:T(8,128)S(1)}, u32[]{:S(2)}, u32[]{:S(2)}) %all-to-all-start.2) | async-done | bytes 262176 | tf_op jit(solution)/shard_map/all_to_all | solution.py:309
  97.8 122.0 %while.27 = (s32[]{:T(128)}, f32[9,10,128]{2,0,1:T(8,128)S(1)}, s32[4,8,2]{1,2,0:T(2,128)S(1)}, f32[4,8,4,256]{3,1,2,0:T(8,128)S(1)}, f32[9,10,128]{2,0,1:T(8,12...) while((s32[]{:T(128)}, f32[9,10,128]{2,0,1:T(8,128)S(1)}, ...), condition=%wide.region_39.40_spmd, body=%wide.region_18.39_spmd.sunk | while | flops 220889376 | bytes 28468952 | solution.py:324
  104.0 4.2 %fusion.260 = (f32[8,256]{1,0:T(8,128)S(1)}, f32[8,256]{1,0:T(8,128)S(1)}, f32[8,128,256]{2,1,0:T(8,128)S(1)}, f32[8,128,256]{2,1,0:T(8,128)S(1)}, f32[8,128,256]{2,1,0:T(8,128)S(1)}) fusion(f32[8,128]{1,0:T(8,128)S(1)} %bitcast.550, f32[8,128]{1,0:T(8,128)S(1)} %bitcast.546, f32[8,256]{1,0:T(8,128)S(1)} %convert_add_fusion.10, ...), kind=kOutput, calls=%fused_computation.167.clone.1 | convolution fusion | flops 17559552 | bytes 4325376 | tf_op jit(solution)/shard_map/while/body/eval_jaxpr/transpose(jvp(vmap()))/dot_general | solution.py:188
  111.3 2.5 %fusion.265 = f32[8,128,256]{2,0,1:T(8,128)S(1)} fusion(f32[8,128,256]{2,1,0:T(8,128)S(1)} %get-tuple-element.915), kind=kOutput, calls=%fused_computation.136.clone.1 | output fusion | flops 33292288 | bytes 2097152 | tf_op jit(solution)/shard_map/while/body/eval_jaxpr/transpose(jvp(vmap(jit(cumsum))))/reduce_window_sum | solution.py:186
  113.8 2.7 %fusion.262 = (f32[8,256]{1,0:T(8,128)S(1)}, f32[8,128,256]{2,1,0:T(8,128)S(1)}, f32[8,128,256]{2,1,0:T(8,128)S(1)}) fusion(f32[8,128,256]{2,0,1:T(8,128)S(1)} %fusion.261, f32[8,256]{1,0:T(8,128)S(1)} %get-tuple-element.909, f32[8,128]{1,0:T(8,128)S(1)} %bitcast.552, f32[8,128]{1,0:T(8,128)S(1)} %bitcast.548, ...), kind=kOutput, calls=%fused_computation.537.clone.1 | convolution fusion | flops 14153728 | bytes 3252224 | tf_op jit(solution)/shard_map/while/body/eval_jaxpr/transpose(jvp(vmap()))/dot_general | solution.py:188
  116.5 2.5 %fusion.263 = f32[8,128,256]{2,0,1:T(8,128)S(1)} fusion(f32[8,128,256]{2,1,0:T(8,128)S(1)} %get-tuple-element.910), kind=kOutput, calls=%fused_computation.146.clone.1 | output fusion | flops 33292288 | bytes 2097152 | tf_op jit(solution)/shard_map/while/body/eval_jaxpr/transpose(jvp(vmap(jit(cumsum))))/reduce_window_sum | solution.py:186
  119.1 7.6 %fusion.266 = (f32[8,128]{1,0:T(8,128)S(1)}, f32[8,128]{1,0:T(8,128)S(1)}, f32[8,128]{1,0:T(8,128)S(1)}, f32[8,128]{1,0:T(8,128)S(1)}, f32[8,128]{1,0:T(8,128)S(...) fusion(f32[8,128]{1,0:T(8,128)S(1)} %bitcast.549, ...), kind=kLoop, calls=%fused_computation.122.clone.1 | loop fusion | flops 25415680 | bytes 7479296 | tf_op jit(solution)/shard_map/while/body/eval_jaxpr/transpose(jvp(vmap()))/reduce_sum | solution.py:182
  134.5 4.2 %fusion.260 = (f32[8,256]{1,0:T(8,128)S(1)}, f32[8,256]{1,0:T(8,128)S(1)}, f32[8,128,256]{2,1,0:T(8,128)S(1)}, f32[8,128,256]{2,1,0:T(8,128)S(1)}, f32[8,128,256]{2,1,0:T(8,128)S(1)}) fusion(f32[8,128]{1,0:T(8,128)S(1)} %bitcast.550, f32[8,128]{1,0:T(8,128)S(1)} %bitcast.546, f32[8,256]{1,0:T(8,128)S(1)} %convert_add_fusion.10, ...), kind=kOutput, calls=%fused_computation.167.clone.1 | convolution fusion | flops 17559552 | bytes 4325376 | tf_op jit(solution)/shard_map/while/body/eval_jaxpr/transpose(jvp(vmap()))/dot_general | solution.py:188
  141.8 2.5 %fusion.265 = f32[8,128,256]{2,0,1:T(8,128)S(1)} fusion(f32[8,128,256]{2,1,0:T(8,128)S(1)} %get-tuple-element.915), kind=kOutput, calls=%fused_computation.136.clone.1 | output fusion | flops 33292288 | bytes 2097152 | tf_op jit(solution)/shard_map/while/body/eval_jaxpr/transpose(jvp(vmap(jit(cumsum))))/reduce_window_sum | solution.py:186
  144.3 2.7 %fusion.262 = (f32[8,256]{1,0:T(8,128)S(1)}, f32[8,128,256]{2,1,0:T(8,128)S(1)}, f32[8,128,256]{2,1,0:T(8,128)S(1)}) fusion(f32[8,128,256]{2,0,1:T(8,128)S(1)} %fusion.261, f32[8,256]{1,0:T(8,128)S(1)} %get-tuple-element.909, f32[8,128]{1,0:T(8,128)S(1)} %bitcast.552, f32[8,128]{1,0:T(8,128)S(1)} %bitcast.548, ...), kind=kOutput, calls=%fused_computation.537.clone.1 | convolution fusion | flops 14153728 | bytes 3252224 | tf_op jit(solution)/shard_map/while/body/eval_jaxpr/transpose(jvp(vmap()))/dot_general | solution.py:188
  147.1 2.5 %fusion.263 = f32[8,128,256]{2,0,1:T(8,128)S(1)} fusion(f32[8,128,256]{2,1,0:T(8,128)S(1)} %get-tuple-element.910), kind=kOutput, calls=%fused_computation.146.clone.1 | output fusion | flops 33292288 | bytes 2097152 | tf_op jit(solution)/shard_map/while/body/eval_jaxpr/transpose(jvp(vmap(jit(cumsum))))/reduce_window_sum | solution.py:186
  149.6 7.6 %fusion.266 = (f32[8,128]{1,0:T(8,128)S(1)}, f32[8,128]{1,0:T(8,128)S(1)}, f32[8,128]{1,0:T(8,128)S(1)}, f32[8,128]{1,0:T(8,128)S(1)}, f32[8,128]{1,0:T(8,128)S(...) fusion(f32[8,128]{1,0:T(8,128)S(1)} %bitcast.549, ...), kind=kLoop, calls=%fused_computation.122.clone.1 | loop fusion | flops 25415680 | bytes 7479296 | tf_op jit(solution)/shard_map/while/body/eval_jaxpr/transpose(jvp(vmap()))/reduce_sum | solution.py:182
  165.0 4.2 %fusion.260 = (f32[8,256]{1,0:T(8,128)S(1)}, f32[8,256]{1,0:T(8,128)S(1)}, f32[8,128,256]{2,1,0:T(8,128)S(1)}, f32[8,128,256]{2,1,0:T(8,128)S(1)}, f32[8,128,256]{2,1,0:T(8,128)S(1)}) fusion(f32[8,128]{1,0:T(8,128)S(1)} %bitcast.550, f32[8,128]{1,0:T(8,128)S(1)} %bitcast.546, f32[8,256]{1,0:T(8,128)S(1)} %convert_add_fusion.10, ...), kind=kOutput, calls=%fused_computation.167.clone.1 | convolution fusion | flops 17559552 | bytes 4325376 | tf_op jit(solution)/shard_map/while/body/eval_jaxpr/transpose(jvp(vmap()))/dot_general | solution.py:188
  172.3 2.5 %fusion.265 = f32[8,128,256]{2,0,1:T(8,128)S(1)} fusion(f32[8,128,256]{2,1,0:T(8,128)S(1)} %get-tuple-element.915), kind=kOutput, calls=%fused_computation.136.clone.1 | output fusion | flops 33292288 | bytes 2097152 | tf_op jit(solution)/shard_map/while/body/eval_jaxpr/transpose(jvp(vmap(jit(cumsum))))/reduce_window_sum | solution.py:186
  174.8 2.7 %fusion.262 = (f32[8,256]{1,0:T(8,128)S(1)}, f32[8,128,256]{2,1,0:T(8,128)S(1)}, f32[8,128,256]{2,1,0:T(8,128)S(1)}) fusion(f32[8,128,256]{2,0,1:T(8,128)S(1)} %fusion.261, f32[8,256]{1,0:T(8,128)S(1)} %get-tuple-element.909, f32[8,128]{1,0:T(8,128)S(1)} %bitcast.552, f32[8,128]{1,0:T(8,128)S(1)} %bitcast.548, ...), kind=kOutput, calls=%fused_computation.537.clone.1 | convolution fusion | flops 14153728 | bytes 3252224 | tf_op jit(solution)/shard_map/while/body/eval_jaxpr/transpose(jvp(vmap()))/dot_general | solution.py:188
  177.6 2.5 %fusion.263 = f32[8,128,256]{2,0,1:T(8,128)S(1)} fusion(f32[8,128,256]{2,1,0:T(8,128)S(1)} %get-tuple-element.910), kind=kOutput, calls=%fused_computation.146.clone.1 | output fusion | flops 33292288 | bytes 2097152 | tf_op jit(solution)/shard_map/while/body/eval_jaxpr/transpose(jvp(vmap(jit(cumsum))))/reduce_window_sum | solution.py:186
  180.1 7.6 %fusion.266 = (f32[8,128]{1,0:T(8,128)S(1)}, f32[8,128]{1,0:T(8,128)S(1)}, f32[8,128]{1,0:T(8,128)S(1)}, f32[8,128]{1,0:T(8,128)S(1)}, f32[8,128]{1,0:T(8,128)S(...) fusion(f32[8,128]{1,0:T(8,128)S(1)} %bitcast.549, ...), kind=kLoop, calls=%fused_computation.122.clone.1 | loop fusion | flops 25415680 | bytes 7479296 | tf_op jit(solution)/shard_map/while/body/eval_jaxpr/transpose(jvp(vmap()))/reduce_sum | solution.py:182
  195.5 4.2 %fusion.260 = (f32[8,256]{1,0:T(8,128)S(1)}, f32[8,256]{1,0:T(8,128)S(1)}, f32[8,128,256]{2,1,0:T(8,128)S(1)}, f32[8,128,256]{2,1,0:T(8,128)S(1)}, f32[8,128,256]{2,1,0:T(8,128)S(1)}) fusion(f32[8,128]{1,0:T(8,128)S(1)} %bitcast.550, f32[8,128]{1,0:T(8,128)S(1)} %bitcast.546, f32[8,256]{1,0:T(8,128)S(1)} %convert_add_fusion.10, ...), kind=kOutput, calls=%fused_computation.167.clone.1 | convolution fusion | flops 17559552 | bytes 4325376 | tf_op jit(solution)/shard_map/while/body/eval_jaxpr/transpose(jvp(vmap()))/dot_general | solution.py:188
  200.4 2.4 %fusion.268 = f32[8,3,128]{2,1,0:T(4,128)S(1)} fusion(f32[8,128,256]{2,0,1:T(8,128)S(1)} %fusion.261, f32[8,256]{1,0:T(8,128)S(1)} %get-tuple-element.909, f32[8,128]{1,0:T(8,128)S(1)} %bitcast.551, f32[8,128]{1,0:T(8,128)S(1)} %bitcast.547, f32[8,256]{1,0:T(8,128)S(1)} %convert_add_fusion.10, f32[8,128]{1,0:T(8,128)S(1)} %bitcast.543, ...), kind=kOutput, calls=%fused_computation.161.clone.1 | convolution fusion | flops 13631488 | bytes 1142784 | tf_op jit(solution)/shard_map/while/body/eval_jaxpr/transpose(jvp(vmap()))/dot_general | solution.py:188
  202.8 2.5 %fusion.265 = f32[8,128,256]{2,0,1:T(8,128)S(1)} fusion(f32[8,128,256]{2,1,0:T(8,128)S(1)} %get-tuple-element.915), kind=kOutput, calls=%fused_computation.136.clone.1 | output fusion | flops 33292288 | bytes 2097152 | tf_op jit(solution)/shard_map/while/body/eval_jaxpr/transpose(jvp(vmap(jit(cumsum))))/reduce_window_sum | solution.py:186
  205.3 2.7 %fusion.262 = (f32[8,256]{1,0:T(8,128)S(1)}, f32[8,128,256]{2,1,0:T(8,128)S(1)}, f32[8,128,256]{2,1,0:T(8,128)S(1)}) fusion(f32[8,128,256]{2,0,1:T(8,128)S(1)} %fusion.261, f32[8,256]{1,0:T(8,128)S(1)} %get-tuple-element.909, f32[8,128]{1,0:T(8,128)S(1)} %bitcast.552, f32[8,128]{1,0:T(8,128)S(1)} %bitcast.548, ...), kind=kOutput, calls=%fused_computation.537.clone.1 | convolution fusion | flops 14153728 | bytes 3252224 | tf_op jit(solution)/shard_map/while/body/eval_jaxpr/transpose(jvp(vmap()))/dot_general | solution.py:188
  208.1 2.5 %fusion.263 = f32[8,128,256]{2,0,1:T(8,128)S(1)} fusion(f32[8,128,256]{2,1,0:T(8,128)S(1)} %get-tuple-element.910), kind=kOutput, calls=%fused_computation.146.clone.1 | output fusion | flops 33292288 | bytes 2097152 | tf_op jit(solution)/shard_map/while/body/eval_jaxpr/transpose(jvp(vmap(jit(cumsum))))/reduce_window_sum | solution.py:186
  210.6 7.6 %fusion.266 = (f32[8,128]{1,0:T(8,128)S(1)}, f32[8,128]{1,0:T(8,128)S(1)}, f32[8,128]{1,0:T(8,128)S(1)}, f32[8,128]{1,0:T(8,128)S(1)}, f32[8,128]{1,0:T(8,128)S(...) fusion(f32[8,128]{1,0:T(8,128)S(1)} %bitcast.549, ...), kind=kLoop, calls=%fused_computation.122.clone.1 | loop fusion | flops 25415680 | bytes 7479296 | tf_op jit(solution)/shard_map/while/body/eval_jaxpr/transpose(jvp(vmap()))/reduce_sum | solution.py:182
  221.1 2.6 %collective-permute-start.2 = (f32[59,128]{1,0:T(8,128)S(1)}, f32[59,128]{1,0:T(8,128)S(1)}, u32[]{:S(2)}, u32[]{:S(2)}) collective-permute-start(f32[59,128]{1,0:T(8,128)S(1)} %get-tuple-element.658), channel_id=1, source_target_pairs={{0,8},{8,16},{16,24},{1,9},{9,17},{17,25},{2,10},{10,18},{18,26},{... | collective-permute-start | bytes 90632 | tf_op jit(solution)/shard_map/ppermute | solution.py:48
  223.8 2.9 %collective-permute-start.3 = (f32[59,128]{1,0:T(8,128)S(1)}, f32[59,128]{1,0:T(8,128)S(1)}, u32[]{:S(2)}, u32[]{:S(2)}) collective-permute-start(f32[59,128]{1,0:T(8,128)S(1)} %get-tuple-element.659), channel_id=1, source_target_pairs={{8,0},{16,8},{24,16},{9,1},{17,9},{25,17},{10,2},{18,10},{26,18},{... | collective-permute-start | bytes 90632 | tf_op jit(solution)/shard_map/ppermute | solution.py:51
  (476 shorter events, 104.8 us)
Async XLA Ops:
  0.6 19.1 %copy-start = (f32[59,1024]{1,0:T(8,128)S(1)}, f32[59,1024]{1,0:T(8,128)}, u32[]{:S(2)}) copy-start(f32[59,1024]{1,0:T(8,128)} %param.13) | copy-start | bytes 724996
  4.5 63.5 %all-to-all-start = ((f32[8,1,8]{2,1,0:T(1,128)}), f32[8,1,8]{2,1,0:T(1,128)S(1)}, u32[]{:S(2)}, u32[]{:S(2)}) async-start(f32[8,1,8]{2,1,0:T(1,128)} %bitcast.65), calls=%async_computation | async-start | bytes 8192 | tf_op jit(solution)/shard_map/all_to_all | solution.py:298
  11.6 8.2 %collective-permute-start.1 = (f32[59,128]{1,0:T(8,128)S(1)}, f32[59,128]{1,0:T(8,128)S(1)}, u32[]{:S(2)}, u32[]{:S(2)}) collective-permute-start(f32[59,128]{1,0:T(8,128)S(1)} %get-tuple-element.668), channel_id=1, source_target_pairs={{8,0},{16,8},{24,16},{9,1},{17,9},{25,17},{10,2},{18,10},{26,18},{... | collective-permute-start | bytes 90632 | tf_op jit(solution)/shard_map/ppermute | solution.py:51
  14.5 5.3 %collective-permute-start = (f32[59,128]{1,0:T(8,128)S(1)}, f32[59,128]{1,0:T(8,128)S(1)}, u32[]{:S(2)}, u32[]{:S(2)}) collective-permute-start(f32[59,128]{1,0:T(8,128)S(1)} %get-tuple-element.669), channel_id=1, source_target_pairs={{0,8},{8,16},{16,24},{1,9},{9,17},{17,25},{2,10},{10,18},{18,26},{... | collective-permute-start | bytes 90632 | tf_op jit(solution)/shard_map/ppermute | solution.py:48
  17.6 0.7 copy-start.7
  18.9 0.7 copy-start.6
  68.0 15.0 %all-to-all-start.1 = ((f32[8,8,1024]{2,1,0:T(8,128)}), f32[8,8,1024]{2,1,0:T(8,128)S(1)}, u32[]{:S(2)}, u32[]{:S(2)}) async-start(f32[8,8,1024]{2,1,0:T(8,128)} %fusion.129), calls=%async_computation.1 | async-start | bytes 524288 | tf_op jit(solution)/shard_map/all_to_all | solution.py:291
  83.7 0.7 copy-start.3
  83.7 0.7 copy-start.4
  86.3 11.2 %all-to-all-start.2 = ((f32[8,8,1024]{2,1,0:T(8,128)}), f32[8,8,1024]{2,1,0:T(8,128)S(1)}, u32[]{:S(2)}, u32[]{:S(2)}) async-start(f32[8,8,1024]{2,1,0:T(8,128)} %fusion.132), calls=%async_computation.2 | async-start | bytes 524288 | tf_op jit(solution)/shard_map/all_to_all | solution.py:309
  89.9 0.7 copy-start.5
  221.1 5.6 %collective-permute-start.2 = (f32[59,128]{1,0:T(8,128)S(1)}, f32[59,128]{1,0:T(8,128)S(1)}, u32[]{:S(2)}, u32[]{:S(2)}) collective-permute-start(f32[59,128]{1,0:T(8,128)S(1)} %get-tuple-element.658), channel_id=1, source_target_pairs={{0,8},{8,16},{16,24},{1,9},{9,17},{17,25},{2,10},{10,18},{18,26},{... | collective-permute-start | bytes 90632 | tf_op jit(solution)/shard_map/ppermute | solution.py:48
  223.8 5.4 %copy-start.1 = (f32[59,1024]{1,0:T(8,128)S(1)}, f32[59,1024]{1,0:T(8,128)}, u32[]{:S(2)}) copy-start(f32[59,1024]{1,0:T(8,128)} %param.14) | copy-start | bytes 724996
  223.8 5.4 %copy-start.2 = (f32[59,1024]{1,0:T(8,128)S(1)}, f32[59,1024]{1,0:T(8,128)}, u32[]{:S(2)}) copy-start(f32[59,1024]{1,0:T(8,128)} %param.15) | copy-start | bytes 724996
  223.8 5.4 %collective-permute-start.3 = (f32[59,128]{1,0:T(8,128)S(1)}, f32[59,128]{1,0:T(8,128)S(1)}, u32[]{:S(2)}, u32[]{:S(2)}) collective-permute-start(f32[59,128]{1,0:T(8,128)S(1)} %get-tuple-element.659), channel_id=1, source_target_pairs={{8,0},{16,8},{24,16},{9,1},{17,9},{25,17},{10,2},{18,10},{26,18},{... | collective-permute-start | bytes 90632 | tf_op jit(solution)/shard_map/ppermute | solution.py:51
where the time goes:
time: 231 us; the launch traced here: 230 us
  other arithmetic  101 us (44%)
  matrix products  57.1 us (25%)
  starting transfers between devices  27.1 us (12%)
  local copies, waits for them, and re-layouts  24.8 us (11%)
  waiting for transfers between devices  17.2 us (7%)
    dot_general x24, matrix products, render_piece(): jnp.dot(colour, weight, precision=lax.Precision.HIGHEST)  53.7 us
    another operation x24, other arithmetic, render_piece(): before = carry_log[None, :] + jnp.cumsum(log_keep, axis=0) - log_keep  42.2 us
    reduce_sum x4, other arithmetic, render_piece(): conic_yy[:, None] * offset_y * offset_y  30.2 us
    reduce_sum x4, other arithmetic, render_piece(): carry_log = carry_log + jnp.sum(log_keep, axis=0)  8.21 us
    all_to_all x1, waiting for transfers between devices, on_device(): lax.all_to_all(slot_rows.reshape(doms, capacity, 4 * PIX), 'dom', split_a...  8.02 us
    all_to_all x1, waiting for transfers between devices, on_device(): lax.all_to_all(slot_back.reshape(doms, capacity, 4 * PIX), 'dom', split_a...  6.78 us
    all_to_all x1, starting transfers between devices, on_device(): lax.all_to_all(slot_labels.reshape(doms, capacity), 'dom', split_axis=0,...  6.37 us
    gather x16, local copies, waits for them, and re-layouts, render_listed(): present[blocks_row] * (slot_ids < live_row).astype(present.dtype)  5.91 us
  transfers between devices with their start and end apart: 7, of which 3 were waited for; matrix products, arithmetic and copies ran while one was open for 22% of the time, Pallas kernels for 0%

commit v1 on v0

v1 whole, which is shorter than its diff:
```python
import math

import numpy as np
import jax
import jax.numpy as jnp
from jax import lax
from jax.experimental import pallas as pl
from jax.experimental.pallas import tpu as pltpu
from jax.sharding import PartitionSpec as P

PARAMS = 59
TSIDE = 16
WIN = 8
BLOCK = 128
MAXD = 8
PIX = 256

harmonic_zero = 0.28209479177387814
harmonic_one = 0.4886025119029199
harmonic_two = (
    1.0925484305920792,
    -1.0925484305920792,
    0.31539156525252005,
    -1.0925484305920792,
    0.5462742152960396,
)
harmonic_three = (
    -0.5900435899266435,
    2.890611442640554,
    -0.4570457994644658,
    0.3731763325901154,
    -0.4570457994644658,
    1.445305721320277,
    -0.5900435899266435,
)
beta_one = 0.9
beta_two = 0.999
rate = 0.001
adam_step = 100
tiny = 1e-08
log2_e = math.log2(math.e)
ln_2 = math.log(2.0)

LANES = 128
SUBL = 8
ROWS = BLOCK // SUBL
GROUP = LANES // 4
BASIS = 16
KE = 3 * BASIS
KC = 6 * SUBL
SLOTS = 16
f32 = jnp.float32
bf16 = jnp.bfloat16


def splat_rows(rows):
    mean_x, mean_y, mean_z = rows[0], rows[1], rows[2]
    scales = [jnp.exp(rows[3]), jnp.exp(rows[4]), jnp.exp(rows[5])]
    norm_sq = rows[6] * rows[6] + rows[7] * rows[7] + rows[8] * rows[8] + rows[9] * rows[9]
    inv_norm = 1.0 / jnp.sqrt(norm_sq)
    quat_w, quat_x, quat_y, quat_z = [rows[6 + i] * inv_norm for i in range(4)]
    rotation = [
        [
            1 - 2 * (quat_y * quat_y + quat_z * quat_z),
            2 * (quat_x * quat_y - quat_w * quat_z),
            2 * (quat_x * quat_z + quat_w * quat_y),
        ],
        [
            2 * (quat_x * quat_y + quat_w * quat_z),
            1 - 2 * (quat_x * quat_x + quat_z * quat_z),
            2 * (quat_y * quat_z - quat_w * quat_x),
        ],
        [
            2 * (quat_x * quat_z - quat_w * quat_y),
            2 * (quat_y * quat_z + quat_w * quat_x),
            1 - 2 * (quat_x * quat_x + quat_y * quat_y),
        ],
    ]
    focal_px = 0.3125 * float(WIN * TSIDE)
    inv_z = 1.0 / mean_z
    scale_z = focal_px * inv_z
    off_u = scale_z * mean_x
    off_v = scale_z * mean_y
    slope_u = off_u * inv_z
    slope_v = off_v * inv_z
    proj_u = [(scale_z * rotation[0][i] - slope_u * rotation[2][i]) * scales[i] for i in range(3)]
    proj_v = [(scale_z * rotation[1][i] - slope_v * rotation[2][i]) * scales[i] for i in range(3)]
    sigma_xx = proj_u[0] * proj_u[0] + proj_u[1] * proj_u[1] + proj_u[2] * proj_u[2] + 0.3
    sigma_xy = proj_u[0] * proj_v[0] + proj_u[1] * proj_v[1] + proj_u[2] * proj_v[2]
    sigma_yy = proj_v[0] * proj_v[0] + proj_v[1] * proj_v[1] + proj_v[2] * proj_v[2] + 0.3
    determinant = sigma_xx * sigma_yy - sigma_xy * sigma_xy
    inv_det = log2_e / determinant
    con_xx = sigma_yy * inv_det
    con_xy = -sigma_xy * inv_det
    con_yy = sigma_xx * inv_det
    lin_x = con_xx * off_u + con_xy * off_v
    lin_y = con_xy * off_u + con_yy * off_v
    logit = rows[10]
    log_opacity = (logit - jnp.log(1.0 + jnp.exp(logit))) * log2_e
    const = log_opacity - 0.5 * (lin_x * off_u + lin_y * off_v)
    coefs = [const, lin_x, lin_y, -0.5 * con_xx, -con_xy, -0.5 * con_yy]
    inv_len = 1.0 / jnp.sqrt(mean_x * mean_x + mean_y * mean_y + mean_z * mean_z)
    dir_x, dir_y, dir_z = mean_x * inv_len, mean_y * inv_len, mean_z * inv_len
    sq_x, sq_y, sq_z = dir_x * dir_x, dir_y * dir_y, dir_z * dir_z
    harmonics = [
        None,
        -harmonic_one * dir_y,
        harmonic_one * dir_z,
        -harmonic_one * dir_x,
        harmonic_two[0] * dir_x * dir_y,
        harmonic_two[1] * dir_y * dir_z,
        harmonic_two[2] * (2 * sq_z - sq_x - sq_y),
        harmonic_two[3] * dir_x * dir_z,
        harmonic_two[4] * (sq_x - sq_y),
        harmonic_three[0] * dir_y * (3 * sq_x - sq_y),
        harmonic_three[1] * dir_x * dir_y * dir_z,
        harmonic_three[2] * dir_y * (4 * sq_z - sq_x - sq_y),
        harmonic_three[3] * dir_z * (2 * sq_z - 3 * sq_x - 3 * sq_y),
        harmonic_three[4] * dir_x * (4 * sq_z - sq_x - sq_y),
        harmonic_three[5] * dir_z * (sq_x - sq_y),
        harmonic_three[6] * dir_x * (sq_x - 3 * sq_y),
    ]
    colours = []
    for colour_no in range(3):
        base = 11 + 16 * colour_no
        total = rows[base] * harmonic_zero
        for k in range(1, 16):
            total = total + rows[base + k] * harmonics[k]
        colours.append(jnp.maximum(total + 0.5, 0.0))
    return coefs, colours


def split3(value):
    high = value.astype(bf16).astype(f32)
    rest = value - high
    middle = rest.astype(bf16).astype(f32)
    return high, middle, rest - middle


def split2(value):
    high = value.astype(bf16)
    return high, (value - high.astype(f32)).astype(bf16)


def pixel_basis(pieces):
    tiles = np.arange(pieces)[:, None]
    pixels = np.arange(PIX)[None, :]
    half = WIN * TSIDE / 2
    pos_x = TSIDE * (tiles % WIN) + pixels % TSIDE + 0.5 - half
    pos_y = TSIDE * (tiles // WIN) + pixels // TSIDE + 0.5 - half
    rows = [np.ones_like(pos_x), pos_x, pos_y]
    for product in (pos_x * pos_x, pos_x * pos_y, pos_y * pos_y):
        high = product.astype(bf16).astype(np.float64)
        rows += [high, product - high]
    table = np.zeros((pieces, BASIS, PIX))
    for row_no, row in enumerate(rows):
        table[:, row_no] = row
    return table.astype(bf16)


def basis_coefs(coefs):
    return [coefs[i] for i in (0, 1, 2, 3, 3, 4, 4, 5, 5)]


def lane_order(shape, inverse):
    lane = lax.broadcasted_iota(jnp.int32, shape, 1)
    if inverse:
        return (lane % ROWS) * SUBL + lane // ROWS
    return (lane % SUBL) * ROWS + lane // SUBL


def prefix_product(total):
    sub = lax.broadcasted_iota(jnp.int32, total.shape, 0)
    run = total
    for step in (1, 2, 4):
        run = jnp.where(sub >= step, run * pltpu.roll(run, step, 0), run)
    before = jnp.where(sub >= 1, pltpu.roll(run, 1, 0), 1.0)
    return before, run[SUBL - 1 :]


def suffix_affine(total, keep, behind):
    sub = lax.broadcasted_iota(jnp.int32, total.shape, 0)
    value, gain = total, keep
    for step in (1, 2, 4):
        inside = sub < SUBL - step
        next_value = jnp.where(inside, pltpu.roll(value, SUBL - step, 0), 0.0)
        next_gain = jnp.where(inside, pltpu.roll(gain, SUBL - step, 0), 1.0)
        value = value + gain * next_value
        gain = gain * next_gain
    whole = value + gain * behind
    after = jnp.where(sub < SUBL - 1, pltpu.roll(whole, SUBL - 1, 0), behind)
    return after, whole[:1]


def slot_blocks(blocks_ref, live_ref, piece, own_blocks):
    found = []
    for slot in range(2):
        block = blocks_ref[piece, slot]
        index = jnp.where(
            block == 0, own_blocks, jnp.where(block > own_blocks, own_blocks + 1, block - 1)
        )
        found.append(jnp.where(slot < live_ref[piece], index, own_blocks + 2))
    return found


def forward_kernel(
    blocks_ref,
    live_ref,
    place_ref,
    params_ref,
    low_ref,
    high_ref,
    target_ref,
    labels_ref,
    basis_ref,
    out_ref,
    tab_e_ref,
    tab_c_ref,
    rows_ref,
    stage_e_ref,
    stage_c_ref,
    stage_t_ref,
    colour_ref,
    result_ref,
):
    doms, pieces = out_ref.shape[0], basis_ref.shape[0]
    own_blocks = params_ref.shape[1] // BLOCK
    region_idx, regions = place_ref[0], place_ref[1]
    for block in range(own_blocks):
        rows_ref[pl.ds(block, PARAMS, stride=SLOTS), :] = params_ref[
            :, block * BLOCK : (block + 1) * BLOCK
        ]
    rows_ref[pl.ds(own_blocks, PARAMS, stride=SLOTS), :] = low_ref[...]
    rows_ref[pl.ds(own_blocks + 1, PARAMS, stride=SLOTS), :] = high_ref[...]
    coefs, colours = splat_rows(
        [rows_ref[i * SLOTS : (i + 1) * SLOTS, :] for i in range(PARAMS)]
    )
    shape = (SLOTS, LANES)
    slot = lax.broadcasted_iota(jnp.int32, shape, 0)
    present = (
        (slot < own_blocks)
        | ((slot == own_blocks) & (region_idx > 0))
        | ((slot == own_blocks + 1) & (region_idx < regions - 1))
    )
    order = lane_order(shape, False)

    def settled(value, absent):
        return jnp.take_along_axis(jnp.where(present, value, absent), order, axis=1)

    coefs = [settled(value, -1e9 if i == 0 else 0.0) for i, value in enumerate(coefs)]
    colours = [settled(value, 0.0) for value in colours]
    stage_e_ref[...] = jnp.zeros_like(stage_e_ref)
    stage_c_ref[...] = jnp.zeros_like(stage_c_ref)
    stage_t_ref[...] = jnp.zeros_like(stage_t_ref)
    parts = basis_coefs([split3(value) for value in coefs])
    for row_no, triple in enumerate(parts):
        for level in range(3):
            stage_e_ref[pl.ds(level * BASIS + row_no, SLOTS, stride=KE), :] = triple[level]
    for colour_no, value in enumerate(colours):
        triple = split3(value)
        for group, level in enumerate((0, 1, 2, 0, 1, 0)):
            stage_c_ref[pl.ds(group * SUBL + colour_no, SLOTS, stride=KC), :] = triple[level]
        for level in range(2):
            stage_t_ref[pl.ds(level * SUBL + colour_no, SLOTS, stride=BASIS), :] = triple[level]
    for block in range(own_blocks + 3):
        span = slice(block * BLOCK, (block + 1) * BLOCK)
        tab_e_ref[span, :] = stage_e_ref[block * KE : (block + 1) * KE, :].T.astype(bf16)
        tab_c_ref[span, :] = stage_c_ref[block * KC : (block + 1) * KC, :].T.astype(bf16)
        colour_ref[block] = stage_t_ref[block * BASIS : (block + 1) * BASIS, :].astype(bf16)

    def render(piece):
        unit = basis_ref[piece]
        rhs = jnp.concatenate([unit, unit, unit], axis=0)
        carry = None
        weights, left = [], []
        for index in slot_blocks(blocks_ref, live_ref, piece, own_blocks):
            start = pl.multiple_of(index * BLOCK, BLOCK)
            alphas = jnp.exp2(
                jnp.dot(tab_e_ref[pl.ds(start, BLOCK), :], rhs, preferred_element_type=f32)
            )
            keep, local = None, []
            for row in range(ROWS):
                alpha = alphas[row * SUBL : (row + 1) * SUBL]
                weight = alpha if keep is None else alpha * keep
                keep = 1.0 - alpha if keep is None else keep - weight
                local.append(weight)
            before, total = prefix_product(keep)
            if carry is not None:
                before, total = before * carry, total * carry
            carry = total
            weights += [weight * before for weight in local]
            left.append(colour_ref[index])
        high, low = split2(jnp.concatenate(weights, axis=0))
        lhs = jnp.concatenate(left, axis=1)
        sums = jnp.dot(lhs, high, preferred_element_type=f32)
        sums = sums + jnp.dot(lhs, low, preferred_element_type=f32)
        sums = sums[:SUBL] + sums[SUBL:]
        row_no = lax.broadcasted_iota(jnp.int32, sums.shape, 0)
        sums = jnp.where(row_no == 3, 1.0 - carry, sums)
        for half in range(PIX // LANES):
            span = pl.ds(half * SUBL * pieces + piece, SUBL, stride=pieces)
            result_ref[span, :] = sums[:, half * LANES : (half + 1) * LANES]

    def step(pair, carry):
        render(2 * pair)
        render(2 * pair + 1)
        return carry

    lax.fori_loop(0, pieces // 2, step, 0)
    width = PIX // doms
    lane = lax.broadcasted_iota(jnp.int32, (pieces, LANES), 1)
    tile_lane = lax.broadcasted_iota(jnp.int32, (SUBL, LANES), 1)
    labels = jnp.broadcast_to(labels_ref[...], (SUBL, LANES))
    tiles = target_ref.shape[0]
    for dom in range(doms):
        half, offset = divmod(dom * width, LANES)
        span = slice(half * LANES, (half + 1) * LANES)
        packed, aimed = None, None
        for channel in range(4):
            shift = (channel * GROUP - offset) % LANES
            first = (half * SUBL + channel) * pieces
            value = result_ref[first : first + pieces, :]
            value = pltpu.roll(value, shift, 1) if shift else value
            packed = value if packed is None else jnp.where(lane >= channel * GROUP, value, packed)
            if channel < 3:
                value = target_ref[:, channel, span]
                value = pltpu.roll(value, shift, 1) if shift else value
            else:
                value = labels
            aimed = value if aimed is None else jnp.where(tile_lane >= channel * GROUP, value, aimed)
        out_ref[dom, :pieces, :] = packed
        out_ref[dom, pieces : pieces + tiles, :] = aimed


def composite_kernel(background_ref, arrived_ref, out_ref):
    doms, pieces = out_ref.shape[0], out_ref.shape[1]
    tiles = arrived_ref.shape[1] - pieces
    all_pieces, all_tiles = doms * pieces, doms * tiles
    per_row = LANES // GROUP
    lane = lax.broadcasted_iota(jnp.int32, (1, LANES), 1)
    label_rows = []
    for dom in range(doms):
        place = dom % per_row
        value = arrived_ref[dom, pieces : pieces + 1, :]
        shift = ((place - 3) * GROUP) % LANES
        value = pltpu.roll(value, shift, 1) if shift else value
        if place == 0:
            label_rows.append(value)
        else:
            label_rows[-1] = jnp.where(lane >= place * GROUP, value, label_rows[-1])
    cell_no = lax.broadcasted_iota(jnp.int32, (MAXD * all_tiles, LANES), 0).astype(f32)
    chosen = jnp.concatenate(
        [jnp.where(cell_no == row, 1.0, 0.0).astype(bf16) for row in label_rows], axis=1
    )

    def moved(matrix, values, dims):
        triple = jnp.concatenate([part.astype(bf16) for part in split3(values)], axis=1)
        wide = lax.dot_general(matrix, triple, (dims, ((), ())), preferred_element_type=f32)
        return wide[:, :LANES] + wide[:, LANES : 2 * LANES] + wide[:, 2 * LANES :]

    data = arrived_ref[:, :pieces, :].reshape(all_pieces, LANES)
    cells = moved(chosen, data, ((1,), (0,)))
    goal = arrived_ref[:, pieces:, :].reshape(all_tiles, LANES)
    lane = lax.broadcasted_iota(jnp.int32, (all_tiles, LANES), 1)
    last = lane >= 3 * GROUP
    backdrop = jnp.where(
        lane < GROUP,
        background_ref[0],
        jnp.where(lane < 2 * GROUP, background_ref[1], background_ref[2]),
    )

    def spread(value):
        return pltpu.roll(value, GROUP, 1) + pltpu.roll(value, 2 * GROUP, 1) + pltpu.roll(
            value, 3 * GROUP, 1
        )

    fronts, through, layers = [], [], []
    front = jnp.ones((all_tiles, LANES), f32)
    composite = jnp.zeros((all_tiles, LANES), f32)
    for depth in range(MAXD):
        layer = cells[depth * all_tiles : (depth + 1) * all_tiles]
        passed = jnp.where(last, 1.0 - layer, 0.0)
        passed = passed + spread(passed)
        fronts.append(front)
        through.append(passed)
        layers.append(layer)
        composite = composite + front * layer
        front = front * passed
    residual = jnp.where(last, 0.0, composite + front * backdrop - goal)
    behind = backdrop
    grads = [None] * MAXD
    for depth in reversed(range(MAXD)):
        grads[depth] = fronts[depth] * jnp.where(last, spread(residual * behind), residual)
        behind = layers[depth] + through[depth] * behind
    back = moved(chosen, jnp.concatenate(grads, axis=0), ((0,), (0,)))
    out_ref[...] = back.reshape(out_ref.shape)


def backward_kernel(
    blocks_ref,
    live_ref,
    place_ref,
    back_ref,
    tab_e_ref,
    tab_c_ref,
    basis_ref,
    own_ref,
    low_ref,
    high_ref,
    grad_ref,
    sums_ref,
):
    doms, pieces = back_ref.shape[0], back_ref.shape[1]
    own_blocks = own_ref.shape[1]
    width = PIX // doms
    lane = lax.broadcasted_iota(jnp.int32, (pieces, LANES), 1)
    for channel in range(4):
        for half in range(PIX // LANES):
            gathered = None
            for dom in range(half * LANES // width, (half + 1) * LANES // width):
                offset = dom * width - half * LANES
                shift = (offset - channel * GROUP) % LANES
                value = back_ref[dom]
                value = pltpu.roll(value, shift, 1) if shift else value
                gathered = value if gathered is None else jnp.where(lane >= offset, value, gathered)
            first = (half * SUBL + channel) * pieces
            grad_ref[first : first + pieces, :] = gathered
            first = (half * SUBL + 4 + channel) * pieces
            grad_ref[first : first + pieces, :] = jnp.zeros_like(gathered)
    sums_ref[...] = jnp.zeros_like(sums_ref)

    def pull(piece):
        unit = basis_ref[piece]
        rhs = jnp.concatenate([unit, unit, unit], axis=0)
        halves = [
            grad_ref[pl.ds(half * SUBL * pieces + piece, SUBL, stride=pieces), :]
            for half in range(PIX // LANES)
        ]
        grads = jnp.concatenate(halves, axis=1)
        g_high, g_mid, g_low = split3(grads)
        g_rhs = jnp.concatenate([g_high, g_high, g_high, g_mid, g_mid, g_low], axis=0).astype(bf16)
        g_lhs = jnp.concatenate([g_high, g_mid], axis=0).astype(bf16)
        indices = slot_blocks(blocks_ref, live_ref, piece, own_blocks)
        carry, slots = None, []
        for index in indices:
            start = pl.multiple_of(index * BLOCK, BLOCK)
            alphas = jnp.exp2(
                jnp.dot(tab_e_ref[pl.ds(start, BLOCK), :], rhs, preferred_element_type=f32)
            )
            shades = jnp.dot(tab_c_ref[pl.ds(start, BLOCK), :], g_rhs, preferred_element_type=f32)
            keep, total, local = None, None, []
            for row in range(ROWS):
                alpha = alphas[row * SUBL : (row + 1) * SUBL]
                weight = alpha if keep is None else alpha * keep
                keep = 1.0 - alpha if keep is None else keep - weight
                value = weight * shades[row * SUBL : (row + 1) * SUBL]
                total = value if total is None else total + value
                local.append(weight)
            before, whole = prefix_product(keep)
            if carry is not None:
                before, whole = before * carry, whole * carry
            carry = whole
            slots.append((alphas, shades, local, before, total, keep))
        behind = grads[3:4]
        for index, (alphas, shades, local, before, total, keep) in zip(
            reversed(indices), reversed(slots)
        ):
            hidden, behind = suffix_affine(total, keep, behind)
            pulls, weights = [None] * ROWS, [None] * ROWS
            for row in reversed(range(ROWS)):
                span = slice(row * SUBL, (row + 1) * SUBL)
                weight = local[row] * before
                gap = shades[span] - hidden
                weights[row] = weight
                pulls[row] = weight * gap
                hidden = hidden + alphas[span] * gap
            along = (((1,), (1,)), ((), ()))
            added = []
            for left, right in ((unit, pulls), (g_lhs, weights)):
                high, low = split2(jnp.concatenate(right, axis=0))
                part = lax.dot_general(left, high, along, preferred_element_type=f32)
                added.append(
                    part + lax.dot_general(left, low, along, preferred_element_type=f32)
                )
            start = pl.multiple_of(index * 2 * BASIS, 2 * BASIS)
            span = pl.ds(start, 2 * BASIS)
            sums_ref[span, :] = sums_ref[span, :] + jnp.concatenate(added, axis=0)

    def step(pair, carry):
        pull(2 * pair)
        pull(2 * pair + 1)
        return carry

    lax.fori_loop(0, pieces // 2, step, 0)

    def rows_of(row):
        return sums_ref[pl.ds(row, SLOTS, stride=2 * BASIS), :]

    moments = [rows_of(0), rows_of(1), rows_of(2)]
    moments += [rows_of(3 + 2 * i) + rows_of(4 + 2 * i) for i in range(3)]
    terms = [value * ln_2 for value in moments]
    terms += [rows_of(BASIS + i) + rows_of(BASIS + SUBL + i) for i in range(3)]
    order = lane_order((SLOTS, LANES), True)
    low_ref[...] = jnp.zeros_like(low_ref)
    high_ref[...] = jnp.zeros_like(high_ref)
    for term_no, value in enumerate(terms):
        value = jnp.take_along_axis(value, order, axis=1)
        own_ref[term_no] = value[:own_blocks]
        low_ref[term_no : term_no + 1, :] = value[own_blocks : own_blocks + 1]
        high_ref[term_no : term_no + 1, :] = value[own_blocks + 1 : own_blocks + 2]


def update_kernel(
    params_ref,
    first_ref,
    second_ref,
    own_ref,
    from_low_ref,
    from_high_ref,
    gradient_ref,
    new_params_ref,
    new_first_ref,
    new_second_ref,
    rows_ref,
    grads_ref,
):
    own_blocks = own_ref.shape[1]
    for block in range(own_blocks):
        rows_ref[pl.ds(block, PARAMS, stride=own_blocks), :] = params_ref[
            :, block * BLOCK : (block + 1) * BLOCK
        ]
    rows = [rows_ref[i * own_blocks : (i + 1) * own_blocks, :] for i in range(PARAMS)]
    slot = lax.broadcasted_iota(jnp.int32, (own_blocks, LANES), 0)
    cots = []
    for term_no in range(9):
        low = jnp.where(slot == 0, from_low_ref[term_no : term_no + 1, :], 0.0)
        high = jnp.where(slot == own_blocks - 1, from_high_ref[term_no : term_no + 1, :], 0.0)
        cots.append(own_ref[term_no] + low + high)
    _, pull_back = jax.vjp(splat_rows, rows)
    pulled = pull_back((cots[:6], cots[6:]))[0]
    for i in range(PARAMS):
        grads_ref[i * own_blocks : (i + 1) * own_blocks, :] = pulled[i]
    for block in range(own_blocks):
        span = slice(block * BLOCK, (block + 1) * BLOCK)
        gradient = grads_ref[pl.ds(block, PARAMS, stride=own_blocks), :]
        new_first = beta_one * first_ref[:, span] + (1 - beta_one) * gradient
        new_second = beta_two * second_ref[:, span] + (1 - beta_two) * gradient * gradient
        update = (
            new_first
            / (1 - beta_one**adam_step)
            / (jnp.sqrt(new_second / (1 - beta_two**adam_step)) + tiny)
        )
        gradient_ref[:, span] = gradient
        new_params_ref[:, span] = params_ref[:, span] - rate * update
        new_first_ref[:, span] = new_first
        new_second_ref[:, span] = new_second


def swap_neighbours(to_lower, to_upper):
    count = lax.axis_size("region")
    even = lax.axis_index("region") % 2 == 0
    inner = [(i, i ^ 1) for i in range(count) if (i ^ 1) < count]
    outer = [(i, i + 1) for i in range(1, count - 1, 2)]
    outer += [(target, source) for source, target in outer]
    first = lax.ppermute(jnp.where(even, to_upper, to_lower), "region", inner)
    second = lax.ppermute(jnp.where(even, to_lower, to_upper), "region", outer)
    return jnp.where(even, second, first), jnp.where(even, first, second)


def on_device(
    params,
    first_moment,
    second_moment,
    piece_blocks,
    piece_live,
    piece_owner,
    piece_cell,
    target,
    background,
):
    own_blocks = params.shape[1] // BLOCK
    doms = lax.axis_size("dom")
    pieces = piece_live.shape[1]
    tiles = target.shape[1]
    low, high = swap_neighbours(params[:, :BLOCK], params[:, -BLOCK:])
    cell = piece_cell[0]
    label = (cell % MAXD) * (doms * tiles) + piece_owner[0] * tiles + cell // MAXD
    labels = jnp.pad(label.astype(f32)[None], ((0, 0), (LANES - GROUP, GROUP - pieces)))
    place = jnp.stack([lax.axis_index("region"), jnp.int32(lax.axis_size("region"))])
    basis = jnp.asarray(pixel_basis(pieces))
    smem = pl.BlockSpec(memory_space=pltpu.SMEM)
    vmem = pl.BlockSpec(memory_space=pltpu.VMEM)
    table_rows = (own_blocks + 3) * BLOCK
    payload, tab_e, tab_c = pl.pallas_call(
        forward_kernel,
        out_shape=(
            jax.ShapeDtypeStruct((doms, pieces + tiles, LANES), f32),
            jax.ShapeDtypeStruct((table_rows, KE), bf16),
            jax.ShapeDtypeStruct((table_rows, KC), bf16),
        ),
        in_specs=[smem] * 3 + [vmem] * 6,
        out_specs=(vmem, vmem, vmem),
        scratch_shapes=[
            pltpu.VMEM((64 * SLOTS, LANES), f32),
            pltpu.VMEM((SLOTS * KE, LANES), f32),
            pltpu.VMEM((SLOTS * KC, LANES), f32),
            pltpu.VMEM((SLOTS * BASIS, LANES), f32),
            pltpu.VMEM((own_blocks + 3, BASIS, LANES), bf16),
            pltpu.VMEM((PIX // LANES * SUBL * pieces, LANES), f32),
        ],
        name="forward",
    )(piece_blocks[0], piece_live[0], place, params, low, high, target[0], labels, basis)
    arrived = lax.all_to_all(payload, "dom", split_axis=0, concat_axis=0, tiled=True)
    back = pl.pallas_call(
        composite_kernel,
        out_shape=jax.ShapeDtypeStruct((doms, pieces, LANES), f32),
        in_specs=[smem, vmem],
        out_specs=vmem,
        name="composite",
    )(background, arrived)
    returned = lax.all_to_all(back, "dom", split_axis=0, concat_axis=0, tiled=True)
    own, to_lower, to_upper = pl.pallas_call(
        backward_kernel,
        out_shape=(
            jax.ShapeDtypeStruct((9, own_blocks, LANES), f32),
            jax.ShapeDtypeStruct((SLOTS, LANES), f32),
            jax.ShapeDtypeStruct((SLOTS, LANES), f32),
        ),
        in_specs=[smem] * 3 + [vmem] * 4,
        out_specs=(vmem, vmem, vmem),
        scratch_shapes=[
            pltpu.VMEM((PIX // LANES * SUBL * pieces, LANES), f32),
            pltpu.VMEM((SLOTS * 2 * BASIS, LANES), f32),
        ],
        name="backward",
    )(piece_blocks[0], piece_live[0], place, returned, tab_e, tab_c, basis)
    from_low, from_high = swap_neighbours(to_lower, to_upper)
    shape = jax.ShapeDtypeStruct(params.shape, f32)
    return pl.pallas_call(
        update_kernel,
        out_shape=(shape, shape, shape, shape),
        in_specs=[vmem] * 6,
        out_specs=(vmem,) * 4,
        scratch_shapes=[
            pltpu.VMEM((64 * own_blocks, LANES), f32),
            pltpu.VMEM((64 * own_blocks, LANES), f32),
        ],
        name="update",
    )(params, first_moment, second_moment, own, from_low, from_high)


def solution(mesh):
    in_specs = (
        P(None, ("region", "dom")),
        P(None, ("region", "dom")),
        P(None, ("region", "dom")),
        P(("region", "dom"), None, None),
        P(("region", "dom"), None),
        P(("region", "dom"), None),
        P(("region", "dom"), None),
        P(("region", "dom"), None, None, None),
        P(),
    )
    out_specs = (P(None, ("region", "dom")),) * 4
    return jax.shard_map(
        on_device, mesh=mesh, in_specs=in_specs, out_specs=out_specs, check_vma=False
    )
```

time: 231 us -> 72.1 us (0.31)
  other arithmetic: 101 us -> 3.42 us
  matrix products: 57.1 us -> 0 us
  Pallas kernels: 0 us -> 32.2 us
  blocking collectives: 0 us -> 22.9 us
  local copies, waits for them, and re-layouts: 24.8 us -> 1.97 us
  starting transfers between devices: 27.1 us -> 9 us
  waiting for transfers between devices: 17.2 us -> 1.32 us
    dot_general x29 -> x0, matrix products: 57.1 us -> none  [the longest x24 53.7 us: render_piece(): jnp.dot(colour, weight, precision=lax.Precision.HIGHEST)]
    another operation x27 -> x1, other arithmetic: 42.3 us -> 0.65 us  [on_device(): jnp.stack([lax.axis_index('region'), jnp.int32(lax.axis_size('region'))])]
    reduce_sum x13 -> x0, other arithmetic: 39.5 us -> none  [the longest x4 30.2 us: render_piece(): conic_yy[:, None] * offset_y * offset_y]
    pallas_call x0 -> x4, Pallas kernels: none -> 32.2 us  [the longest x1 17.5 us: on_device(): pl.pallas_call(backward_kernel, out_shape=(jax.ShapeDtypeStruct((9, own_b...]
    all_to_all x0 -> x2, blocking collectives: none -> 22.9 us  [the longest x1 12.1 us: on_device(): lax.all_to_all(payload, 'dom', split_axis=0, concat_axis=0, tiled=True)]
    all_to_all x3 -> x0, starting transfers between devices: 15.7 us -> none  [the longest x1 6.37 us: on_device(): lax.all_to_all(slot_labels.reshape(doms, capacity), 'dom', split_axis=0,...]
    all_to_all x3 -> x0, waiting for transfers between devices: 14.8 us -> none  [the longest x1 8.02 us: on_device(): lax.all_to_all(slot_rows.reshape(doms, capacity, 4 * PIX), 'dom', split_a...]
    gather x32 -> x0, local copies, waits for them, and re-layouts: 10.5 us -> none  [the longest x16 5.91 us: render_listed(): present[blocks_row] * (slot_ids < live_row).astype(present.dtype)]
  transfers between devices with their start and end apart: 7 -> 4, of which waited for: 3 -> 1; matrix products, arithmetic and copies ran while one was open for 22% -> 4% of each run, Pallas kernels for 0% -> 0%
where the time goes in v1:
time: 72.1 us; the launch traced here: 71.6 us
  Pallas kernels  32.2 us (45%)
  blocking collectives  22.9 us (32%)
  starting transfers between devices  9 us (12%)
  other arithmetic  3.42 us (5%)
  local copies, waits for them, and re-layouts  1.97 us (3%)
  waiting for transfers between devices  1.32 us (2%)
    pallas_call x1, Pallas kernels, on_device(): pl.pallas_call(backward_kernel, out_shape=(jax.ShapeDtypeStruct((9, own_b...  17.5 us
    all_to_all x1, blocking collectives, on_device(): lax.all_to_all(payload, 'dom', split_axis=0, concat_axis=0, tiled=True)  12.1 us
    all_to_all x1, blocking collectives, on_device(): lax.all_to_all(back, 'dom', split_axis=0, concat_axis=0, tiled=True)  10.9 us
    pallas_call x1, Pallas kernels, on_device(): pl.pallas_call(forward_kernel, out_shape=(jax.ShapeDtypeStruct((doms, pie...  9.62 us
    ppermute x2, starting transfers between devices, swap_neighbours(): second = lax.ppermute(jnp.where(even, to_lower, to_upper), 'region', outer)  8.75 us
    pallas_call x1, Pallas kernels, on_device(): pl.pallas_call(composite_kernel, out_shape=jax.ShapeDtypeStruct((doms, pi...  2.56 us
    pallas_call x1, Pallas kernels, on_device(): pl.pallas_call(update_kernel, out_shape=(shape, shape, shape, shape), in_...  2.48 us
    select_n x2, other arithmetic, swap_neighbours(): first = lax.ppermute(jnp.where(even, to_upper, to_lower), 'region', inner)  1.52 us
  transfers between devices with their start and end apart: 4, of which 1 were waited for; matrix products, arithmetic and copies ran while one was open for 4% of the time, Pallas kernels for 0%

profile of v1, /device:TPU:1, one launch (start us, length us, event | category | flops | bytes accessed | tf_op | source)
XLA Modules:
  0.0 71.6 jit_solution(7845453614369873319)
XLA Ops:
  0.6 0.0 copy-start.2
  0.7 0.0 copy-start.3
  0.7 0.0 copy-start.1
  0.7 0.8 %slice_select_fusion = (f32[59,128]{1,0:T(8,128)S(1)}, f32[59,128]{1,0:T(8,128)S(1)}) fusion(f32[59,1024]{1,0:T(8,128)} %params_ref.3, pred[]{:T(512)S(6)} %eq.9), kind=kLoop, calls=%fused_computation.1 | loop fusion | flops 15104 | bytes 120833 | tf_op jit(solution)/shard_map/jit(_where)/select_n | solution.py:565
  1.5 0.0 copy-start
  1.5 0.1 collective-permute-start.1
  1.6 4.5 %collective-permute-start = (f32[59,128]{1,0:T(8,128)S(1)}, f32[59,128]{1,0:T(8,128)S(1)}, u32[]{:S(2)}, u32[]{:S(2)}) collective-permute-start(f32[59,128]{1,0:T(8,128)S(1)} %get-tuple-element.17), channel_id=1, source_target_pairs={{8,16},{16,8},{9,17},{17,9},{10,18},{18,10},{11,19},{19,11},{12,20... | collective-permute-start | bytes 90632 | tf_op jit(solution)/shard_map/ppermute | solution.py:566
  6.1 0.0 copy-done.2
  6.1 0.0 copy-done.3
  6.1 0.7 pad_add_fusion.place_ref
  6.7 0.0 copy-done.1
  6.7 0.7 copy.16.blocks_ref
  7.4 0.0 copy-done
  7.4 0.6 copy.18
  8.1 0.6 pad.4.labels_ref
  8.7 0.0 collective-permute-done.1
  8.7 0.0 collective-permute-done
  8.7 0.6 broadcast_select_fusion
  9.3 9.6 %forward.1 = (f32[8,40,128]{2,1,0:T(8,128)}, bf16[1408,48]{1,0:T(8,128)(2,1)}, bf16[1408,48]{1,0:T(8,128)(2,1)}) custom-call(s32[32,2]{1,0:T(8,128)} %copy.16.blocks_ref, s32[32]{0:T(128)} %bitcast.7, s32[2]{0:T(128)} %pad_add_fusion.place_ref, f32[59,1024]{1,0:T(8,128)} %params_ref.3, f32[59,128]{1,0:T(8,128)} %get-tuple-element.19.low_ref, ...), custom_call_target="tpu_custom_call" | custom-call | tf_op jit(solution)/shard_map/forward/pallas_call | solution.py:594
  19.0 12.1 %all_to_all.10.arrived_ref = f32[8,40,128]{2,1,0:T(8,128)} all-to-all(f32[8,40,128]{2,1,0:T(8,128)} %get-tuple-element.10), channel_id=1, replica_groups=mesh['region'=4,'dom'=8] {'dom'}, dimensions={0} | all-to-all | bytes 327680 | tf_op jit(solution)/shard_map/all_to_all | solution.py:613
  31.0 2.6 %composite.1 = f32[8,32,128]{2,1,0:T(8,128)} custom-call(f32[3]{0:T(128)} %background_ref.1, f32[8,40,128]{2,1,0:T(8,128)} %all_to_all.10.arrived_ref), custom_call_target="tpu_custom_call" | custom-call | tf_op jit(solution)/shard_map/composite/pallas_call | solution.py:614
  33.6 10.9 %all_to_all.11.back_ref = f32[8,32,128]{2,1,0:T(8,128)} all-to-all(f32[8,32,128]{2,1,0:T(8,128)} %composite.1), channel_id=1, replica_groups=mesh['region'=4,'dom'=8] {'dom'}, dimensions={0} | all-to-all | bytes 262144 | tf_op jit(solution)/shard_map/all_to_all | solution.py:621
  44.5 17.5 %backward.1 = (f32[9,8,128]{2,1,0:T(8,128)}, f32[16,128]{1,0:T(8,128)}, f32[16,128]{1,0:T(8,128)}) custom-call(s32[32,2]{1,0:T(8,128)} %copy.16.blocks_ref, s32[32]{0:T(128)} %bitcast.8, s32[2]{0:T(128)} %pad_add_fusion.place_ref, f32[8,32,128]{2,1,0:T(8,128)} %all_to_all.11.back_ref, bf16[1408,48]{1,0:T(8,128)(2,1)} %get-tuple-element.11.tab_e_ref, ...), custom_call_target="tpu_custom_call" | custom-call | tf_op jit(solution)/shard_map/backward/pallas_call | solution.py:622
  62.0 0.7 %broadcast_select_fusion.4 = (f32[16,128]{1,0:T(8,128)S(1)}, f32[16,128]{1,0:T(8,128)S(1)}) fusion(f32[16,128]{1,0:T(8,128)} %get-tuple-element.15, f32[16,128]{1,0:T(8,128)} %get-tuple-element.14, pred[]{:T(512)S(6)} %eq.9), kind=kLoop, calls=%fused_computation.7 | loop fusion | flops 4096 | bytes 32769 | tf_op jit(solution)/shard_map/jit(_where)/select_n | solution.py:565
  62.7 0.2 collective-permute-start.3
  62.9 4.3 %collective-permute-start.2 = (f32[16,128]{1,0:T(8,128)S(1)}, f32[16,128]{1,0:T(8,128)S(1)}, u32[]{:S(2)}, u32[]{:S(2)}) collective-permute-start(f32[16,128]{1,0:T(8,128)S(1)} %get-tuple-element.23), channel_id=1, source_target_pairs={{8,16},{16,8},{9,17},{17,9},{10,18},{18,10},{11,19},{19,11},{12,20... | collective-permute-start | bytes 24584 | tf_op jit(solution)/shard_map/ppermute | solution.py:566
  67.1 0.0 collective-permute-done.3
  67.2 1.3 %collective-permute-done.2 = f32[16,128]{1,0:T(8,128)S(1)} collective-permute-done((f32[16,128]{1,0:T(8,128)S(1)}, f32[16,128]{1,0:T(8,128)S(1)}, u32[]{:S(2)}, u32[]{:S(2)}) %collective-permute-start.2) | collective-permute-done | bytes 8224 | tf_op jit(solution)/shard_map/ppermute | solution.py:566
  68.5 0.6 broadcast_select_fusion.2
  69.1 2.5 %update.1 = (f32[59,1024]{1,0:T(8,128)}, f32[59,1024]{1,0:T(8,128)}, f32[59,1024]{1,0:T(8,128)}, f32[59,1024]{1,0:T(8,128)}) custom-call(f32[59,1024]{1,0:T(8,128)} %params_ref.3, f32[59,1024]{1,0:T(8,128)} %first_ref.1, f32[59,1024]{1,0:T(8,128)} %second_ref.1, f32[9,8,128]{2,1,0:T(8,128)} %get-tuple-element.13.own_ref, ...), custom_call_target="tpu_custom_call" | custom-call | tf_op jit(solution)/shard_map/update/pallas_call | solution.py:639
  (1 shorter events, 0.0 us)
Async XLA Ops:
  0.6 5.4 %copy-start.2 = (s32[1,32]{1,0:T(1,128)S(1)}, s32[1,32]{1,0:T(1,128)}, u32[]{:S(2)}) copy-start(s32[1,32]{1,0:T(1,128)} %param.16) | copy-start | bytes 388
  0.7 5.4 %copy-start.3 = (s32[1,32]{1,0:T(1,128)S(1)}, s32[1,32]{1,0:T(1,128)}, u32[]{:S(2)}) copy-start(s32[1,32]{1,0:T(1,128)} %param.15) | copy-start | bytes 388
  0.7 6.1 %copy-start.1 = (s32[1,32,2]{1,2,0:T(2,128)S(1)}, s32[1,32,2]{1,2,0:T(2,128)}, u32[]{:S(2)}) copy-start(s32[1,32,2]{1,2,0:T(2,128)} %param.13) | copy-start | bytes 772
  1.5 6.0 %copy-start = (f32[1,8,3,256]{3,1,2,0:T(8,128)S(1)}, f32[1,8,3,256]{3,1,2,0:T(8,128)}, u32[]{:S(2)}) copy-start(f32[1,8,3,256]{3,1,2,0:T(8,128)} %param.17) | copy-start | bytes 73732
  1.5 7.2 %collective-permute-start.1 = (f32[59,128]{1,0:T(8,128)S(1)}, f32[59,128]{1,0:T(8,128)S(1)}, u32[]{:S(2)}, u32[]{:S(2)}) collective-permute-start(f32[59,128]{1,0:T(8,128)S(1)} %get-tuple-element.16), channel_id=1, source_target_pairs={{0,8},{8,0},{16,24},{24,16},{1,9},{9,1},{17,25},{25,17},{2,10},{10... | collective-permute-start | bytes 90632 | tf_op jit(solution)/shard_map/ppermute | solution.py:565
  1.6 7.2 %collective-permute-start = (f32[59,128]{1,0:T(8,128)S(1)}, f32[59,128]{1,0:T(8,128)S(1)}, u32[]{:S(2)}, u32[]{:S(2)}) collective-permute-start(f32[59,128]{1,0:T(8,128)S(1)} %get-tuple-element.17), channel_id=1, source_target_pairs={{8,16},{16,8},{9,17},{17,9},{10,18},{18,10},{11,19},{19,11},{12,20... | collective-permute-start | bytes 90632 | tf_op jit(solution)/shard_map/ppermute | solution.py:566
  62.7 4.4 %collective-permute-start.3 = (f32[16,128]{1,0:T(8,128)S(1)}, f32[16,128]{1,0:T(8,128)S(1)}, u32[]{:S(2)}, u32[]{:S(2)}) collective-permute-start(f32[16,128]{1,0:T(8,128)S(1)} %get-tuple-element.22), channel_id=1, source_target_pairs={{0,8},{8,0},{16,24},{24,16},{1,9},{9,1},{17,25},{25,17},{2,10},{10... | collective-permute-start | bytes 24584 | tf_op jit(solution)/shard_map/ppermute | solution.py:565
  62.9 5.6 %collective-permute-start.2 = (f32[16,128]{1,0:T(8,128)S(1)}, f32[16,128]{1,0:T(8,128)S(1)}, u32[]{:S(2)}, u32[]{:S(2)}) collective-permute-start(f32[16,128]{1,0:T(8,128)S(1)} %get-tuple-element.23), channel_id=1, source_target_pairs={{8,16},{16,8},{9,17},{17,9},{10,18},{18,10},{11,19},{19,11},{12,20... | collective-permute-start | bytes 24584 | tf_op jit(solution)/shard_map/ppermute | solution.py:566

commit v2 on v1

v2 whole, which is shorter than its diff:
```python
import math

import numpy as np
import jax
import jax.numpy as jnp
from jax import lax
from jax.experimental import pallas as pl
from jax.experimental.pallas import tpu as pltpu
from jax.sharding import PartitionSpec as P

PARAMS = 59
TSIDE = 16
WIN = 8
BLOCK = 128
MAXD = 8
PIX = 256

harmonic_zero = 0.28209479177387814
harmonic_one = 0.4886025119029199
harmonic_two = (
    1.0925484305920792,
    -1.0925484305920792,
    0.31539156525252005,
    -1.0925484305920792,
    0.5462742152960396,
)
harmonic_three = (
    -0.5900435899266435,
    2.890611442640554,
    -0.4570457994644658,
    0.3731763325901154,
    -0.4570457994644658,
    1.445305721320277,
    -0.5900435899266435,
)
beta_one = 0.9
beta_two = 0.999
rate = 0.001
adam_step = 100
tiny = 1e-08
log2_e = math.log2(math.e)
ln_2 = math.log(2.0)

LANES = 128
SUBL = 8
ROWS = BLOCK // SUBL
GROUP = LANES // 4
BASIS = 9
KE = 32
KC = 2 * SUBL
KT = KE + KC
TOP = 16
SLOTS = 16
f32 = jnp.float32
bf16 = jnp.bfloat16


def splat_rows(rows):
    mean_x, mean_y, mean_z = rows[0], rows[1], rows[2]
    scales = [jnp.exp(rows[3]), jnp.exp(rows[4]), jnp.exp(rows[5])]
    norm_sq = rows[6] * rows[6] + rows[7] * rows[7] + rows[8] * rows[8] + rows[9] * rows[9]
    inv_norm = 1.0 / jnp.sqrt(norm_sq)
    quat_w, quat_x, quat_y, quat_z = [rows[6 + i] * inv_norm for i in range(4)]
    rotation = [
        [
            1 - 2 * (quat_y * quat_y + quat_z * quat_z),
            2 * (quat_x * quat_y - quat_w * quat_z),
            2 * (quat_x * quat_z + quat_w * quat_y),
        ],
        [
            2 * (quat_x * quat_y + quat_w * quat_z),
            1 - 2 * (quat_x * quat_x + quat_z * quat_z),
            2 * (quat_y * quat_z - quat_w * quat_x),
        ],
        [
            2 * (quat_x * quat_z - quat_w * quat_y),
            2 * (quat_y * quat_z + quat_w * quat_x),
            1 - 2 * (quat_x * quat_x + quat_y * quat_y),
        ],
    ]
    focal_px = 0.3125 * float(WIN * TSIDE)
    inv_z = 1.0 / mean_z
    scale_z = focal_px * inv_z
    off_u = scale_z * mean_x
    off_v = scale_z * mean_y
    slope_u = off_u * inv_z
    slope_v = off_v * inv_z
    proj_u = [(scale_z * rotation[0][i] - slope_u * rotation[2][i]) * scales[i] for i in range(3)]
    proj_v = [(scale_z * rotation[1][i] - slope_v * rotation[2][i]) * scales[i] for i in range(3)]
    sigma_xx = proj_u[0] * proj_u[0] + proj_u[1] * proj_u[1] + proj_u[2] * proj_u[2] + 0.3
    sigma_xy = proj_u[0] * proj_v[0] + proj_u[1] * proj_v[1] + proj_u[2] * proj_v[2]
    sigma_yy = proj_v[0] * proj_v[0] + proj_v[1] * proj_v[1] + proj_v[2] * proj_v[2] + 0.3
    determinant = sigma_xx * sigma_yy - sigma_xy * sigma_xy
    inv_det = log2_e / determinant
    con_xx = sigma_yy * inv_det
    con_xy = -sigma_xy * inv_det
    con_yy = sigma_xx * inv_det
    lin_x = con_xx * off_u + con_xy * off_v
    lin_y = con_xy * off_u + con_yy * off_v
    logit = rows[10]
    log_opacity = (logit - jnp.log(1.0 + jnp.exp(logit))) * log2_e
    const = log_opacity - 0.5 * (lin_x * off_u + lin_y * off_v)
    coefs = [const, lin_x, lin_y, -0.5 * con_xx, -con_xy, -0.5 * con_yy]
    inv_len = 1.0 / jnp.sqrt(mean_x * mean_x + mean_y * mean_y + mean_z * mean_z)
    dir_x, dir_y, dir_z = mean_x * inv_len, mean_y * inv_len, mean_z * inv_len
    sq_x, sq_y, sq_z = dir_x * dir_x, dir_y * dir_y, dir_z * dir_z
    harmonics = [
        None,
        -harmonic_one * dir_y,
        harmonic_one * dir_z,
        -harmonic_one * dir_x,
        harmonic_two[0] * dir_x * dir_y,
        harmonic_two[1] * dir_y * dir_z,
        harmonic_two[2] * (2 * sq_z - sq_x - sq_y),
        harmonic_two[3] * dir_x * dir_z,
        harmonic_two[4] * (sq_x - sq_y),
        harmonic_three[0] * dir_y * (3 * sq_x - sq_y),
        harmonic_three[1] * dir_x * dir_y * dir_z,
        harmonic_three[2] * dir_y * (4 * sq_z - sq_x - sq_y),
        harmonic_three[3] * dir_z * (2 * sq_z - 3 * sq_x - 3 * sq_y),
        harmonic_three[4] * dir_x * (4 * sq_z - sq_x - sq_y),
        harmonic_three[5] * dir_z * (sq_x - sq_y),
        harmonic_three[6] * dir_x * (sq_x - 3 * sq_y),
    ]
    colours = []
    for colour_no in range(3):
        base = 11 + 16 * colour_no
        total = rows[base] * harmonic_zero
        for k in range(1, 16):
            total = total + rows[base + k] * harmonics[k]
        colours.append(jnp.maximum(total + 0.5, 0.0))
    return coefs, colours


def split3(value):
    high = value.astype(bf16).astype(f32)
    rest = value - high
    middle = rest.astype(bf16).astype(f32)
    return high, middle, rest - middle


def split2(value):
    high = value.astype(bf16)
    return high, (value - high.astype(f32)).astype(bf16)


def pixel_basis(pieces):
    tiles = np.arange(pieces)[:, None]
    pixels = np.arange(PIX)[None, :]
    half = WIN * TSIDE / 2
    pos_x = TSIDE * (tiles % WIN) + pixels % TSIDE + 0.5 - half
    pos_y = TSIDE * (tiles // WIN) + pixels // TSIDE + 0.5 - half
    rows = [np.ones_like(pos_x), pos_x, pos_y]
    for product in (pos_x * pos_x, pos_x * pos_y, pos_y * pos_y):
        high = product.astype(bf16).astype(np.float64)
        rows += [high, product - high]
    table = np.zeros((pieces, KE, PIX))
    for row_no, row in enumerate(rows * 3):
        table[:, row_no] = row
    return table.astype(bf16)


def basis_coefs(coefs):
    return [coefs[i] for i in (0, 1, 2, 3, 3, 4, 4, 5, 5)]


def lane_order(shape, inverse):
    lane = lax.broadcasted_iota(jnp.int32, shape, 1)
    if inverse:
        return (lane % ROWS) * SUBL + lane // ROWS
    return (lane % SUBL) * ROWS + lane // SUBL


def prefix_product(total):
    sub = lax.broadcasted_iota(jnp.int32, total.shape, 0)
    run = total
    for step in (1, 2, 4):
        run = jnp.where(sub >= step, run * pltpu.roll(run, step, 0), run)
    before = jnp.where(sub >= 1, pltpu.roll(run, 1, 0), 1.0)
    return before, run[SUBL - 1 :]


def suffix_affine(total, keep, behind):
    sub = lax.broadcasted_iota(jnp.int32, total.shape, 0)
    value, gain = total, keep
    for step in (1, 2, 4):
        inside = sub < SUBL - step
        next_value = jnp.where(inside, pltpu.roll(value, SUBL - step, 0), 0.0)
        next_gain = jnp.where(inside, pltpu.roll(gain, SUBL - step, 0), 1.0)
        value = value + gain * next_value
        gain = gain * next_gain
    whole = value + gain * behind
    after = jnp.where(sub < SUBL - 1, pltpu.roll(whole, SUBL - 1, 0), behind)
    return after, whole[:1]


def list_items(blocks_ref, live_ref, items_ref, pieces, own_blocks):
    room = pieces + SUBL
    doubles, singles = jnp.int32(0), jnp.int32(0)
    for piece in range(pieces):
        entries = []
        for slot in range(2):
            block = blocks_ref[slot, piece]
            place = jnp.where(block == 0, own_blocks + 1, block - 1)
            entries.append(place * 64 + piece)
        items_ref[doubles] = entries[0]
        items_ref[room + doubles] = entries[1]
        items_ref[2 * room + singles] = entries[0]
        second = live_ref[0, piece] - 1
        doubles = doubles + second
        singles = singles + 1 - second
    for spare in range(6):
        items_ref[2 * room + singles + spare] = (own_blocks + 2) * 64 + pieces
    items_ref[3 * room] = doubles
    items_ref[3 * room + 1] = (doubles + (singles + 1) // 2 + 1) // 2


def item_slots(items_ref, item, pieces):
    room = pieces + SUBL
    doubles = items_ref[3 * room]
    chained = item < doubles
    single = 2 * (room + item - doubles)
    first = items_ref[jnp.where(chained, item, single)]
    second = items_ref[jnp.where(chained, room + item, single + 1)]
    slots = []
    for entry in (first, second):
        slots.append((entry % 64, pl.multiple_of(entry // 64 * BLOCK, BLOCK)))
    return chained, slots


def pipelined(pairs, front, back):
    front(0, 0)

    def step(pair, carry):
        for side in range(2):
            front(2 * pair + side + 1, 1 - side)
            back(2 * pair + side, side)
        return carry

    lax.fori_loop(0, pairs, step, 0)


def exponents(table_ref, basis_ref, piece, start, pieces):
    unit = basis_ref[jnp.minimum(piece, pieces - 1)]
    rhs = jnp.concatenate([unit, jnp.zeros((KC, PIX), bf16)], axis=0)
    return jnp.dot(table_ref[pl.ds(start, BLOCK), :], rhs, preferred_element_type=f32)


def forward_kernel(
    blocks_ref,
    live_ref,
    owner_ref,
    cell_ref,
    params_ref,
    inner_ref,
    outer_ref,
    target_ref,
    basis_ref,
    out_ref,
    table_ref,
    items_ref,
    own_rows_ref,
    copy_rows_ref,
    stage_ref,
    colour_ref,
    result_ref,
    local_refs,
    before_refs,
    left_refs,
):
    doms, pieces = out_ref.shape[0], basis_ref.shape[0]
    own_blocks = params_ref.shape[1] // BLOCK
    region_idx, regions = lax.axis_index("region"), lax.axis_size("region")
    even = region_idx % 2 == 0
    list_items(blocks_ref, live_ref, items_ref, pieces, own_blocks)
    for block in range(own_blocks):
        own_rows_ref[pl.ds(block, PARAMS, stride=SUBL), :] = params_ref[
            :, block * BLOCK : (block + 1) * BLOCK
        ]
    inner, outer = inner_ref[...], outer_ref[...]
    copy_rows_ref[pl.ds(0, PARAMS, stride=SUBL), :] = jnp.where(even, inner, outer)
    copy_rows_ref[pl.ds(1, PARAMS, stride=SUBL), :] = jnp.where(even, outer, inner)
    rows = []
    for i in range(PARAMS):
        span = slice(i * SUBL, (i + 1) * SUBL)
        rows.append(jnp.concatenate([own_rows_ref[span, :], copy_rows_ref[span, :]], axis=0))
    coefs, colours = splat_rows(rows)
    shape = (SLOTS, LANES)
    slot_no = lax.broadcasted_iota(jnp.int32, shape, 0)
    present = (
        (slot_no < own_blocks)
        | ((slot_no == own_blocks) & (region_idx < regions - 1))
        | ((slot_no == own_blocks + 1) & (region_idx > 0))
    )
    order = lane_order(shape, False)

    def settled(value, absent):
        return jnp.take_along_axis(jnp.where(present, value, absent), order, axis=1)

    coefs = [settled(value, -1e9 if i == 0 else 0.0) for i, value in enumerate(coefs)]
    colours = [settled(value, 0.0) for value in colours]
    nothing = jnp.zeros(shape, f32)
    parts = basis_coefs([split3(value) for value in coefs])
    lines = [parts[row % BASIS][row // BASIS] for row in range(3 * BASIS)]
    lines += [nothing] * (KE - 3 * BASIS)
    triples = [split3(value) for value in colours]
    for level in (0, 0, 1, 0, 0, 1):
        lines += [triple[level] for triple in triples] + [nothing]
    for row, value in enumerate(lines):
        group, place = divmod(row, SUBL)
        base = group * SLOTS * SUBL + place
        stage_ref[pl.ds(base, SUBL, stride=SUBL), :] = value[:SUBL]
        stage_ref[pl.ds(base + SUBL * SUBL, 4, stride=SUBL), :] = value[SUBL : SUBL + 4]
    for block in range(own_blocks + 3):
        tiles = [
            stage_ref[(group * SLOTS + block) * SUBL : (group * SLOTS + block + 1) * SUBL, :]
            for group in range(len(lines) // SUBL)
        ]
        span = slice(block * BLOCK, (block + 1) * BLOCK)
        table_ref[span, :] = jnp.concatenate(tiles[: KT // SUBL], axis=0).T.astype(bf16)
        colour_ref[block] = jnp.concatenate(tiles[KT // SUBL :] * 2, axis=0).astype(bf16)

    def front(item, side):
        chained, slots = item_slots(items_ref, item, pieces)
        carry = None
        for slot, (piece, start) in enumerate(slots):
            alphas = jnp.exp2(exponents(table_ref, basis_ref, piece, start, pieces))
            keep = None
            for row in range(ROWS):
                alpha = alphas[row * SUBL : (row + 1) * SUBL]
                weight = alpha if keep is None else alpha * keep
                keep = 1.0 - alpha if keep is None else keep - weight
                first = slot * BLOCK + row * SUBL
                local_refs[side][first : first + SUBL, :] = weight
            before, total = prefix_product(keep)
            if slot == 1:
                carry = jnp.where(chained, carry, 1.0)
                before, total = before * carry, total * carry
            carry = total
            before_refs[side][slot * SUBL : (slot + 1) * SUBL, :] = before
            left_refs[side][slot : slot + 1, :] = total

    def back(item, side):
        chained, slots = item_slots(items_ref, item, pieces)
        sums = None
        for slot, (piece, start) in enumerate(slots):
            before = before_refs[side][slot * SUBL : (slot + 1) * SUBL, :]
            weights = []
            for row in range(ROWS):
                first = slot * BLOCK + row * SUBL
                weights.append(local_refs[side][first : first + SUBL, :] * before)
            high, low = split2(jnp.concatenate(weights, axis=0))
            left = colour_ref[start // BLOCK]
            wide = jnp.dot(left, high, preferred_element_type=f32)
            wide = (wide + jnp.dot(left, low, preferred_element_type=f32))[:SUBL]
            wide = wide + pltpu.roll(wide, 4, 0)
            sums = wide + jnp.where(chained, sums, 0.0) if slot else wide
            row_no = lax.broadcasted_iota(jnp.int32, sums.shape, 0)
            value = jnp.where(row_no == 3, 1.0 - left_refs[side][slot : slot + 1, :], sums)
            for half in range(PIX // LANES):
                first = pl.multiple_of((half * (pieces + 1) + piece) * SUBL, SUBL)
                result_ref[pl.ds(first, SUBL), :] = value[:, half * LANES : (half + 1) * LANES]

    pipelined(items_ref[3 * (pieces + SUBL) + 1], front, back)
    width = PIX // doms
    lane = lax.broadcasted_iota(jnp.int32, (pieces, LANES), 1)
    tile_lane = lax.broadcasted_iota(jnp.int32, (SUBL, LANES), 1)
    tiles = target_ref.shape[1]
    cell = cell_ref[...]
    labels = (cell % MAXD) * (doms * tiles) + owner_ref[...] * tiles + cell // MAXD
    labels = jnp.concatenate(
        [jnp.zeros((1, LANES - pieces), f32), labels.astype(f32)], axis=1
    )
    labels = jnp.broadcast_to(labels, (SUBL, LANES))
    for dom in range(doms):
        half, offset = divmod(dom * width, LANES)
        span = slice(half * LANES, (half + 1) * LANES)
        packed, aimed = None, None
        for channel in range(4):
            shift = (channel * GROUP - offset) % LANES
            first = half * (pieces + 1) * SUBL + channel
            value = result_ref[pl.ds(first, pieces, stride=SUBL), :]
            value = pltpu.roll(value, shift, 1) if shift else value
            packed = value if packed is None else jnp.where(lane >= channel * GROUP, value, packed)
            if channel < 3:
                value = target_ref[channel, :, span]
                value = pltpu.roll(value, shift, 1) if shift else value
            else:
                value = labels
            aimed = value if aimed is None else jnp.where(tile_lane >= channel * GROUP, value, aimed)
        out_ref[dom, :pieces, :] = packed
        out_ref[dom, pieces : pieces + tiles, :] = aimed


def composite_kernel(background_ref, arrived_ref, out_ref):
    doms, pieces = out_ref.shape[0], out_ref.shape[1]
    tiles = arrived_ref.shape[1] - pieces
    all_pieces, all_tiles = doms * pieces, doms * tiles
    per_row = LANES // GROUP
    lane = lax.broadcasted_iota(jnp.int32, (1, LANES), 1)
    label_rows = []
    for dom in range(doms):
        place = dom % per_row
        value = arrived_ref[dom, pieces : pieces + 1, :]
        shift = ((place - 3) * GROUP) % LANES
        value = pltpu.roll(value, shift, 1) if shift else value
        if place == 0:
            label_rows.append(value)
        else:
            label_rows[-1] = jnp.where(lane >= place * GROUP, value, label_rows[-1])
    cells_all = MAXD * all_tiles
    cell_no = lax.broadcasted_iota(jnp.int32, (cells_all, LANES), 0).astype(f32)
    to_cells = jnp.concatenate(
        [jnp.where(cell_no == row, 1.0, 0.0).astype(bf16) for row in label_rows], axis=1
    )
    upright = jnp.concatenate([jnp.broadcast_to(row, (SUBL, LANES)).T for row in label_rows], axis=0)
    cell_no = lax.broadcasted_iota(jnp.int32, (all_pieces, cells_all), 1).astype(f32)
    to_pieces = jnp.where(cell_no == upright[:, :1], 1.0, 0.0).astype(bf16)

    def moved(matrix, values):
        triple = jnp.concatenate([part.astype(bf16) for part in split3(values)], axis=1)
        wide = jnp.dot(matrix, triple, preferred_element_type=f32)
        return wide[:, :LANES] + wide[:, LANES : 2 * LANES] + wide[:, 2 * LANES :]

    data = arrived_ref[:, :pieces, :].reshape(all_pieces, LANES)
    cells = moved(to_cells, data)
    goal = arrived_ref[:, pieces:, :].reshape(all_tiles, LANES)
    lane = lax.broadcasted_iota(jnp.int32, (all_tiles, LANES), 1)
    last = lane >= 3 * GROUP
    backdrop = jnp.where(
        lane < GROUP,
        background_ref[0],
        jnp.where(lane < 2 * GROUP, background_ref[1], background_ref[2]),
    )

    def spread(value):
        return pltpu.roll(value, GROUP, 1) + pltpu.roll(value, 2 * GROUP, 1) + pltpu.roll(
            value, 3 * GROUP, 1
        )

    fronts, through, layers = [], [], []
    front = jnp.ones((all_tiles, LANES), f32)
    composite = jnp.zeros((all_tiles, LANES), f32)
    for depth in range(MAXD):
        layer = cells[depth * all_tiles : (depth + 1) * all_tiles]
        passed = jnp.where(last, 1.0 - layer, 0.0)
        passed = passed + spread(passed)
        fronts.append(front)
        through.append(passed)
        layers.append(layer)
        composite = composite + front * layer
        front = front * passed
    residual = jnp.where(last, 0.0, composite + front * backdrop - goal)
    behind = backdrop
    grads = [None] * MAXD
    for depth in reversed(range(MAXD)):
        grads[depth] = fronts[depth] * jnp.where(last, spread(residual * behind), residual)
        behind = layers[depth] + through[depth] * behind
    back = moved(to_pieces, jnp.concatenate(grads, axis=0))
    out_ref[...] = back.reshape(out_ref.shape)


def backward_kernel(
    items_ref,
    back_ref,
    table_ref,
    basis_ref,
    own_ref,
    inner_ref,
    outer_ref,
    grad_ref,
    sums_ref,
    alpha_refs,
    shade_refs,
    local_refs,
    before_refs,
    hidden_refs,
):
    doms, pieces = back_ref.shape[0], back_ref.shape[1]
    own_blocks = own_ref.shape[1]
    width = PIX // doms
    lane = lax.broadcasted_iota(jnp.int32, (pieces, LANES), 1)
    grad_ref[...] = jnp.zeros_like(grad_ref)
    sums_ref[...] = jnp.zeros_like(sums_ref)
    for half in range(PIX // LANES):
        for channel in range(4):
            gathered = None
            for dom in range(half * LANES // width, (half + 1) * LANES // width):
                offset = dom * width - half * LANES
                shift = (offset - channel * GROUP) % LANES
                value = back_ref[dom]
                value = pltpu.roll(value, shift, 1) if shift else value
                gathered = value if gathered is None else jnp.where(lane >= offset, value, gathered)
            first = half * (pieces + 1) * SUBL + channel
            grad_ref[pl.ds(first, pieces, stride=SUBL), :] = gathered

    def grads_of(piece):
        halves = []
        for half in range(PIX // LANES):
            first = pl.multiple_of((half * (pieces + 1) + piece) * SUBL, SUBL)
            halves.append(grad_ref[pl.ds(first, SUBL), :])
        grads = jnp.concatenate(halves, axis=1)
        upper = lax.broadcasted_iota(jnp.int32, grads.shape, 0) < 4
        high, middle, low = split3(grads)
        first = jnp.where(upper, high, pltpu.roll(middle, 4, 0))
        return grads, first, jnp.where(upper, high, pltpu.roll(low, 4, 0))

    def front(item, side):
        chained, slots = item_slots(items_ref, item, pieces)
        carry, ends = None, []
        for slot, (piece, start) in enumerate(slots):
            alphas = jnp.exp2(exponents(table_ref, basis_ref, piece, start, pieces))
            grads, first, second = grads_of(piece)
            rhs = jnp.concatenate([first, second], axis=0).astype(bf16)
            rhs = jnp.concatenate([jnp.zeros((KE, PIX), bf16), rhs], axis=0)
            shades = jnp.dot(table_ref[pl.ds(start, BLOCK), :], rhs, preferred_element_type=f32)
            span = slice(slot * BLOCK, (slot + 1) * BLOCK)
            alpha_refs[side][span, :] = alphas
            shade_refs[side][span, :] = shades
            keep, total = None, None
            for row in range(ROWS):
                alpha = alphas[row * SUBL : (row + 1) * SUBL]
                weight = alpha if keep is None else alpha * keep
                keep = 1.0 - alpha if keep is None else keep - weight
                value = weight * shades[row * SUBL : (row + 1) * SUBL]
                total = value if total is None else total + value
                first = slot * BLOCK + row * SUBL
                local_refs[side][first : first + SUBL, :] = weight
            before, whole = prefix_product(keep)
            if slot == 1:
                before = before * jnp.where(chained, carry, 1.0)
            carry = whole
            before_refs[side][slot * SUBL : (slot + 1) * SUBL, :] = before
            ends.append((total, keep, grads[3:4]))
        behind = None
        for slot in (1, 0):
            total, keep, final = ends[slot]
            behind = jnp.where(chained, behind, final) if slot == 0 else final
            hidden, behind = suffix_affine(total, keep, behind)
            hidden_refs[side][slot * SUBL : (slot + 1) * SUBL, :] = hidden

    def back(item, side):
        along = (((1,), (1,)), ((), ()))
        _, slots = item_slots(items_ref, item, pieces)
        for slot, (piece, start) in enumerate(slots):
            before = before_refs[side][slot * SUBL : (slot + 1) * SUBL, :]
            hidden = hidden_refs[side][slot * SUBL : (slot + 1) * SUBL, :]
            pulls, weights = [None] * ROWS, [None] * ROWS
            for row in reversed(range(ROWS)):
                first = slot * BLOCK + row * SUBL
                span = slice(first, first + SUBL)
                weight = local_refs[side][span, :] * before
                gap = shade_refs[side][span, :] - hidden
                weights[row] = weight
                pulls[row] = weight * gap
                hidden = hidden + alpha_refs[side][span, :] * gap
            unit = basis_ref[jnp.minimum(piece, pieces - 1)][:TOP]
            _, first, second = grads_of(piece)
            g_lhs = jnp.concatenate([first, second], axis=0).astype(bf16)
            for base, left, values in ((0, unit, pulls), (2, g_lhs, weights)):
                part = None
                for value in split2(jnp.concatenate(values, axis=0)):
                    product = lax.dot_general(left, value, along, preferred_element_type=f32)
                    part = product if part is None else part + product
                for group in range(2 if base == 0 else 1):
                    row = (base + group) * SLOTS * SUBL + start // BLOCK * SUBL
                    rows = pl.ds(pl.multiple_of(row, SUBL), SUBL)
                    sums_ref[rows, :] = (
                        sums_ref[rows, :] + part[group * SUBL : (group + 1) * SUBL]
                    )

    pipelined(items_ref[3 * (pieces + SUBL) + 1], front, back)

    def rows_of(row):
        group, place = divmod(row, SUBL)
        return sums_ref[pl.ds(group * SLOTS * SUBL + place, SLOTS, stride=SUBL), :]

    moments = [rows_of(0), rows_of(1), rows_of(2)]
    moments += [rows_of(3 + 2 * i) + rows_of(4 + 2 * i) for i in range(3)]
    terms = [value * ln_2 for value in moments]
    terms += [rows_of(TOP + i) + rows_of(TOP + 4 + i) for i in range(3)]
    order = lane_order((SLOTS, LANES), True)
    even = lax.axis_index("region") % 2 == 0
    inner_ref[...] = jnp.zeros_like(inner_ref)
    outer_ref[...] = jnp.zeros_like(outer_ref)
    for term_no, value in enumerate(terms):
        value = jnp.take_along_axis(value, order, axis=1)
        own_ref[term_no] = value[:own_blocks]
        high = value[own_blocks : own_blocks + 1]
        low = value[own_blocks + 1 : own_blocks + 2]
        inner_ref[term_no : term_no + 1, :] = jnp.where(even, high, low)
        outer_ref[term_no : term_no + 1, :] = jnp.where(even, low, high)


def update_kernel(
    params_ref,
    first_ref,
    second_ref,
    own_ref,
    inner_ref,
    outer_ref,
    gradient_ref,
    new_params_ref,
    new_first_ref,
    new_second_ref,
    rows_ref,
    grads_ref,
):
    own_blocks = own_ref.shape[1]
    for block in range(own_blocks):
        rows_ref[pl.ds(block, PARAMS, stride=own_blocks), :] = params_ref[
            :, block * BLOCK : (block + 1) * BLOCK
        ]
    rows = [rows_ref[i * own_blocks : (i + 1) * own_blocks, :] for i in range(PARAMS)]
    slot = lax.broadcasted_iota(jnp.int32, (own_blocks, LANES), 0)
    even = lax.axis_index("region") % 2 == 0
    from_low = jnp.where(even, outer_ref[...], inner_ref[...])
    from_high = jnp.where(even, inner_ref[...], outer_ref[...])
    cots = []
    for term_no in range(9):
        low = jnp.where(slot == 0, from_low[term_no : term_no + 1, :], 0.0)
        high = jnp.where(slot == own_blocks - 1, from_high[term_no : term_no + 1, :], 0.0)
        cots.append(own_ref[term_no] + low + high)
    _, pull_back = jax.vjp(splat_rows, rows)
    pulled = pull_back((cots[:6], cots[6:]))[0]
    for i in range(PARAMS):
        grads_ref[i * own_blocks : (i + 1) * own_blocks, :] = pulled[i]
    for block in range(own_blocks):
        span = slice(block * BLOCK, (block + 1) * BLOCK)
        gradient = grads_ref[pl.ds(block, PARAMS, stride=own_blocks), :]
        new_first = beta_one * first_ref[:, span] + (1 - beta_one) * gradient
        new_second = beta_two * second_ref[:, span] + (1 - beta_two) * gradient * gradient
        update = (
            new_first
            / (1 - beta_one**adam_step)
            / (jnp.sqrt(new_second / (1 - beta_two**adam_step)) + tiny)
        )
        gradient_ref[:, span] = gradient
        new_params_ref[:, span] = params_ref[:, span] - rate * update
        new_first_ref[:, span] = new_first
        new_second_ref[:, span] = new_second


def exchange(to_inner, to_outer):
    count = lax.axis_size("region")
    inner = [(i, i ^ 1) for i in range(count) if (i ^ 1) < count]
    outer = [(i, i + 1) for i in range(1, count - 1, 2)]
    outer += [(target, source) for source, target in outer]
    return lax.ppermute(to_inner, "region", inner), lax.ppermute(to_outer, "region", outer)


def on_device(
    params,
    first_moment,
    second_moment,
    piece_blocks,
    piece_live,
    piece_owner,
    piece_cell,
    target,
    background,
):
    own_blocks = params.shape[1] // BLOCK
    doms = lax.axis_size("dom")
    pieces = piece_live.shape[1]
    tiles = target.shape[1]
    even = lax.axis_index("region") % 2 == 0
    low, high = params[:, :BLOCK], params[:, -BLOCK:]
    inner, outer = exchange(jnp.where(even, high, low), jnp.where(even, low, high))
    basis = jnp.asarray(pixel_basis(pieces))
    smem = pl.BlockSpec(memory_space=pltpu.SMEM)
    vmem = pl.BlockSpec(memory_space=pltpu.VMEM)
    plane = pltpu.VMEM((2 * BLOCK, PIX), f32)
    strip = pltpu.VMEM((2 * SUBL, PIX), f32)
    piece_rows = pltpu.VMEM((PIX // LANES * (pieces + 1) * SUBL, LANES), f32)
    payload, table, items = pl.pallas_call(
        forward_kernel,
        out_shape=(
            jax.ShapeDtypeStruct((doms, pieces + tiles, LANES), f32),
            jax.ShapeDtypeStruct(((own_blocks + 3) * BLOCK, KT), bf16),
            jax.ShapeDtypeStruct((3 * (pieces + SUBL) + 2,), jnp.int32),
        ),
        in_specs=[smem] * 2 + [vmem] * 7,
        out_specs=(vmem, vmem, smem),
        scratch_shapes=[
            pltpu.VMEM((64 * SUBL, LANES), f32),
            pltpu.VMEM((64 * SUBL, LANES), f32),
            pltpu.VMEM(((KT // SUBL + 1) * SLOTS * SUBL, LANES), f32),
            pltpu.VMEM((own_blocks + 3, TOP, LANES), bf16),
            piece_rows,
            [plane] * 2,
            [strip] * 2,
            [strip] * 2,
        ],
        name="forward",
    )(
        piece_blocks[0].T,
        piece_live,
        piece_owner,
        piece_cell,
        params,
        inner,
        outer,
        jnp.transpose(target[0], (1, 0, 2)),
        basis,
    )
    arrived = lax.all_to_all(payload, "dom", split_axis=0, concat_axis=0, tiled=True)
    back = pl.pallas_call(
        composite_kernel,
        out_shape=jax.ShapeDtypeStruct((doms, pieces, LANES), f32),
        in_specs=[smem, vmem],
        out_specs=vmem,
        name="composite",
    )(background, arrived)
    returned = lax.all_to_all(back, "dom", split_axis=0, concat_axis=0, tiled=True)
    own, to_inner, to_outer = pl.pallas_call(
        backward_kernel,
        out_shape=(
            jax.ShapeDtypeStruct((9, own_blocks, LANES), f32),
            jax.ShapeDtypeStruct((SLOTS, LANES), f32),
            jax.ShapeDtypeStruct((SLOTS, LANES), f32),
        ),
        in_specs=[smem] + [vmem] * 3,
        out_specs=(vmem, vmem, vmem),
        scratch_shapes=[
            piece_rows,
            pltpu.VMEM((3 * SLOTS * SUBL, LANES), f32),
            [plane] * 2,
            [plane] * 2,
            [plane] * 2,
            [strip] * 2,
            [strip] * 2,
        ],
        name="backward",
    )(items, returned, table, basis)
    inner, outer = exchange(to_inner, to_outer)
    shape = jax.ShapeDtypeStruct(params.shape, f32)
    return pl.pallas_call(
        update_kernel,
        out_shape=(shape, shape, shape, shape),
        in_specs=[vmem] * 6,
        out_specs=(vmem,) * 4,
        scratch_shapes=[
            pltpu.VMEM((64 * own_blocks, LANES), f32),
            pltpu.VMEM((64 * own_blocks, LANES), f32),
        ],
        name="update",
    )(params, first_moment, second_moment, own, inner, outer)


def solution(mesh):
    in_specs = (
        P(None, ("region", "dom")),
        P(None, ("region", "dom")),
        P(None, ("region", "dom")),
        P(("region", "dom"), None, None),
        P(("region", "dom"), None),
        P(("region", "dom"), None),
        P(("region", "dom"), None),
        P(("region", "dom"), None, None, None),
        P(),
    )
    out_specs = (P(None, ("region", "dom")),) * 4
    return jax.shard_map(
        on_device, mesh=mesh, in_specs=in_specs, out_specs=out_specs, check_vma=False
    )
```

time: 72.1 us -> 62 us (0.86)
  Pallas kernels: 32.2 us -> 22.7 us
  waiting for transfers between devices: 1.32 us -> 4.35 us
  other arithmetic: 3.42 us -> 0.78 us
  local copies, waits for them, and re-layouts: 1.97 us -> 1.21 us
    pallas_call x1, Pallas kernels: 17.5 us -> 9.89 us  [on_device(): pl.pallas_call(backward_kernel, out_shape=(jax.ShapeDtypeStruct((9, own_b...]
    ppermute x4, waiting for transfers between devices: 1.32 us -> 4.35 us  [the longest x2 4.35 us: exchange(): lax.ppermute(to_outer, 'region', outer)]
    select_n x4 -> x1, other arithmetic: 2.75 us -> 0.78 us  [on_device(): jnp.where(even, low, high)]
    pallas_call x1, Pallas kernels: 9.62 us -> 7.68 us  [on_device(): pl.pallas_call(forward_kernel, out_shape=(jax.ShapeDtypeStruct((doms, pie...]
  transfers between devices with their start and end apart: 4 -> 4, of which waited for: 1 -> 2; matrix products, arithmetic and copies ran while one was open for 4% -> 0% of each run, Pallas kernels for 0% -> 0%
where the time goes in v2:
time: 62 us; the launch traced here: 61.4 us
  blocking collectives  22.8 us (37%)
  Pallas kernels  22.7 us (37%)
  starting transfers between devices  8.91 us (14%)
  waiting for transfers between devices  4.35 us (7%)
  local copies, waits for them, and re-layouts  1.21 us (2%)
  other arithmetic  0.78 us (1%)
  between operations  0.7 us (1%)
    all_to_all x1, blocking collectives, on_device(): lax.all_to_all(payload, 'dom', split_axis=0, concat_axis=0, tiled=True)  12.6 us
    all_to_all x1, blocking collectives, on_device(): lax.all_to_all(back, 'dom', split_axis=0, concat_axis=0, tiled=True)  10.2 us
    pallas_call x1, Pallas kernels, on_device(): pl.pallas_call(backward_kernel, out_shape=(jax.ShapeDtypeStruct((9, own_b...  9.89 us
    pallas_call x1, Pallas kernels, on_device(): pl.pallas_call(forward_kernel, out_shape=(jax.ShapeDtypeStruct((doms, pie...  7.68 us
    ppermute x2, starting transfers between devices, exchange(): lax.ppermute(to_outer, 'region', outer)  6.78 us
    ppermute x2, waiting for transfers between devices, exchange(): lax.ppermute(to_outer, 'region', outer)  4.35 us
    pallas_call x1, Pallas kernels, on_device(): pl.pallas_call(composite_kernel, out_shape=jax.ShapeDtypeStruct((doms, pi...  2.59 us
    pallas_call x1, Pallas kernels, on_device(): pl.pallas_call(update_kernel, out_shape=(shape, shape, shape, shape), in_...  2.48 us
  transfers between devices with their start and end apart: 4, of which 2 were waited for; matrix products, arithmetic and copies ran while one was open for 0% of the time, Pallas kernels for 0%

profile of v2, /device:TPU:1, one launch (start us, length us, event | category | flops | bytes accessed | tf_op | source)
XLA Modules:
  0.0 61.4 jit_solution(9475398917690040261)
XLA Ops:
  0.6 0.8 %slice_select_fusion = (f32[59,128]{1,0:T(8,128)S(1)}, f32[59,128]{1,0:T(8,128)S(1)}) fusion(f32[59,1024]{1,0:T(8,128)} %params_ref.3, pred[]{:T(512)S(6)} %eq.5), kind=kLoop, calls=%fused_computation | loop fusion | flops 15104 | bytes 120833 | tf_op jit(solution)/shard_map/jit(_where)/select_n | solution.py:669
  1.4 4.5 %collective-permute-start.1 = (f32[59,128]{1,0:T(8,128)S(1)}, f32[59,128]{1,0:T(8,128)S(1)}, u32[]{:S(2)}, u32[]{:S(2)}) collective-permute-start(f32[59,128]{1,0:T(8,128)S(1)} %get-tuple-element.16), channel_id=1, source_target_pairs={{8,16},{16,8},{9,17},{17,9},{10,18},{18,10},{11,19},{19,11},{12,20... | collective-permute-start | bytes 90632 | tf_op jit(solution)/shard_map/ppermute | solution.py:649
  5.9 0.1 collective-permute-start
  6.0 1.5 %collective-permute-done.1.outer_ref = f32[59,128]{1,0:T(8,128)S(1)} collective-permute-done((f32[59,128]{1,0:T(8,128)S(1)}, f32[59,128]{1,0:T(8,128)S(1)}, u32[]{:S(2)}, u32[]{:S(2)}) %collective-permute-start.1) | collective-permute-done | bytes 30240 | tf_op jit(solution)/shard_map/ppermute | solution.py:649
  7.5 0.0 copy-start
  7.5 0.0 collective-permute-done.inner_ref
  7.5 0.0 copy-start.1
  7.5 0.6 copy-done
  8.1 0.0 copy-done.1
  8.1 7.7 %forward.1 = (f32[8,40,128]{2,1,0:T(8,128)}, bf16[1408,48]{1,0:T(8,128)(2,1)}, s32[122]{0:T(128)}) custom-call(s32[2,32]{1,0:T(2,128)} %bitcast.7, s32[1,32]{1,0:T(1,128)} %live_ref.1, s32[1,32]{1,0:T(1,128)} %owner_ref.1, s32[1,32]{1,0:T(1,128)} %cell_ref.1, f32[59,1024]{1,0:T(8,128)} %params_ref.3, f32[59,128]{1,0:T(8,128)} %copy-done.1, ...), custom_call_target="tpu_custom_call" | custom-call | tf_op jit(solution)/shard_map/forward/pallas_call | solution.py:676
  15.8 12.6 %all_to_all.10.arrived_ref = f32[8,40,128]{2,1,0:T(8,128)} all-to-all(f32[8,40,128]{2,1,0:T(8,128)} %get-tuple-element.11), channel_id=1, replica_groups=mesh['region'=4,'dom'=8] {'dom'}, dimensions={0} | all-to-all | bytes 327680 | tf_op jit(solution)/shard_map/all_to_all | solution.py:707
  28.4 2.6 %composite.1 = f32[8,32,128]{2,1,0:T(8,128)} custom-call(f32[3]{0:T(128)} %background_ref.1, f32[8,40,128]{2,1,0:T(8,128)} %all_to_all.10.arrived_ref), custom_call_target="tpu_custom_call" | custom-call | tf_op jit(solution)/shard_map/composite/pallas_call | solution.py:708
  31.0 10.2 %all_to_all.11.back_ref = f32[8,32,128]{2,1,0:T(8,128)} all-to-all(f32[8,32,128]{2,1,0:T(8,128)} %composite.1), channel_id=1, replica_groups=mesh['region'=4,'dom'=8] {'dom'}, dimensions={0} | all-to-all | bytes 262144 | tf_op jit(solution)/shard_map/all_to_all | solution.py:715
  41.2 9.9 %backward.1 = (f32[9,8,128]{2,1,0:T(8,128)}, f32[16,128]{1,0:T(8,128)}, f32[16,128]{1,0:T(8,128)}) custom-call(s32[122]{0:T(128)} %get-tuple-element.10.items_ref, f32[8,32,128]{2,1,0:T(8,128)} %all_to_all.11.back_ref, bf16[1408,48]{1,0:T(8,128)(2,1)} %get-tuple-element.12.table_ref, bf16[32,32,256]{2,1,0:T(8,128)(2,1)} %constant.21.clone.basis_ref), custom_call_target="tpu_custom_call" | custom-call | tf_op jit(solution)/shard_map/backward/pallas_call | solution.py:716
  51.1 2.1 %collective-permute-start.2 = (f32[16,128]{1,0:T(8,128)}, f32[16,128]{1,0:T(8,128)S(1)}, u32[]{:S(2)}, u32[]{:S(2)}) collective-permute-start(f32[16,128]{1,0:T(8,128)} %get-tuple-element.14), channel_id=1, source_target_pairs={{0,8},{8,0},{16,24},{24,16},{1,9},{9,1},{17,25},{25,17},{2,10},{10... | collective-permute-start | bytes 24584 | tf_op jit(solution)/shard_map/ppermute | solution.py:649
  53.1 2.3 %collective-permute-start.3 = (f32[16,128]{1,0:T(8,128)}, f32[16,128]{1,0:T(8,128)S(1)}, u32[]{:S(2)}, u32[]{:S(2)}) collective-permute-start(f32[16,128]{1,0:T(8,128)} %get-tuple-element.15), channel_id=1, source_target_pairs={{8,16},{16,8},{9,17},{17,9},{10,18},{18,10},{11,19},{19,11},{12,20... | collective-permute-start | bytes 24584 | tf_op jit(solution)/shard_map/ppermute | solution.py:649
  55.5 0.0 collective-permute-done.2.inner_ref
  55.5 0.0 copy-start.2
  55.5 2.8 %collective-permute-done.3.outer_ref = f32[16,128]{1,0:T(8,128)S(1)} collective-permute-done((f32[16,128]{1,0:T(8,128)}, f32[16,128]{1,0:T(8,128)S(1)}, u32[]{:S(2)}, u32[]{:S(2)}) %collective-permute-start.3) | collective-permute-done | bytes 8224 | tf_op jit(solution)/shard_map/ppermute | solution.py:649
  58.3 0.0 copy-start.3
  58.3 0.0 copy-done.2
  58.3 0.6 copy-done.3
  58.9 2.5 %update.1 = (f32[59,1024]{1,0:T(8,128)}, f32[59,1024]{1,0:T(8,128)}, f32[59,1024]{1,0:T(8,128)}, f32[59,1024]{1,0:T(8,128)}) custom-call(f32[59,1024]{1,0:T(8,128)} %params_ref.3, f32[59,1024]{1,0:T(8,128)} %first_ref.1, f32[59,1024]{1,0:T(8,128)} %second_ref.1, f32[9,8,128]{2,1,0:T(8,128)} %get-tuple-element.13.own_ref, f32[16,128]{1,0:T(8,128)} %copy-done.2, ...), custom_call_target="tpu_custom_call" | custom-call | tf_op jit(solution)/shard_map/update/pallas_call | solution.py:738
Async XLA Ops:
  1.4 6.1 %collective-permute-start.1 = (f32[59,128]{1,0:T(8,128)S(1)}, f32[59,128]{1,0:T(8,128)S(1)}, u32[]{:S(2)}, u32[]{:S(2)}) collective-permute-start(f32[59,128]{1,0:T(8,128)S(1)} %get-tuple-element.16), channel_id=1, source_target_pairs={{8,16},{16,8},{9,17},{17,9},{10,18},{18,10},{11,19},{19,11},{12,20... | collective-permute-start | bytes 90632 | tf_op jit(solution)/shard_map/ppermute | solution.py:649
  5.9 1.6 %collective-permute-start = (f32[59,128]{1,0:T(8,128)S(1)}, f32[59,128]{1,0:T(8,128)S(1)}, u32[]{:S(2)}, u32[]{:S(2)}) collective-permute-start(f32[59,128]{1,0:T(8,128)S(1)} %get-tuple-element.17), channel_id=1, source_target_pairs={{0,8},{8,0},{16,24},{24,16},{1,9},{9,1},{17,25},{25,17},{2,10},{10... | collective-permute-start | bytes 90632 | tf_op jit(solution)/shard_map/ppermute | solution.py:649
  7.5 0.6 %copy-start = (f32[59,128]{1,0:T(8,128)}, f32[59,128]{1,0:T(8,128)S(1)}, u32[]{:S(2)}) copy-start(f32[59,128]{1,0:T(8,128)S(1)} %collective-permute-done.1.outer_ref) | copy-start | bytes 90628
  7.5 0.6 %copy-start.1 = (f32[59,128]{1,0:T(8,128)}, f32[59,128]{1,0:T(8,128)S(1)}, u32[]{:S(2)}) copy-start(f32[59,128]{1,0:T(8,128)S(1)} %collective-permute-done.inner_ref) | copy-start | bytes 90628
  51.1 4.4 %collective-permute-start.2 = (f32[16,128]{1,0:T(8,128)}, f32[16,128]{1,0:T(8,128)S(1)}, u32[]{:S(2)}, u32[]{:S(2)}) collective-permute-start(f32[16,128]{1,0:T(8,128)} %get-tuple-element.14), channel_id=1, source_target_pairs={{0,8},{8,0},{16,24},{24,16},{1,9},{9,1},{17,25},{25,17},{2,10},{10... | collective-permute-start | bytes 24584 | tf_op jit(solution)/shard_map/ppermute | solution.py:649
  53.1 5.2 %collective-permute-start.3 = (f32[16,128]{1,0:T(8,128)}, f32[16,128]{1,0:T(8,128)S(1)}, u32[]{:S(2)}, u32[]{:S(2)}) collective-permute-start(f32[16,128]{1,0:T(8,128)} %get-tuple-element.15), channel_id=1, source_target_pairs={{8,16},{16,8},{9,17},{17,9},{10,18},{18,10},{11,19},{19,11},{12,20... | collective-permute-start | bytes 24584 | tf_op jit(solution)/shard_map/ppermute | solution.py:649
  55.5 2.9 %copy-start.2 = (f32[16,128]{1,0:T(8,128)}, f32[16,128]{1,0:T(8,128)S(1)}, u32[]{:S(2)}) copy-start(f32[16,128]{1,0:T(8,128)S(1)} %collective-permute-done.2.inner_ref) | copy-start | bytes 24580
  58.3 0.6 copy-start.3

commit v3 on v2

--- a/solution.py
+++ b/solution.py
@@ -51,6 +51,7 @@
 KT = KE + KC
 TOP = 16
 SLOTS = 16
+vmem_limit = 12 * 2**20
 f32 = jnp.float32
 bf16 = jnp.bfloat16
 
@@ -693,6 +694,7 @@
             [strip] * 2,
         ],
         name="forward",
+        compiler_params=pltpu.CompilerParams(vmem_limit_bytes=vmem_limit),
     )(
         piece_blocks[0].T,
         piece_live,
@@ -711,6 +713,7 @@
         in_specs=[smem, vmem],
         out_specs=vmem,
         name="composite",
+        compiler_params=pltpu.CompilerParams(vmem_limit_bytes=vmem_limit),
     )(background, arrived)
     returned = lax.all_to_all(back, "dom", split_axis=0, concat_axis=0, tiled=True)
     own, to_inner, to_outer = pl.pallas_call(
@@ -732,6 +735,7 @@
             [strip] * 2,
         ],
         name="backward",
+        compiler_params=pltpu.CompilerParams(vmem_limit_bytes=vmem_limit),
     )(items, returned, table, basis)
     inner, outer = exchange(to_inner, to_outer)
     shape = jax.ShapeDtypeStruct(params.shape, f32)
@@ -745,6 +749,7 @@
             pltpu.VMEM((64 * own_blocks, LANES), f32),
         ],
         name="update",
+        compiler_params=pltpu.CompilerParams(vmem_limit_bytes=vmem_limit),
     )(params, first_moment, second_moment, own, inner, outer)
 
 

time: 62 us -> 58.1 us (0.937)
  Pallas kernels: 22.7 us -> 17.3 us
  local copies, waits for them, and re-layouts: 1.21 us -> 2.71 us
  starting transfers between devices: 8.91 us -> 9.91 us
  blocking collectives: 22.8 us -> 22 us
    pallas_call x1, Pallas kernels: 9.89 us -> 8.05 us  [on_device(): pl.pallas_call(backward_kernel, out_shape=(jax.ShapeDtypeStruct((9, own_b...]
    unnamed x8 -> x24, local copies, waits for them, and re-layouts: 1.21 us -> 2.71 us
    pallas_call x1, Pallas kernels: 7.68 us -> 6.37 us  [on_device(): pl.pallas_call(forward_kernel, out_shape=(jax.ShapeDtypeStruct((doms, pie...]
    ppermute x2, starting transfers between devices: 2.13 us -> 3.29 us  [exchange(): lax.ppermute(to_inner, 'region', inner)]
    pallas_call x1, Pallas kernels: 2.48 us -> 1.36 us  [on_device(): pl.pallas_call(update_kernel, out_shape=(shape, shape, shape, shape), in_...]
    pallas_call x1, Pallas kernels: 2.59 us -> 1.55 us  [on_device(): pl.pallas_call(composite_kernel, out_shape=jax.ShapeDtypeStruct((doms, pi...]
where the time goes in v3:
time: 58.1 us; the launch traced here: 57.8 us
  blocking collectives  22 us (38%)
  Pallas kernels  17.3 us (30%)
  starting transfers between devices  9.91 us (17%)
  waiting for transfers between devices  4.31 us (7%)
  local copies, waits for them, and re-layouts  2.71 us (5%)
  other arithmetic  0.79 us (1%)
  between operations  0.75 us (1%)
    all_to_all x1, blocking collectives, on_device(): lax.all_to_all(payload, 'dom', split_axis=0, concat_axis=0, tiled=True)  12.4 us
    all_to_all x1, blocking collectives, on_device(): lax.all_to_all(back, 'dom', split_axis=0, concat_axis=0, tiled=True)  9.59 us
    pallas_call x1, Pallas kernels, on_device(): pl.pallas_call(backward_kernel, out_shape=(jax.ShapeDtypeStruct((9, own_b...  8.05 us
    ppermute x2, starting transfers between devices, exchange(): lax.ppermute(to_outer, 'region', outer)  6.62 us
    pallas_call x1, Pallas kernels, on_device(): pl.pallas_call(forward_kernel, out_shape=(jax.ShapeDtypeStruct((doms, pie...  6.37 us
    ppermute x2, waiting for transfers between devices, exchange(): lax.ppermute(to_outer, 'region', outer)  4.31 us
    ppermute x2, starting transfers between devices, exchange(): lax.ppermute(to_inner, 'region', inner)  3.29 us
    unnamed x24, local copies, waits for them, and re-layouts  2.71 us
  transfers between devices with their start and end apart: 4, of which 2 were waited for; matrix products, arithmetic and copies ran while one was open for 0% of the time, Pallas kernels for 0%

profile of v3, /device:TPU:1, one launch (start us, length us, event | category | flops | bytes accessed | tf_op | source)
XLA Modules:
  0.0 57.8 jit_solution(11840783365632672407)
XLA Ops:
  0.6 0.0 copy-start.6
  0.7 0.8 %slice_select_fusion = (f32[59,128]{1,0:T(8,128)S(1)}, f32[59,128]{1,0:T(8,128)S(1)}) fusion(f32[59,1024]{1,0:T(8,128)} %params_ref.3, pred[]{:T(512)S(6)} %eq.5), kind=kLoop, calls=%fused_computation | loop fusion | flops 15104 | bytes 120833 | tf_op jit(solution)/shard_map/jit(_where)/select_n | solution.py:670
  1.4 4.5 %collective-permute-start.1 = (f32[59,128]{1,0:T(8,128)S(1)}, f32[59,128]{1,0:T(8,128)S(1)}, u32[]{:S(2)}, u32[]{:S(2)}) collective-permute-start(f32[59,128]{1,0:T(8,128)S(1)} %get-tuple-element.16), channel_id=1, source_target_pairs={{8,16},{16,8},{9,17},{17,9},{10,18},{18,10},{11,19},{19,11},{12,20... | collective-permute-start | bytes 90632 | tf_op jit(solution)/shard_map/ppermute | solution.py:650
  5.9 0.1 collective-permute-start
  6.0 1.5 %collective-permute-done.1.outer_ref = f32[59,128]{1,0:T(8,128)S(1)} collective-permute-done((f32[59,128]{1,0:T(8,128)S(1)}, f32[59,128]{1,0:T(8,128)S(1)}, u32[]{:S(2)}, u32[]{:S(2)}) %collective-permute-start.1) | collective-permute-done | bytes 30240 | tf_op jit(solution)/shard_map/ppermute | solution.py:650
  7.5 0.0 collective-permute-done.inner_ref
  7.5 0.0 copy-start.9
  7.5 0.0 copy-start.10
  7.5 0.0 copy-start.8
  7.5 0.0 copy-done.6
  7.6 0.6 %copy-done.9 = s32[1,32]{1,0:T(1,128)S(1)} copy-done((s32[1,32]{1,0:T(1,128)S(1)}, s32[1,32]{1,0:T(1,128)}, u32[]{:S(2)}) %copy-start.9) | copy-done | bytes 152
  8.2 0.0 copy-done.10
  8.2 0.0 copy-done.7
  8.2 0.0 copy-done.8
  8.2 1.0 %copy-done = bf16[32,32,256]{2,1,0:T(8,128)(2,1)S(1)} copy-done((bf16[32,32,256]{2,1,0:T(8,128)(2,1)S(1)}, bf16[32,32,256]{2,1,0:T(8,128)(2,1)}, u32[]{:S(2)}) %copy-start) | copy-done | bytes 524312
  9.3 0.9 %copy-done.2 = f32[59,1024]{1,0:T(8,128)S(1)} copy-done((f32[59,1024]{1,0:T(8,128)S(1)}, f32[59,1024]{1,0:T(8,128)}, u32[]{:S(2)}) %copy-start.2) | copy-done | bytes 241688
  10.2 6.4 %forward.1 = (f32[8,40,128]{2,1,0:T(8,128)S(1)}, bf16[1408,48]{1,0:T(8,128)(2,1)S(1)}, s32[122]{0:T(128)S(1)}) custom-call(s32[2,32]{1,0:T(2,128)S(1)} %bitcast.7, s32[1,32]{1,0:T(1,128)S(1)} %copy-done.8, s32[1,32]{1,0:T(1,128)S(1)} %copy-done.9, s32[1,32]{1,0:T(1,128)S(1)} %copy-done.10, f32[59,1024]{1,0:T(8,128)S(1)} %copy-done.2, ...), custom_call_target="tpu_custom_call" | custom-call | tf_op jit(solution)/shard_map/forward/pallas_call | solution.py:677
  16.6 0.0 copy-start.1
  16.6 12.4 %all_to_all.10.arrived_ref = f32[8,40,128]{2,1,0:T(8,128)S(1)} all-to-all(f32[8,40,128]{2,1,0:T(8,128)S(1)} %get-tuple-element.11), channel_id=1, replica_groups=mesh['region'=4,'dom'=8] {'dom'}, dimensions={0} | all-to-all | bytes 327680 | tf_op jit(solution)/shard_map/all_to_all | solution.py:709
  29.0 0.0 copy-done.11
  29.0 1.5 %composite.1 = f32[8,32,128]{2,1,0:T(8,128)S(1)} custom-call(f32[3]{0:T(128)S(1)} %copy-done.11, f32[8,40,128]{2,1,0:T(8,128)S(1)} %all_to_all.10.arrived_ref), custom_call_target="tpu_custom_call" | custom-call | tf_op jit(solution)/shard_map/composite/pallas_call | solution.py:710
  30.6 9.6 %all_to_all.11.back_ref = f32[8,32,128]{2,1,0:T(8,128)S(1)} all-to-all(f32[8,32,128]{2,1,0:T(8,128)S(1)} %composite.1), channel_id=1, replica_groups=mesh['region'=4,'dom'=8] {'dom'}, dimensions={0} | all-to-all | bytes 262144 | tf_op jit(solution)/shard_map/all_to_all | solution.py:718
  40.2 0.0 copy-done.1
  40.2 8.0 %backward.1 = (f32[9,8,128]{2,1,0:T(8,128)S(1)}, f32[16,128]{1,0:T(8,128)S(1)}, f32[16,128]{1,0:T(8,128)S(1)}) custom-call(s32[122]{0:T(128)S(1)} %get-tuple-element.10.items_ref, f32[8,32,128]{2,1,0:T(8,128)S(1)} %all_to_all.11.back_ref, bf16[1408,48]{1,0:T(8,128)(2,1)S(1)} %get-tuple-element.12.table_ref, bf16[32,32,256]{2,1,0:T(8,128)(2,1)S(1)} %copy-done.1), custom_call_target="tpu_custom_call" | custom-call | tf_op jit(solution)/shard_map/backward/pallas_call | solution.py:719
  48.2 3.2 %collective-permute-start.2 = (f32[16,128]{1,0:T(8,128)S(1)}, f32[16,128]{1,0:T(8,128)S(1)}, u32[]{:S(2)}, u32[]{:S(2)}) collective-permute-start(f32[16,128]{1,0:T(8,128)S(1)} %get-tuple-element.14), channel_id=1, source_target_pairs={{0,8},{8,0},{16,24},{24,16},{1,9},{9,1},{17,25},{25,17},{2,10},{10... | collective-permute-start | bytes 24584 | tf_op jit(solution)/shard_map/ppermute | solution.py:650
  51.5 2.1 %collective-permute-start.3 = (f32[16,128]{1,0:T(8,128)S(1)}, f32[16,128]{1,0:T(8,128)S(1)}, u32[]{:S(2)}, u32[]{:S(2)}) collective-permute-start(f32[16,128]{1,0:T(8,128)S(1)} %get-tuple-element.15), channel_id=1, source_target_pairs={{8,16},{16,8},{9,17},{17,9},{10,18},{18,10},{11,19},{19,11},{12,20... | collective-permute-start | bytes 24584 | tf_op jit(solution)/shard_map/ppermute | solution.py:650
  53.6 0.0 collective-permute-done.2.inner_ref
  53.6 2.8 %collective-permute-done.3.outer_ref = f32[16,128]{1,0:T(8,128)S(1)} collective-permute-done((f32[16,128]{1,0:T(8,128)S(1)}, f32[16,128]{1,0:T(8,128)S(1)}, u32[]{:S(2)}, u32[]{:S(2)}) %collective-permute-start.3) | collective-permute-done | bytes 8224 | tf_op jit(solution)/shard_map/ppermute | solution.py:650
  56.4 0.0 copy-done.3
  56.4 0.0 copy-done.4
  56.4 0.0 copy-done.5
  56.4 1.4 %update.1 = (f32[59,1024]{1,0:T(8,128)}, f32[59,1024]{1,0:T(8,128)}, f32[59,1024]{1,0:T(8,128)}, f32[59,1024]{1,0:T(8,128)}) custom-call(f32[59,1024]{1,0:T(8,128)S(1)} %copy-done.3, f32[59,1024]{1,0:T(8,128)S(1)} %copy-done.4, f32[59,1024]{1,0:T(8,128)S(1)} %copy-done.5, f32[9,8,128]{2,1,0:T(8,128)S(1)} %get-tuple-element.13.own_ref, ...), custom_call_target="tpu_custom_call" | custom-call | tf_op jit(solution)/shard_map/update/pallas_call | solution.py:742
  (7 shorter events, 0.0 us)
Async XLA Ops:
  0.6 6.9 %copy-start.6 = (f32[1,8,3,256]{3,1,2,0:T(8,128)S(1)}, f32[1,8,3,256]{3,1,2,0:T(8,128)}, u32[]{:S(2)}) copy-start(f32[1,8,3,256]{3,1,2,0:T(8,128)} %param.17) | copy-start | bytes 73732
  1.4 6.1 %collective-permute-start.1 = (f32[59,128]{1,0:T(8,128)S(1)}, f32[59,128]{1,0:T(8,128)S(1)}, u32[]{:S(2)}, u32[]{:S(2)}) collective-permute-start(f32[59,128]{1,0:T(8,128)S(1)} %get-tuple-element.16), channel_id=1, source_target_pairs={{8,16},{16,8},{9,17},{17,9},{10,18},{18,10},{11,19},{19,11},{12,20... | collective-permute-start | bytes 90632 | tf_op jit(solution)/shard_map/ppermute | solution.py:650
  5.9 1.6 %collective-permute-start = (f32[59,128]{1,0:T(8,128)S(1)}, f32[59,128]{1,0:T(8,128)S(1)}, u32[]{:S(2)}, u32[]{:S(2)}) collective-permute-start(f32[59,128]{1,0:T(8,128)S(1)} %get-tuple-element.17), channel_id=1, source_target_pairs={{0,8},{8,0},{16,24},{24,16},{1,9},{9,1},{17,25},{25,17},{2,10},{10... | collective-permute-start | bytes 90632 | tf_op jit(solution)/shard_map/ppermute | solution.py:650
  7.5 0.7 %copy-start.9 = (s32[1,32]{1,0:T(1,128)S(1)}, s32[1,32]{1,0:T(1,128)}, u32[]{:S(2)}) copy-start(s32[1,32]{1,0:T(1,128)} %owner_ref.1) | copy-start | bytes 388
  7.5 0.7 %copy-start.10 = (s32[1,32]{1,0:T(1,128)S(1)}, s32[1,32]{1,0:T(1,128)}, u32[]{:S(2)}) copy-start(s32[1,32]{1,0:T(1,128)} %cell_ref.1) | copy-start | bytes 388
  7.5 0.7 %copy-start.7 = (s32[1,32,2]{1,2,0:T(2,128)S(1)}, s32[1,32,2]{1,2,0:T(2,128)}, u32[]{:S(2)}) copy-start(s32[1,32,2]{1,2,0:T(2,128)} %param.13) | copy-start | bytes 772
  7.5 0.7 %copy-start.8 = (s32[1,32]{1,0:T(1,128)S(1)}, s32[1,32]{1,0:T(1,128)}, u32[]{:S(2)}) copy-start(s32[1,32]{1,0:T(1,128)} %live_ref.1) | copy-start | bytes 388
  8.2 1.0 %copy-start = (bf16[32,32,256]{2,1,0:T(8,128)(2,1)S(1)}, bf16[32,32,256]{2,1,0:T(8,128)(2,1)}, u32[]{:S(2)}) copy-start(bf16[32,32,256]{2,1,0:T(8,128)(2,1)} %constant.21.clone.basis_ref) | copy-start | bytes 1572868
  9.3 0.9 %copy-start.2 = (f32[59,1024]{1,0:T(8,128)S(1)}, f32[59,1024]{1,0:T(8,128)}, u32[]{:S(2)}) copy-start(f32[59,1024]{1,0:T(8,128)} %params_ref.3) | copy-start | bytes 724996
  10.2 18.8 %copy-start.11 = (f32[3]{0:T(128)S(1)}, f32[3]{0:T(128)}, u32[]{:S(2)}) copy-start(f32[3]{0:T(128)} %background_ref.1) | copy-start | bytes 40
  16.6 23.6 %copy-start.1 = (bf16[32,32,256]{2,1,0:T(8,128)(2,1)S(1)}, bf16[32,32,256]{2,1,0:T(8,128)(2,1)}, u32[]{:S(2)}) copy-start(bf16[32,32,256]{2,1,0:T(8,128)(2,1)} %constant.21.clone.basis_ref) | copy-start | bytes 1572868
  40.2 16.2 %copy-start.3 = (f32[59,1024]{1,0:T(8,128)S(1)}, f32[59,1024]{1,0:T(8,128)}, u32[]{:S(2)}) copy-start(f32[59,1024]{1,0:T(8,128)} %params_ref.3) | copy-start | bytes 724996
  40.2 16.2 %copy-start.4 = (f32[59,1024]{1,0:T(8,128)S(1)}, f32[59,1024]{1,0:T(8,128)}, u32[]{:S(2)}) copy-start(f32[59,1024]{1,0:T(8,128)} %first_ref.1) | copy-start | bytes 724996
  40.2 16.2 %copy-start.5 = (f32[59,1024]{1,0:T(8,128)S(1)}, f32[59,1024]{1,0:T(8,128)}, u32[]{:S(2)}) copy-start(f32[59,1024]{1,0:T(8,128)} %second_ref.1) | copy-start | bytes 724996
  48.2 5.4 %collective-permute-start.2 = (f32[16,128]{1,0:T(8,128)S(1)}, f32[16,128]{1,0:T(8,128)S(1)}, u32[]{:S(2)}, u32[]{:S(2)}) collective-permute-start(f32[16,128]{1,0:T(8,128)S(1)} %get-tuple-element.14), channel_id=1, source_target_pairs={{0,8},{8,0},{16,24},{24,16},{1,9},{9,1},{17,25},{25,17},{2,10},{10... | collective-permute-start | bytes 24584 | tf_op jit(solution)/shard_map/ppermute | solution.py:650
  51.5 5.0 %collective-permute-start.3 = (f32[16,128]{1,0:T(8,128)S(1)}, f32[16,128]{1,0:T(8,128)S(1)}, u32[]{:S(2)}, u32[]{:S(2)}) collective-permute-start(f32[16,128]{1,0:T(8,128)S(1)} %get-tuple-element.15), channel_id=1, source_target_pairs={{8,16},{16,8},{9,17},{17,9},{10,18},{18,10},{11,19},{19,11},{12,20... | collective-permute-start | bytes 24584 | tf_op jit(solution)/shard_map/ppermute | solution.py:650

commit v4 on v2

--- a/solution.py
+++ b/solution.py
@@ -51,6 +51,7 @@
 KT = KE + KC
 TOP = 16
 SLOTS = 16
+vmem_limit = 12 * 2**20
 f32 = jnp.float32
 bf16 = jnp.bfloat16
 
@@ -196,106 +197,100 @@
 
 def list_items(blocks_ref, live_ref, items_ref, pieces, own_blocks):
     room = pieces + SUBL
-    doubles, singles = jnp.int32(0), jnp.int32(0)
+    size = 3 * room + 2
+    doubles = [jnp.int32(0), jnp.int32(size)]
+    singles = [jnp.int32(2 * room), jnp.int32(size + 2 * room)]
     for piece in range(pieces):
-        entries = []
+        places = []
         for slot in range(2):
             block = blocks_ref[slot, piece]
-            place = jnp.where(block == 0, own_blocks + 1, block - 1)
-            entries.append(place * 64 + piece)
-        items_ref[doubles] = entries[0]
-        items_ref[room + doubles] = entries[1]
-        items_ref[2 * room + singles] = entries[0]
+            places.append(jnp.where(block == 0, own_blocks + 1, block - 1))
         second = live_ref[0, piece] - 1
-        doubles = doubles + second
-        singles = singles + 1 - second
-    for spare in range(6):
-        items_ref[2 * room + singles + spare] = (own_blocks + 2) * 64 + pieces
-    items_ref[3 * room] = doubles
-    items_ref[3 * room + 1] = (doubles + (singles + 1) // 2 + 1) // 2
+        edge = jnp.where(second > 0, jnp.maximum(places[0], places[1]), places[0]) >= own_blocks
+        double = jnp.where(edge, doubles[1], doubles[0])
+        single = jnp.where(edge, singles[1], singles[0])
+        entry = places[0] * 64 + piece
+        items_ref[double] = entry
+        items_ref[room + double] = places[1] * 64 + piece
+        items_ref[single] = entry
+        edge_second = jnp.where(edge, second, 0)
+        edge_first = jnp.where(edge, 1 - second, 0)
+        doubles = [doubles[0] + second - edge_second, doubles[1] + edge_second]
+        singles = [singles[0] + 1 - second - edge_first, singles[1] + edge_first]
+    counts, sizes = [], []
+    for which in range(2):
+        for spare in range(6):
+            items_ref[singles[which] + spare] = (own_blocks + 2) * 64 + pieces
+        counts.append(doubles[which] - which * size)
+        sizes.append(counts[which] + (singles[which] - which * size - 2 * room + 1) // 2)
+    items_ref[size - 2] = counts[0]
+    items_ref[size - 1] = counts[1]
+    items_ref[2 * size - 2] = sizes[1]
+    items_ref[2 * size - 1] = sizes[0] + sizes[1]
+
+
+def item_ranges(items_ref, pieces):
+    size = 3 * (pieces + SUBL) + 2
+    return (items_ref[2 * size - 2] + 1) // 2, (items_ref[2 * size - 1] + 1) // 2
 
 
 def item_slots(items_ref, item, pieces):
     room = pieces + SUBL
-    doubles = items_ref[3 * room]
+    size = 3 * room + 2
+    edges = items_ref[2 * size - 2]
+    edge = item < edges
+    doubles = jnp.where(edge, items_ref[size - 1], items_ref[size - 2])
+    base = jnp.where(edge, size, 0)
+    item = jnp.where(edge, item, item - edges)
     chained = item < doubles
-    single = 2 * (room + item - doubles)
-    first = items_ref[jnp.where(chained, item, single)]
-    second = items_ref[jnp.where(chained, room + item, single + 1)]
-    slots = []
+    single = base + 2 * (room + item - doubles)
+    first = items_ref[jnp.where(chained, base + item, single)]
+    second = items_ref[jnp.where(chained, base + room + item, single + 1)]
+    found = [chained.astype(jnp.int32)]
     for entry in (first, second):
-        slots.append((entry % 64, pl.multiple_of(entry // 64 * BLOCK, BLOCK)))
-    return chained, slots
-
-
-def pipelined(pairs, front, back):
-    front(0, 0)
+        found += [entry & 63, lax.shift_right_logical(entry, 6)]
+    return tuple(found)
+
+
+def pipelined(items_ref, pieces, begin, end, multiply, front, back):
+    def slots_of(item):
+        return item_slots(items_ref, item, pieces)
+
+    first = slots_of(2 * begin)
+    front(first, multiply(first), 0)
 
     def step(pair, carry):
-        for side in range(2):
-            front(2 * pair + side + 1, 1 - side)
-            back(2 * pair + side, side)
-        return carry
-
-    lax.fori_loop(0, pairs, step, 0)
-
-
-def exponents(table_ref, basis_ref, piece, start, pieces):
+        this, middle, last = carry
+        ahead = multiply(middle)
+        further = multiply(last)
+        back(this, 0)
+        front(middle, ahead, 1)
+        back(middle, 1)
+        front(last, further, 0)
+        return last, slots_of(2 * pair + 3), slots_of(2 * pair + 4)
+
+    lax.fori_loop(begin, end, step, (first, slots_of(2 * begin + 1), slots_of(2 * begin + 2)))
+
+
+def block_rows(block):
+    return pl.ds(pl.multiple_of(block * BLOCK, BLOCK), BLOCK)
+
+
+def exponents(table_ref, basis_ref, piece, block, pieces):
     unit = basis_ref[jnp.minimum(piece, pieces - 1)]
     rhs = jnp.concatenate([unit, jnp.zeros((KC, PIX), bf16)], axis=0)
-    return jnp.dot(table_ref[pl.ds(start, BLOCK), :], rhs, preferred_element_type=f32)
-
-
-def forward_kernel(
-    blocks_ref,
-    live_ref,
-    owner_ref,
-    cell_ref,
-    params_ref,
-    inner_ref,
-    outer_ref,
-    target_ref,
-    basis_ref,
-    out_ref,
-    table_ref,
-    items_ref,
-    own_rows_ref,
-    copy_rows_ref,
-    stage_ref,
-    colour_ref,
-    result_ref,
-    local_refs,
-    before_refs,
-    left_refs,
-):
-    doms, pieces = out_ref.shape[0], basis_ref.shape[0]
-    own_blocks = params_ref.shape[1] // BLOCK
-    region_idx, regions = lax.axis_index("region"), lax.axis_size("region")
-    even = region_idx % 2 == 0
-    list_items(blocks_ref, live_ref, items_ref, pieces, own_blocks)
-    for block in range(own_blocks):
-        own_rows_ref[pl.ds(block, PARAMS, stride=SUBL), :] = params_ref[
-            :, block * BLOCK : (block + 1) * BLOCK
-        ]
-    inner, outer = inner_ref[...], outer_ref[...]
-    copy_rows_ref[pl.ds(0, PARAMS, stride=SUBL), :] = jnp.where(even, inner, outer)
-    copy_rows_ref[pl.ds(1, PARAMS, stride=SUBL), :] = jnp.where(even, outer, inner)
-    rows = []
-    for i in range(PARAMS):
-        span = slice(i * SUBL, (i + 1) * SUBL)
-        rows.append(jnp.concatenate([own_rows_ref[span, :], copy_rows_ref[span, :]], axis=0))
+    return jnp.dot(table_ref[block_rows(block), :], rhs, preferred_element_type=f32)
+
+
+def fill_tables(rows, present, places, stage_ref, table_ref, colour_ref):
     coefs, colours = splat_rows(rows)
-    shape = (SLOTS, LANES)
-    slot_no = lax.broadcasted_iota(jnp.int32, shape, 0)
-    present = (
-        (slot_no < own_blocks)
-        | ((slot_no == own_blocks) & (region_idx < regions - 1))
-        | ((slot_no == own_blocks + 1) & (region_idx > 0))
-    )
+    shape = (SUBL, LANES)
     order = lane_order(shape, False)
 
     def settled(value, absent):
-        return jnp.take_along_axis(jnp.where(present, value, absent), order, axis=1)
+        if present is not None:
+            value = jnp.where(present, value, absent)
+        return jnp.take_along_axis(value, order, axis=1)
 
     coefs = [settled(value, -1e9 if i == 0 else 0.0) for i, value in enumerate(coefs)]
     colours = [settled(value, 0.0) for value in colours]
@@ -308,23 +303,32 @@
         lines += [triple[level] for triple in triples] + [nothing]
     for row, value in enumerate(lines):
         group, place = divmod(row, SUBL)
-        base = group * SLOTS * SUBL + place
-        stage_ref[pl.ds(base, SUBL, stride=SUBL), :] = value[:SUBL]
-        stage_ref[pl.ds(base + SUBL * SUBL, 4, stride=SUBL), :] = value[SUBL : SUBL + 4]
-    for block in range(own_blocks + 3):
+        stage_ref[pl.ds(group * SUBL * SUBL + place, SUBL, stride=SUBL), :] = value
+    for sublane, block in enumerate(places):
         tiles = [
-            stage_ref[(group * SLOTS + block) * SUBL : (group * SLOTS + block + 1) * SUBL, :]
+            stage_ref[(group * SUBL + sublane) * SUBL : (group * SUBL + sublane + 1) * SUBL, :]
             for group in range(len(lines) // SUBL)
         ]
         span = slice(block * BLOCK, (block + 1) * BLOCK)
         table_ref[span, :] = jnp.concatenate(tiles[: KT // SUBL], axis=0).T.astype(bf16)
         colour_ref[block] = jnp.concatenate(tiles[KT // SUBL :] * 2, axis=0).astype(bf16)
 
-    def front(item, side):
-        chained, slots = item_slots(items_ref, item, pieces)
+
+def render_items(begin, end, items_ref, table_ref, colour_ref, basis_ref, result_ref, scratch):
+    local_refs, before_refs, left_refs = scratch
+    pieces = basis_ref.shape[0]
+
+    def multiply(found):
+        return [
+            exponents(table_ref, basis_ref, found[1 + 2 * slot], found[2 + 2 * slot], pieces)
+            for slot in range(2)
+        ]
+
+    def front(found, powers, side):
+        chained = found[0] > 0
         carry = None
-        for slot, (piece, start) in enumerate(slots):
-            alphas = jnp.exp2(exponents(table_ref, basis_ref, piece, start, pieces))
+        for slot in range(2):
+            alphas = jnp.exp2(powers[slot])
             keep = None
             for row in range(ROWS):
                 alpha = alphas[row * SUBL : (row + 1) * SUBL]
@@ -340,17 +344,18 @@
             before_refs[side][slot * SUBL : (slot + 1) * SUBL, :] = before
             left_refs[side][slot : slot + 1, :] = total
 
-    def back(item, side):
-        chained, slots = item_slots(items_ref, item, pieces)
+    def back(found, side):
+        chained = found[0] > 0
         sums = None
-        for slot, (piece, start) in enumerate(slots):
+        for slot in range(2):
+            piece, block = found[1 + 2 * slot], found[2 + 2 * slot]
             before = before_refs[side][slot * SUBL : (slot + 1) * SUBL, :]
             weights = []
             for row in range(ROWS):
                 first = slot * BLOCK + row * SUBL
                 weights.append(local_refs[side][first : first + SUBL, :] * before)
             high, low = split2(jnp.concatenate(weights, axis=0))
-            left = colour_ref[start // BLOCK]
+            left = colour_ref[block]
             wide = jnp.dot(left, high, preferred_element_type=f32)
             wide = (wide + jnp.dot(left, low, preferred_element_type=f32))[:SUBL]
             wide = wide + pltpu.roll(wide, 4, 0)
@@ -361,11 +366,71 @@
                 first = pl.multiple_of((half * (pieces + 1) + piece) * SUBL, SUBL)
                 result_ref[pl.ds(first, SUBL), :] = value[:, half * LANES : (half + 1) * LANES]
 
-    pipelined(items_ref[3 * (pieces + SUBL) + 1], front, back)
-    width = PIX // doms
-    lane = lax.broadcasted_iota(jnp.int32, (pieces, LANES), 1)
+    pipelined(items_ref, pieces, begin, end, multiply, front, back)
+
+
+def forward_kernel(
+    far_blocks_ref,
+    far_live_ref,
+    far_params_ref,
+    far_basis_ref,
+    far_owner_ref,
+    far_cell_ref,
+    far_target_ref,
+    table_ref,
+    colour_ref,
+    result_ref,
+    basis_ref,
+    aimed_ref,
+    items_ref,
+    blocks_ref,
+    live_ref,
+    params_ref,
+    owner_ref,
+    cell_ref,
+    target_ref,
+    arrivals,
+    rows_ref,
+    stage_ref,
+    *scratch,
+):
+    pieces = basis_ref.shape[0]
+    own_blocks = params_ref.shape[1] // BLOCK
+    moves = (
+        (far_blocks_ref, blocks_ref),
+        (far_live_ref, live_ref),
+        (far_params_ref, params_ref),
+        (far_owner_ref, owner_ref),
+        (far_cell_ref, cell_ref),
+        (far_target_ref, target_ref),
+        (far_basis_ref, basis_ref),
+    )
+    fetches = [
+        pltpu.make_async_copy(far, near, arrivals.at[i]) for i, (far, near) in enumerate(moves)
+    ]
+    for fetch in fetches:
+        fetch.start()
+    fetches[0].wait()
+    fetches[1].wait()
+    list_items(blocks_ref, live_ref, items_ref, pieces, own_blocks)
+    fetches[2].wait()
+    for block in range(own_blocks):
+        rows_ref[pl.ds(block, PARAMS, stride=SUBL), :] = params_ref[
+            :, block * BLOCK : (block + 1) * BLOCK
+        ]
+    rows = [rows_ref[i * SUBL : (i + 1) * SUBL, :] for i in range(PARAMS)]
+    fill_tables(rows, None, range(own_blocks), stage_ref, table_ref, colour_ref)
+    empty = own_blocks + 2
+    column = lax.broadcasted_iota(jnp.int32, (BLOCK, KT), 1)
+    table_ref[empty * BLOCK : (empty + 1) * BLOCK, :] = jnp.where(column == 0, -1e9, 0.0).astype(
+        bf16
+    )
+    colour_ref[empty] = jnp.zeros((TOP, LANES), bf16)
+    for fetch in fetches[3:]:
+        fetch.wait()
+    doms = aimed_ref.shape[0]
+    width, tiles = PIX // doms, target_ref.shape[1]
     tile_lane = lax.broadcasted_iota(jnp.int32, (SUBL, LANES), 1)
-    tiles = target_ref.shape[1]
     cell = cell_ref[...]
     labels = (cell % MAXD) * (doms * tiles) + owner_ref[...] * tiles + cell // MAXD
     labels = jnp.concatenate(
@@ -375,21 +440,62 @@
     for dom in range(doms):
         half, offset = divmod(dom * width, LANES)
         span = slice(half * LANES, (half + 1) * LANES)
-        packed, aimed = None, None
+        aimed = labels
+        for channel in (2, 1, 0):
+            shift = (channel * GROUP - offset) % LANES
+            value = target_ref[channel, :, span]
+            value = pltpu.roll(value, shift, 1) if shift else value
+            aimed = jnp.where(tile_lane < (channel + 1) * GROUP, value, aimed)
+        aimed_ref[dom] = aimed
+    edge_pairs, pairs = item_ranges(items_ref, pieces)
+    render_items(edge_pairs, pairs, items_ref, table_ref, colour_ref, basis_ref, result_ref, scratch)
+
+
+def forward_edge_kernel(
+    items_ref,
+    inner_ref,
+    outer_ref,
+    aimed_ref,
+    basis_ref,
+    table_in_ref,
+    colour_in_ref,
+    result_in_ref,
+    table_ref,
+    colour_ref,
+    result_ref,
+    out_ref,
+    rows_ref,
+    stage_ref,
+    *scratch,
+):
+    del table_in_ref, colour_in_ref, result_in_ref
+    doms, pieces = out_ref.shape[0], basis_ref.shape[0]
+    own_blocks = table_ref.shape[0] // BLOCK - 3
+    region_idx, regions = lax.axis_index("region"), lax.axis_size("region")
+    even = region_idx % 2 == 0
+    inner, outer = inner_ref[...], outer_ref[...]
+    rows_ref[pl.ds(0, PARAMS, stride=SUBL), :] = jnp.where(even, inner, outer)
+    rows_ref[pl.ds(1, PARAMS, stride=SUBL), :] = jnp.where(even, outer, inner)
+    rows = [rows_ref[i * SUBL : (i + 1) * SUBL, :] for i in range(PARAMS)]
+    sublane = lax.broadcasted_iota(jnp.int32, (SUBL, LANES), 0)
+    present = ((sublane == 0) & (region_idx < regions - 1)) | ((sublane == 1) & (region_idx > 0))
+    places = (own_blocks, own_blocks + 1)
+    fill_tables(rows, present, places, stage_ref, table_ref, colour_ref)
+    render_items(0, item_ranges(items_ref, pieces)[0], items_ref, table_ref, colour_ref, basis_ref, result_ref, scratch)
+    width = PIX // doms
+    lane = lax.broadcasted_iota(jnp.int32, (pieces, LANES), 1)
+    tiles = aimed_ref.shape[1]
+    for dom in range(doms):
+        half, offset = divmod(dom * width, LANES)
+        packed = None
         for channel in range(4):
             shift = (channel * GROUP - offset) % LANES
             first = half * (pieces + 1) * SUBL + channel
             value = result_ref[pl.ds(first, pieces, stride=SUBL), :]
             value = pltpu.roll(value, shift, 1) if shift else value
             packed = value if packed is None else jnp.where(lane >= channel * GROUP, value, packed)
-            if channel < 3:
-                value = target_ref[channel, :, span]
-                value = pltpu.roll(value, shift, 1) if shift else value
-            else:
-                value = labels
-            aimed = value if aimed is None else jnp.where(tile_lane >= channel * GROUP, value, aimed)
         out_ref[dom, :pieces, :] = packed
-        out_ref[dom, pieces : pieces + tiles, :] = aimed
+        out_ref[dom, pieces : pieces + tiles, :] = aimed_ref[dom]
 
 
 def composite_kernel(background_ref, arrived_ref, out_ref):
@@ -460,39 +566,9 @@
     out_ref[...] = back.reshape(out_ref.shape)
 
 
-def backward_kernel(
-    items_ref,
-    back_ref,
-    table_ref,
-    basis_ref,
-    own_ref,
-    inner_ref,
-    outer_ref,
-    grad_ref,
-    sums_ref,
-    alpha_refs,
-    shade_refs,
-    local_refs,
-    before_refs,
-    hidden_refs,
-):
-    doms, pieces = back_ref.shape[0], back_ref.shape[1]
-    own_blocks = own_ref.shape[1]
-    width = PIX // doms
-    lane = lax.broadcasted_iota(jnp.int32, (pieces, LANES), 1)
-    grad_ref[...] = jnp.zeros_like(grad_ref)
-    sums_ref[...] = jnp.zeros_like(sums_ref)
-    for half in range(PIX // LANES):
-        for channel in range(4):
-            gathered = None
-            for dom in range(half * LANES // width, (half + 1) * LANES // width):
-                offset = dom * width - half * LANES
-                shift = (offset - channel * GROUP) % LANES
-                value = back_ref[dom]
-                value = pltpu.roll(value, shift, 1) if shift else value
-                gathered = value if gathered is None else jnp.where(lane >= offset, value, gathered)
-            first = half * (pieces + 1) * SUBL + channel
-            grad_ref[pl.ds(first, pieces, stride=SUBL), :] = gathered
+def pull_items(begin, end, items_ref, table_ref, basis_ref, grad_ref, sums_ref, scratch):
+    alpha_refs, shade_refs, local_refs, before_refs, hidden_refs = scratch
+    pieces = basis_ref.shape[0]
 
     def grads_of(piece):
         halves = []
@@ -505,15 +581,23 @@
         first = jnp.where(upper, high, pltpu.roll(middle, 4, 0))
         return grads, first, jnp.where(upper, high, pltpu.roll(low, 4, 0))
 
-    def front(item, side):
-        chained, slots = item_slots(items_ref, item, pieces)
-        carry, ends = None, []
-        for slot, (piece, start) in enumerate(slots):
-            alphas = jnp.exp2(exponents(table_ref, basis_ref, piece, start, pieces))
+    def multiply(found):
+        products = []
+        for slot in range(2):
+            piece, block = found[1 + 2 * slot], found[2 + 2 * slot]
             grads, first, second = grads_of(piece)
             rhs = jnp.concatenate([first, second], axis=0).astype(bf16)
             rhs = jnp.concatenate([jnp.zeros((KE, PIX), bf16), rhs], axis=0)
-            shades = jnp.dot(table_ref[pl.ds(start, BLOCK), :], rhs, preferred_element_type=f32)
+            shades = jnp.dot(table_ref[block_rows(block), :], rhs, preferred_element_type=f32)
+            powers = exponents(table_ref, basis_ref, piece, block, pieces)
+            products.append((powers, shades, grads[3:4]))
+        return products
+
+    def front(found, products, side):
+        chained = found[0] > 0
+        carry, ends = None, []
+        for slot, (powers, shades, final) in enumerate(products):
+            alphas = jnp.exp2(powers)
             span = slice(slot * BLOCK, (slot + 1) * BLOCK)
             alpha_refs[side][span, :] = alphas
             shade_refs[side][span, :] = shades
@@ -531,7 +615,7 @@
                 before = before * jnp.where(chained, carry, 1.0)
             carry = whole
             before_refs[side][slot * SUBL : (slot + 1) * SUBL, :] = before
-            ends.append((total, keep, grads[3:4]))
+            ends.append((total, keep, final))
         behind = None
         for slot in (1, 0):
             total, keep, final = ends[slot]
@@ -539,10 +623,10 @@
             hidden, behind = suffix_affine(total, keep, behind)
             hidden_refs[side][slot * SUBL : (slot + 1) * SUBL, :] = hidden
 
-    def back(item, side):
+    def back(found, side):
         along = (((1,), (1,)), ((), ()))
-        _, slots = item_slots(items_ref, item, pieces)
-        for slot, (piece, start) in enumerate(slots):
+        for slot in range(2):
+            piece, block = found[1 + 2 * slot], found[2 + 2 * slot]
             before = before_refs[side][slot * SUBL : (slot + 1) * SUBL, :]
             hidden = hidden_refs[side][slot * SUBL : (slot + 1) * SUBL, :]
             pulls, weights = [None] * ROWS, [None] * ROWS
@@ -563,14 +647,21 @@
                     product = lax.dot_general(left, value, along, preferred_element_type=f32)
                     part = product if part is None else part + product
                 for group in range(2 if base == 0 else 1):
-                    row = (base + group) * SLOTS * SUBL + start // BLOCK * SUBL
+                    row = (base + group) * SLOTS * SUBL + block * SUBL
                     rows = pl.ds(pl.multiple_of(row, SUBL), SUBL)
                     sums_ref[rows, :] = (
                         sums_ref[rows, :] + part[group * SUBL : (group + 1) * SUBL]
                     )
 
-    pipelined(items_ref[3 * (pieces + SUBL) + 1], front, back)
-
+    pipelined(items_ref, pieces, begin, end, multiply, front, back)
+
+
+def early_pairs(items_ref, pieces):
+    edge_pairs, pairs = item_ranges(items_ref, pieces)
+    return jnp.minimum(jnp.maximum(edge_pairs, pieces * 3 // 16), pairs), pairs
+
+
+def summed_terms(sums_ref):
     def rows_of(row):
         group, place = divmod(row, SUBL)
         return sums_ref[pl.ds(group * SLOTS * SUBL + place, SLOTS, stride=SUBL), :]
@@ -580,16 +671,58 @@
     terms = [value * ln_2 for value in moments]
     terms += [rows_of(TOP + i) + rows_of(TOP + 4 + i) for i in range(3)]
     order = lane_order((SLOTS, LANES), True)
+    return [jnp.take_along_axis(value, order, axis=1) for value in terms]
+
+
+def backward_edge_kernel(
+    items_ref,
+    back_ref,
+    table_ref,
+    basis_ref,
+    grad_ref,
+    sums_ref,
+    inner_ref,
+    outer_ref,
+    *scratch,
+):
+    doms, pieces = back_ref.shape[0], back_ref.shape[1]
+    own_blocks = table_ref.shape[0] // BLOCK - 3
+    width = PIX // doms
+    lane = lax.broadcasted_iota(jnp.int32, (pieces, LANES), 1)
+    grad_ref[...] = jnp.zeros_like(grad_ref)
+    sums_ref[...] = jnp.zeros_like(sums_ref)
+    for half in range(PIX // LANES):
+        for channel in range(4):
+            gathered = None
+            for dom in range(half * LANES // width, (half + 1) * LANES // width):
+                offset = dom * width - half * LANES
+                shift = (offset - channel * GROUP) % LANES
+                value = back_ref[dom]
+                value = pltpu.roll(value, shift, 1) if shift else value
+                gathered = value if gathered is None else jnp.where(lane >= offset, value, gathered)
+            first = half * (pieces + 1) * SUBL + channel
+            grad_ref[pl.ds(first, pieces, stride=SUBL), :] = gathered
+
+    early, _ = early_pairs(items_ref, pieces)
+    pull_items(0, early, items_ref, table_ref, basis_ref, grad_ref, sums_ref, scratch)
     even = lax.axis_index("region") % 2 == 0
     inner_ref[...] = jnp.zeros_like(inner_ref)
     outer_ref[...] = jnp.zeros_like(outer_ref)
-    for term_no, value in enumerate(terms):
-        value = jnp.take_along_axis(value, order, axis=1)
-        own_ref[term_no] = value[:own_blocks]
+    for term_no, value in enumerate(summed_terms(sums_ref)):
         high = value[own_blocks : own_blocks + 1]
         low = value[own_blocks + 1 : own_blocks + 2]
         inner_ref[term_no : term_no + 1, :] = jnp.where(even, high, low)
         outer_ref[term_no : term_no + 1, :] = jnp.where(even, low, high)
+
+
+def backward_kernel(
+    items_ref, table_ref, basis_ref, grad_ref, edge_sums_ref, own_ref, sums_ref, *scratch
+):
+    sums_ref[...] = edge_sums_ref[...]
+    early, pairs = early_pairs(items_ref, basis_ref.shape[0])
+    pull_items(early, pairs, items_ref, table_ref, basis_ref, grad_ref, sums_ref, scratch)
+    for term_no, value in enumerate(summed_terms(sums_ref)):
+        own_ref[term_no] = value[: own_ref.shape[1]]
 
 
 def update_kernel(
@@ -646,7 +779,8 @@
     inner = [(i, i ^ 1) for i in range(count) if (i ^ 1) < count]
     outer = [(i, i + 1) for i in range(1, count - 1, 2)]
     outer += [(target, source) for source, target in outer]
-    return lax.ppermute(to_inner, "region", inner), lax.ppermute(to_outer, "region", outer)
+    far = lax.ppermute(to_outer, "region", outer)
+    return lax.ppermute(to_inner, "region", inner), far
 
 
 def on_device(
@@ -672,37 +806,81 @@
     vmem = pl.BlockSpec(memory_space=pltpu.VMEM)
     plane = pltpu.VMEM((2 * BLOCK, PIX), f32)
     strip = pltpu.VMEM((2 * SUBL, PIX), f32)
-    piece_rows = pltpu.VMEM((PIX // LANES * (pieces + 1) * SUBL, LANES), f32)
-    payload, table, items = pl.pallas_call(
+    piece_rows = (PIX // LANES * (pieces + 1) * SUBL, LANES)
+    sums_shape = (3 * SLOTS * SUBL, LANES)
+    table_shape = jax.ShapeDtypeStruct(((own_blocks + 3) * BLOCK, KT), bf16)
+    colour_shape = jax.ShapeDtypeStruct((own_blocks + 3, TOP, LANES), bf16)
+    result_shape = jax.ShapeDtypeStruct(piece_rows, f32)
+    forward_scratch = [
+        pltpu.VMEM((64 * SUBL, LANES), f32),
+        pltpu.VMEM(((KT // SUBL + 1) * SUBL * SUBL, LANES), f32),
+        [plane] * 2,
+        [strip] * 2,
+        [strip] * 2,
+    ]
+    backward_scratch = [[plane] * 2, [plane] * 2, [plane] * 2, [strip] * 2, [strip] * 2]
+    params_limit = pltpu.CompilerParams(vmem_limit_bytes=vmem_limit)
+    table, colour, result, basis, aimed, items = pl.pallas_call(
         forward_kernel,
         out_shape=(
-            jax.ShapeDtypeStruct((doms, pieces + tiles, LANES), f32),
-            jax.ShapeDtypeStruct(((own_blocks + 3) * BLOCK, KT), bf16),
-            jax.ShapeDtypeStruct((3 * (pieces + SUBL) + 2,), jnp.int32),
+            table_shape,
+            colour_shape,
+            result_shape,
+            jax.ShapeDtypeStruct(basis.shape, bf16),
+            jax.ShapeDtypeStruct((doms, tiles, LANES), f32),
+            jax.ShapeDtypeStruct((2 * (3 * (pieces + SUBL) + 2),), jnp.int32),
         ),
-        in_specs=[smem] * 2 + [vmem] * 7,
-        out_specs=(vmem, vmem, smem),
+        in_specs=[pl.BlockSpec(memory_space=pltpu.HBM)] * 7,
+        out_specs=(vmem,) * 5 + (smem,),
         scratch_shapes=[
-            pltpu.VMEM((64 * SUBL, LANES), f32),
-            pltpu.VMEM((64 * SUBL, LANES), f32),
-            pltpu.VMEM(((KT // SUBL + 1) * SLOTS * SUBL, LANES), f32),
-            pltpu.VMEM((own_blocks + 3, TOP, LANES), bf16),
-            piece_rows,
-            [plane] * 2,
-            [strip] * 2,
-            [strip] * 2,
-        ],
+            pltpu.SMEM((2, pieces), jnp.int32),
+            pltpu.SMEM((1, pieces), jnp.int32),
+            pltpu.VMEM(params.shape, f32),
+            pltpu.VMEM((1, pieces), jnp.int32),
+            pltpu.VMEM((1, pieces), jnp.int32),
+            pltpu.VMEM((3, tiles, PIX), f32),
+            pltpu.SemaphoreType.DMA((7,)),
+        ]
+        + forward_scratch,
+        compiler_params=params_limit,
         name="forward",
     )(
-        piece_blocks[0].T,
-        piece_live,
-        piece_owner,
-        piece_cell,
-        params,
+        *[
+            pltpu.with_memory_space_constraint(value, pltpu.HBM)
+            for value in (
+                piece_blocks[0].T,
+                piece_live,
+                params,
+                basis,
+                piece_owner,
+                piece_cell,
+                jnp.transpose(target[0], (1, 0, 2)),
+            )
+        ]
+    )
+    table, _, _, payload = pl.pallas_call(
+        forward_edge_kernel,
+        out_shape=(
+            table_shape,
+            colour_shape,
+            result_shape,
+            jax.ShapeDtypeStruct((doms, pieces + tiles, LANES), f32),
+        ),
+        in_specs=[smem] + [vmem] * 7,
+        out_specs=(vmem,) * 4,
+        scratch_shapes=forward_scratch,
+        input_output_aliases={5: 0, 6: 1, 7: 2},
+        compiler_params=params_limit,
+        name="forward_edge",
+    )(
+        items,
         inner,
         outer,
-        jnp.transpose(target[0], (1, 0, 2)),
+        aimed,
         basis,
+        table,
+        colour,
+        result,
     )
     arrived = lax.all_to_all(payload, "dom", split_axis=0, concat_axis=0, tiled=True)
     back = pl.pallas_call(
@@ -710,30 +888,34 @@
         out_shape=jax.ShapeDtypeStruct((doms, pieces, LANES), f32),
         in_specs=[smem, vmem],
         out_specs=vmem,
+        compiler_params=params_limit,
         name="composite",
     )(background, arrived)
     returned = lax.all_to_all(back, "dom", split_axis=0, concat_axis=0, tiled=True)
-    own, to_inner, to_outer = pl.pallas_call(
-        backward_kernel,
+    grads, edge_sums, to_inner, to_outer = pl.pallas_call(
+        backward_edge_kernel,
         out_shape=(
-            jax.ShapeDtypeStruct((9, own_blocks, LANES), f32),
+            result_shape,
+            jax.ShapeDtypeStruct(sums_shape, f32),
             jax.ShapeDtypeStruct((SLOTS, LANES), f32),
             jax.ShapeDtypeStruct((SLOTS, LANES), f32),
         ),
         in_specs=[smem] + [vmem] * 3,
-        out_specs=(vmem, vmem, vmem),
-        scratch_shapes=[
-            piece_rows,
-            pltpu.VMEM((3 * SLOTS * SUBL, LANES), f32),
-            [plane] * 2,
-            [plane] * 2,
-            [plane] * 2,
-            [strip] * 2,
-            [strip] * 2,
-        ],
-        name="backward",
+        out_specs=(vmem,) * 4,
+        scratch_shapes=backward_scratch,
+        compiler_params=params_limit,
+        name="backward_edge",
     )(items, returned, table, basis)
     inner, outer = exchange(to_inner, to_outer)
+    own = pl.pallas_call(
+        backward_kernel,
+        out_shape=jax.ShapeDtypeStruct((9, own_blocks, LANES), f32),
+        in_specs=[smem] + [vmem] * 4,
+        out_specs=vmem,
+        scratch_shapes=[pltpu.VMEM(sums_shape, f32)] + backward_scratch,
+        compiler_params=params_limit,
+        name="backward",
+    )(items, table, basis, grads, edge_sums)
     shape = jax.ShapeDtypeStruct(params.shape, f32)
     return pl.pallas_call(
         update_kernel,
@@ -745,6 +927,7 @@
             pltpu.VMEM((64 * own_blocks, LANES), f32),
         ],
         name="update",
+        compiler_params=pltpu.CompilerParams(vmem_limit_bytes=vmem_limit),
     )(params, first_moment, second_moment, own, inner, outer)
 
 

time: 62 us -> 52.7 us (0.85)
  waiting for transfers between devices: 4.35 us -> 0.01 us
  Pallas kernels: 22.7 us -> 20.1 us
  blocking collectives: 22.8 us -> 20.3 us
  starting transfers between devices: 8.91 us -> 10.4 us
  local copies, waits for them, and re-layouts: 1.21 us -> 0.03 us
    ppermute x4, waiting for transfers between devices: 4.35 us -> 0.01 us  [the longest x2 0.01 us: exchange(): far = lax.ppermute(to_outer, 'region', outer)]
    all_to_all x1, blocking collectives: 10.2 us -> 8.59 us  [on_device(): lax.all_to_all(back, 'dom', split_axis=0, concat_axis=0, tiled=True)]
    ppermute x4, starting transfers between devices: 8.91 us -> 10.4 us  [the longest x2 6.46 us: exchange(): far = lax.ppermute(to_outer, 'region', outer)]
    unnamed x8, local copies, waits for them, and re-layouts: 1.21 us -> 0.03 us
    pallas_call x1, Pallas kernels: 2.48 us -> 1.36 us  [on_device(): pl.pallas_call(update_kernel, out_shape=(shape, shape, shape, shape), in_...]
    pallas_call x1, Pallas kernels: 2.59 us -> 1.55 us  [on_device(): pl.pallas_call(composite_kernel, out_shape=jax.ShapeDtypeStruct((doms, pi...]
    all_to_all x1, blocking collectives: 12.6 us -> 11.8 us  [on_device(): lax.all_to_all(payload, 'dom', split_axis=0, concat_axis=0, tiled=True)]
    pallas_call x2 -> x4, Pallas kernels: 17.6 us -> 17.2 us  [the longest x1 5.56 us: on_device(): pl.pallas_call(forward_kernel, out_shape=(table_shape, colour_shape, resu...]
  transfers between devices with their start and end apart: 4 -> 4, of which waited for: 2 -> 0; matrix products, arithmetic and copies ran while one was open for 0% -> 0% of each run, Pallas kernels for 0% -> 19%
where the time goes in v4:
time: 52.7 us; the launch traced here: 52.4 us
  blocking collectives  20.3 us (39%)
  Pallas kernels  20.1 us (38%)
  starting transfers between devices  10.4 us (20%)
  other arithmetic  0.78 us (1%)
  between operations  0.78 us (1%)
    all_to_all x1, blocking collectives, on_device(): lax.all_to_all(payload, 'dom', split_axis=0, concat_axis=0, tiled=True)  11.8 us
    all_to_all x1, blocking collectives, on_device(): lax.all_to_all(back, 'dom', split_axis=0, concat_axis=0, tiled=True)  8.59 us
    ppermute x2, starting transfers between devices, exchange(): far = lax.ppermute(to_outer, 'region', outer)  6.46 us
    pallas_call x1, Pallas kernels, on_device(): pl.pallas_call(forward_kernel, out_shape=(table_shape, colour_shape, resu...  5.56 us
    pallas_call x1, Pallas kernels, on_device(): pl.pallas_call(backward_edge_kernel, out_shape=(result_shape, jax.ShapeDt...  4.73 us
    pallas_call x1, Pallas kernels, on_device(): pl.pallas_call(backward_kernel, out_shape=jax.ShapeDtypeStruct((9, own_bl...  4.64 us
    ppermute x2, starting transfers between devices, exchange(): return (lax.ppermute(to_inner, 'region', inner), far)  3.93 us
    pallas_call x1, Pallas kernels, on_device(): pl.pallas_call(forward_edge_kernel, out_shape=(table_shape, colour_shape,...  2.25 us
  transfers between devices with their start and end apart: 4, of which 0 were waited for; matrix products, arithmetic and copies ran while one was open for 0% of the time, Pallas kernels for 19%

profile of v4, /device:TPU:1, one launch (start us, length us, event | category | flops | bytes accessed | tf_op | source)
XLA Modules:
  0.0 52.4 jit_solution(5874734626892458785)
XLA Ops:
  0.6 0.8 %slice_select_fusion = (f32[59,128]{1,0:T(8,128)S(1)}, f32[59,128]{1,0:T(8,128)S(1)}) fusion(f32[59,1024]{1,0:T(8,128)} %params_ref.1, pred[]{:T(512)S(6)} %eq.5), kind=kLoop, calls=%fused_computation | loop fusion | flops 15104 | bytes 120833 | tf_op jit(solution)/shard_map/jit(_where)/select_n | solution.py:803
  1.4 4.5 %collective-permute-start.1 = (f32[59,128]{1,0:T(8,128)S(1)}, f32[59,128]{1,0:T(8,128)S(1)}, u32[]{:S(2)}, u32[]{:S(2)}) collective-permute-start(f32[59,128]{1,0:T(8,128)S(1)} %get-tuple-element.28), channel_id=1, source_target_pairs={{8,16},{16,8},{9,17},{17,9},{10,18},{18,10},{11,19},{19,11},{12,20... | collective-permute-start | bytes 90632 | tf_op jit(solution)/shard_map/ppermute | solution.py:782
  5.9 0.1 collective-permute-start
  6.0 5.6 %forward.1 = (bf16[1408,48]{1,0:T(8,128)(2,1)S(1)}, bf16[11,16,128]{2,1,0:T(8,128)(2,1)S(1)}, f32[528,128]{1,0:T(8,128)S(1)}, bf16[32,32,256]{2,1,0:T(8,128)(2,1...) custom-call(s32[2,32]{1,0:T(2,128)} %bitcast.7, s32[1,32]{1,0:T(1,128)} %far_live_ref.1, f32[59,1024]{1,0:T(8,128)} %params_ref.1, ...), custom_call_target="tpu_custom_call" | custom-call | tf_op jit(solution)/shard_map/forward/pallas_call | solution.py:823
  11.6 0.0 collective-permute-done.1.outer_ref
  11.6 0.0 collective-permute-done.inner_ref
  11.6 2.2 %forward_edge.1 = (bf16[1408,48]{1,0:T(8,128)(2,1)S(1)}, bf16[11,16,128]{2,1,0:T(8,128)(2,1)S(1)}, f32[528,128]{1,0:T(8,128)S(1)}, f32[8,40,128]{2,1,0:T(8,128)S(1)}) custom-call(s32[244]{0:T(256)S(1)} %get-tuple-element.16.items_ref, f32[59,128]{1,0:T(8,128)S(1)} %collective-permute-done.inner_ref, ...), custom_call_target="tpu_custom_call", output_to_operand_aliasing={{0}: (5, {}), {1}: (6, {}), {2}: (7, {})} | custom-call | tf_op jit(solution)/shard_map/forward_edge/pallas_call | solution.py:861
  13.8 0.0 copy-start.3
  13.9 11.8 %all_to_all.10.arrived_ref = f32[8,40,128]{2,1,0:T(8,128)S(1)} all-to-all(f32[8,40,128]{2,1,0:T(8,128)S(1)} %get-tuple-element.23), channel_id=1, replica_groups=mesh['region'=4,'dom'=8] {'dom'}, dimensions={0} | all-to-all | bytes 327680 | tf_op jit(solution)/shard_map/all_to_all | solution.py:885
  25.6 0.0 copy-done.3
  25.6 1.5 %composite.1 = f32[8,32,128]{2,1,0:T(8,128)S(1)} custom-call(f32[3]{0:T(128)S(1)} %copy-done.3, f32[8,40,128]{2,1,0:T(8,128)S(1)} %all_to_all.10.arrived_ref), custom_call_target="tpu_custom_call" | custom-call | tf_op jit(solution)/shard_map/composite/pallas_call | solution.py:886
  27.2 8.6 %all_to_all.11.back_ref = f32[8,32,128]{2,1,0:T(8,128)S(1)} all-to-all(f32[8,32,128]{2,1,0:T(8,128)S(1)} %composite.1), channel_id=1, replica_groups=mesh['region'=4,'dom'=8] {'dom'}, dimensions={0} | all-to-all | bytes 262144 | tf_op jit(solution)/shard_map/all_to_all | solution.py:894
  35.8 4.7 %backward_edge.1 = (f32[528,128]{1,0:T(8,128)S(1)}, f32[384,128]{1,0:T(8,128)S(1)}, f32[16,128]{1,0:T(8,128)S(1)}, f32[16,128]{1,0:T(8,128)S(1)}) custom-call(s32[244]{0:T(256)S(1)} %get-tuple-element.16.items_ref, f32[8,32,128]{2,1,0:T(8,128)S(1)} %all_to_all.11.back_ref, bf16[1408,48]{1,0:T(8,128)(2,1)S(1)} %get-tuple-element.22.table_ref, ...), custom_call_target="tpu_custom_call" | custom-call | tf_op jit(solution)/shard_map/backward_edge/pallas_call | solution.py:895
  40.5 3.9 %collective-permute-start.2 = (f32[16,128]{1,0:T(8,128)S(1)}, f32[16,128]{1,0:T(8,128)S(1)}, u32[]{:S(2)}, u32[]{:S(2)}) collective-permute-start(f32[16,128]{1,0:T(8,128)S(1)} %get-tuple-element.26), channel_id=1, source_target_pairs={{0,8},{8,0},{16,24},{24,16},{1,9},{9,1},{17,25},{25,17},{2,10},{10... | collective-permute-start | bytes 24584 | tf_op jit(solution)/shard_map/ppermute | solution.py:783
  44.4 2.0 %collective-permute-start.3 = (f32[16,128]{1,0:T(8,128)S(1)}, f32[16,128]{1,0:T(8,128)S(1)}, u32[]{:S(2)}, u32[]{:S(2)}) collective-permute-start(f32[16,128]{1,0:T(8,128)S(1)} %get-tuple-element.27), channel_id=1, source_target_pairs={{8,16},{16,8},{9,17},{17,9},{10,18},{18,10},{11,19},{19,11},{12,20... | collective-permute-start | bytes 24584 | tf_op jit(solution)/shard_map/ppermute | solution.py:782
  46.3 0.0 copy-start
  46.4 0.0 copy-start.1
  46.4 0.0 copy-start.2
  46.4 4.6 %backward.1.own_ref = f32[9,8,128]{2,1,0:T(8,128)S(1)} custom-call(s32[244]{0:T(256)S(1)} %get-tuple-element.16.items_ref, bf16[1408,48]{1,0:T(8,128)(2,1)S(1)} %get-tuple-element.22.table_ref, bf16[32,32,256]{2,1,0:T(8,128)(2,1)S(1)} %get-tuple-element.18.basis_ref, f32[528,128]{1,0:T(8,128)S(1)} %get-tuple-element.24.grad_ref, ...), custom_call_target="tpu_custom_call" | custom-call | tf_op jit(solution)/shard_map/backward/pallas_call | solution.py:910
  51.0 0.0 collective-permute-done.2.inner_ref
  51.0 0.0 collective-permute-done.3.outer_ref
  51.0 0.0 copy-done
  51.0 0.0 copy-done.1
  51.1 0.0 copy-done.2
  51.1 1.4 %update.1 = (f32[59,1024]{1,0:T(8,128)}, f32[59,1024]{1,0:T(8,128)}, f32[59,1024]{1,0:T(8,128)}, f32[59,1024]{1,0:T(8,128)}) custom-call(f32[59,1024]{1,0:T(8,128)S(1)} %copy-done, f32[59,1024]{1,0:T(8,128)S(1)} %copy-done.1, f32[59,1024]{1,0:T(8,128)S(1)} %copy-done.2, f32[9,8,128]{2,1,0:T(8,128)S(1)} %backward.1.own_ref, ...), custom_call_target="tpu_custom_call" | custom-call | tf_op jit(solution)/shard_map/update/pallas_call | solution.py:920
Async XLA Ops:
  1.4 10.1 %collective-permute-start.1 = (f32[59,128]{1,0:T(8,128)S(1)}, f32[59,128]{1,0:T(8,128)S(1)}, u32[]{:S(2)}, u32[]{:S(2)}) collective-permute-start(f32[59,128]{1,0:T(8,128)S(1)} %get-tuple-element.28), channel_id=1, source_target_pairs={{8,16},{16,8},{9,17},{17,9},{10,18},{18,10},{11,19},{19,11},{12,20... | collective-permute-start | bytes 90632 | tf_op jit(solution)/shard_map/ppermute | solution.py:782
  5.9 5.7 %collective-permute-start = (f32[59,128]{1,0:T(8,128)S(1)}, f32[59,128]{1,0:T(8,128)S(1)}, u32[]{:S(2)}, u32[]{:S(2)}) collective-permute-start(f32[59,128]{1,0:T(8,128)S(1)} %get-tuple-element.29), channel_id=1, source_target_pairs={{0,8},{8,0},{16,24},{24,16},{1,9},{9,1},{17,25},{25,17},{2,10},{10... | collective-permute-start | bytes 90632 | tf_op jit(solution)/shard_map/ppermute | solution.py:783
  13.8 11.8 %copy-start.3 = (f32[3]{0:T(128)S(1)}, f32[3]{0:T(128)}, u32[]{:S(2)}) copy-start(f32[3]{0:T(128)} %background_ref.1) | copy-start | bytes 40
  40.5 10.5 %collective-permute-start.2 = (f32[16,128]{1,0:T(8,128)S(1)}, f32[16,128]{1,0:T(8,128)S(1)}, u32[]{:S(2)}, u32[]{:S(2)}) collective-permute-start(f32[16,128]{1,0:T(8,128)S(1)} %get-tuple-element.26), channel_id=1, source_target_pairs={{0,8},{8,0},{16,24},{24,16},{1,9},{9,1},{17,25},{25,17},{2,10},{10... | collective-permute-start | bytes 24584 | tf_op jit(solution)/shard_map/ppermute | solution.py:783
  44.4 6.7 %collective-permute-start.3 = (f32[16,128]{1,0:T(8,128)S(1)}, f32[16,128]{1,0:T(8,128)S(1)}, u32[]{:S(2)}, u32[]{:S(2)}) collective-permute-start(f32[16,128]{1,0:T(8,128)S(1)} %get-tuple-element.27), channel_id=1, source_target_pairs={{8,16},{16,8},{9,17},{17,9},{10,18},{18,10},{11,19},{19,11},{12,20... | collective-permute-start | bytes 24584 | tf_op jit(solution)/shard_map/ppermute | solution.py:782
  46.3 4.7 %copy-start = (f32[59,1024]{1,0:T(8,128)S(1)}, f32[59,1024]{1,0:T(8,128)}, u32[]{:S(2)}) copy-start(f32[59,1024]{1,0:T(8,128)} %params_ref.1) | copy-start | bytes 724996
  46.4 4.7 %copy-start.1 = (f32[59,1024]{1,0:T(8,128)S(1)}, f32[59,1024]{1,0:T(8,128)}, u32[]{:S(2)}) copy-start(f32[59,1024]{1,0:T(8,128)} %first_ref.1) | copy-start | bytes 724996
  46.4 4.7 %copy-start.2 = (f32[59,1024]{1,0:T(8,128)S(1)}, f32[59,1024]{1,0:T(8,128)}, u32[]{:S(2)}) copy-start(f32[59,1024]{1,0:T(8,128)} %second_ref.1) | copy-start | bytes 724996

commit v5 on v4

--- a/solution.py
+++ b/solution.py
@@ -269,7 +269,14 @@
         front(last, further, 0)
         return last, slots_of(2 * pair + 3), slots_of(2 * pair + 4)
 
-    lax.fori_loop(begin, end, step, (first, slots_of(2 * begin + 1), slots_of(2 * begin + 2)))
+    def two_steps(double, carry):
+        pair = begin + 2 * double
+        return step(pair + 1, step(pair, carry))
+
+    doubles = (end - begin) // 2
+    carry = (first, slots_of(2 * begin + 1), slots_of(2 * begin + 2))
+    carry = lax.fori_loop(0, doubles, two_steps, carry)
+    lax.fori_loop(begin + 2 * doubles, end, step, carry)
 
 
 def block_rows(block):
@@ -410,10 +417,9 @@
     ]
     for fetch in fetches:
         fetch.start()
-    fetches[0].wait()
-    fetches[1].wait()
+    for fetch in fetches[:3]:
+        fetch.wait()
     list_items(blocks_ref, live_ref, items_ref, pieces, own_blocks)
-    fetches[2].wait()
     for block in range(own_blocks):
         rows_ref[pl.ds(block, PARAMS, stride=SUBL), :] = params_ref[
             :, block * BLOCK : (block + 1) * BLOCK
@@ -779,8 +785,9 @@
     inner = [(i, i ^ 1) for i in range(count) if (i ^ 1) < count]
     outer = [(i, i + 1) for i in range(1, count - 1, 2)]
     outer += [(target, source) for source, target in outer]
+    near = lax.ppermute(to_inner, "region", inner)
     far = lax.ppermute(to_outer, "region", outer)
-    return lax.ppermute(to_inner, "region", inner), far
+    return near, far
 
 
 def on_device(

time: 52.7 us -> 52 us (0.987)
  Pallas kernels: 20.1 us -> 17.8 us
  starting transfers between devices: 10.4 us -> 11.9 us
    ppermute x2, starting transfers between devices: 6.46 us -> 7.8 us  [exchange(): far = lax.ppermute(to_outer, 'region', outer)]
    pallas_call x1, Pallas kernels: 4.64 us -> 3.69 us  [on_device(): pl.pallas_call(backward_kernel, out_shape=jax.ShapeDtypeStruct((9, own_bl...]
  transfers between devices with their start and end apart: 4 -> 4, of which waited for: 0 -> 0; matrix products, arithmetic and copies ran while one was open for 0% -> 0% of each run, Pallas kernels for 19% -> 17%
where the time goes in v5:
time: 52 us; the launch traced here: 51.7 us
  blocking collectives  20.5 us (39%)
  Pallas kernels  17.8 us (34%)
  starting transfers between devices  11.9 us (23%)
  other arithmetic  0.78 us (2%)
  between operations  0.77 us (1%)
    all_to_all x1, blocking collectives, on_device(): lax.all_to_all(payload, 'dom', split_axis=0, concat_axis=0, tiled=True)  11.8 us
    all_to_all x1, blocking collectives, on_device(): lax.all_to_all(back, 'dom', split_axis=0, concat_axis=0, tiled=True)  8.69 us
    ppermute x2, starting transfers between devices, exchange(): far = lax.ppermute(to_outer, 'region', outer)  7.8 us
    pallas_call x1, Pallas kernels, on_device(): pl.pallas_call(forward_kernel, out_shape=(table_shape, colour_shape, resu...  5.09 us
    pallas_call x1, Pallas kernels, on_device(): pl.pallas_call(backward_edge_kernel, out_shape=(result_shape, jax.ShapeDt...  4.34 us
    ppermute x2, starting transfers between devices, exchange(): near = lax.ppermute(to_inner, 'region', inner)  4.08 us
    pallas_call x1, Pallas kernels, on_device(): pl.pallas_call(backward_kernel, out_shape=jax.ShapeDtypeStruct((9, own_bl...  3.69 us
    pallas_call x1, Pallas kernels, on_device(): pl.pallas_call(forward_edge_kernel, out_shape=(table_shape, colour_shape,...  1.79 us
  transfers between devices with their start and end apart: 4, of which 0 were waited for; matrix products, arithmetic and copies ran while one was open for 0% of the time, Pallas kernels for 17%

profile of v5, /device:TPU:1, one launch (start us, length us, event | category | flops | bytes accessed | tf_op | source)
XLA Modules:
  0.0 51.7 jit_solution(14262082189744437779)
XLA Ops:
  0.6 0.8 %slice_select_fusion = (f32[59,128]{1,0:T(8,128)S(1)}, f32[59,128]{1,0:T(8,128)S(1)}) fusion(f32[59,1024]{1,0:T(8,128)} %params_ref.1, pred[]{:T(512)S(6)} %eq.5), kind=kLoop, calls=%fused_computation | loop fusion | flops 15104 | bytes 120833 | tf_op jit(solution)/shard_map/jit(_where)/select_n | solution.py:810
  1.4 4.5 %collective-permute-start.1 = (f32[59,128]{1,0:T(8,128)S(1)}, f32[59,128]{1,0:T(8,128)S(1)}, u32[]{:S(2)}, u32[]{:S(2)}) collective-permute-start(f32[59,128]{1,0:T(8,128)S(1)} %get-tuple-element.28), channel_id=1, source_target_pairs={{8,16},{16,8},{9,17},{17,9},{10,18},{18,10},{11,19},{19,11},{12,20... | collective-permute-start | bytes 90632 | tf_op jit(solution)/shard_map/ppermute | solution.py:789
  5.9 0.1 collective-permute-start
  6.0 5.1 %forward.1 = (bf16[1408,48]{1,0:T(8,128)(2,1)S(1)}, bf16[11,16,128]{2,1,0:T(8,128)(2,1)S(1)}, f32[528,128]{1,0:T(8,128)S(1)}, bf16[32,32,256]{2,1,0:T(8,128)(2,1...) custom-call(s32[2,32]{1,0:T(2,128)} %bitcast.7, s32[1,32]{1,0:T(1,128)} %far_live_ref.1, f32[59,1024]{1,0:T(8,128)} %params_ref.1, ...), custom_call_target="tpu_custom_call" | custom-call | tf_op jit(solution)/shard_map/forward/pallas_call | solution.py:830
  11.1 0.0 collective-permute-done.1.outer_ref
  11.1 0.0 collective-permute-done.inner_ref
  11.1 1.8 %forward_edge.1 = (bf16[1408,48]{1,0:T(8,128)(2,1)S(1)}, bf16[11,16,128]{2,1,0:T(8,128)(2,1)S(1)}, f32[528,128]{1,0:T(8,128)S(1)}, f32[8,40,128]{2,1,0:T(8,128)S(1)}) custom-call(s32[244]{0:T(256)S(1)} %get-tuple-element.16.items_ref, f32[59,128]{1,0:T(8,128)S(1)} %collective-permute-done.inner_ref, ...), custom_call_target="tpu_custom_call", output_to_operand_aliasing={{0}: (5, {}), {1}: (6, {}), {2}: (7, {})} | custom-call | tf_op jit(solution)/shard_map/forward_edge/pallas_call | solution.py:868
  12.9 0.0 copy-start.3
  12.9 11.8 %all_to_all.10.arrived_ref = f32[8,40,128]{2,1,0:T(8,128)S(1)} all-to-all(f32[8,40,128]{2,1,0:T(8,128)S(1)} %get-tuple-element.23), channel_id=1, replica_groups=mesh['region'=4,'dom'=8] {'dom'}, dimensions={0} | all-to-all | bytes 327680 | tf_op jit(solution)/shard_map/all_to_all | solution.py:892
  24.7 0.0 copy-done.3
  24.7 1.6 %composite.1 = f32[8,32,128]{2,1,0:T(8,128)S(1)} custom-call(f32[3]{0:T(128)S(1)} %copy-done.3, f32[8,40,128]{2,1,0:T(8,128)S(1)} %all_to_all.10.arrived_ref), custom_call_target="tpu_custom_call" | custom-call | tf_op jit(solution)/shard_map/composite/pallas_call | solution.py:893
  26.2 8.7 %all_to_all.11.back_ref = f32[8,32,128]{2,1,0:T(8,128)S(1)} all-to-all(f32[8,32,128]{2,1,0:T(8,128)S(1)} %composite.1), channel_id=1, replica_groups=mesh['region'=4,'dom'=8] {'dom'}, dimensions={0} | all-to-all | bytes 262144 | tf_op jit(solution)/shard_map/all_to_all | solution.py:901
  34.9 4.3 %backward_edge.1 = (f32[528,128]{1,0:T(8,128)S(1)}, f32[384,128]{1,0:T(8,128)S(1)}, f32[16,128]{1,0:T(8,128)S(1)}, f32[16,128]{1,0:T(8,128)S(1)}) custom-call(s32[244]{0:T(256)S(1)} %get-tuple-element.16.items_ref, f32[8,32,128]{2,1,0:T(8,128)S(1)} %all_to_all.11.back_ref, bf16[1408,48]{1,0:T(8,128)(2,1)S(1)} %get-tuple-element.22.table_ref, ...), custom_call_target="tpu_custom_call" | custom-call | tf_op jit(solution)/shard_map/backward_edge/pallas_call | solution.py:902
  39.3 4.0 %collective-permute-start.2 = (f32[16,128]{1,0:T(8,128)S(1)}, f32[16,128]{1,0:T(8,128)S(1)}, u32[]{:S(2)}, u32[]{:S(2)}) collective-permute-start(f32[16,128]{1,0:T(8,128)S(1)} %get-tuple-element.26), channel_id=1, source_target_pairs={{0,8},{8,0},{16,24},{24,16},{1,9},{9,1},{17,25},{25,17},{2,10},{10... | collective-permute-start | bytes 24584 | tf_op jit(solution)/shard_map/ppermute | solution.py:788
  43.3 3.3 %collective-permute-start.3 = (f32[16,128]{1,0:T(8,128)S(1)}, f32[16,128]{1,0:T(8,128)S(1)}, u32[]{:S(2)}, u32[]{:S(2)}) collective-permute-start(f32[16,128]{1,0:T(8,128)S(1)} %get-tuple-element.27), channel_id=1, source_target_pairs={{8,16},{16,8},{9,17},{17,9},{10,18},{18,10},{11,19},{19,11},{12,20... | collective-permute-start | bytes 24584 | tf_op jit(solution)/shard_map/ppermute | solution.py:789
  46.6 0.0 copy-start
  46.6 0.0 copy-start.1
  46.6 0.0 copy-start.2
  46.7 3.7 %backward.1.own_ref = f32[9,8,128]{2,1,0:T(8,128)S(1)} custom-call(s32[244]{0:T(256)S(1)} %get-tuple-element.16.items_ref, bf16[1408,48]{1,0:T(8,128)(2,1)S(1)} %get-tuple-element.22.table_ref, bf16[32,32,256]{2,1,0:T(8,128)(2,1)S(1)} %get-tuple-element.18.basis_ref, f32[528,128]{1,0:T(8,128)S(1)} %get-tuple-element.24.grad_ref, ...), custom_call_target="tpu_custom_call" | custom-call | tf_op jit(solution)/shard_map/backward/pallas_call | solution.py:917
  50.3 0.0 collective-permute-done.2.inner_ref
  50.3 0.0 collective-permute-done.3.outer_ref
  50.4 0.0 copy-done
  50.4 0.0 copy-done.1
  50.4 0.0 copy-done.2
  50.4 1.4 %update.1 = (f32[59,1024]{1,0:T(8,128)}, f32[59,1024]{1,0:T(8,128)}, f32[59,1024]{1,0:T(8,128)}, f32[59,1024]{1,0:T(8,128)}) custom-call(f32[59,1024]{1,0:T(8,128)S(1)} %copy-done, f32[59,1024]{1,0:T(8,128)S(1)} %copy-done.1, f32[59,1024]{1,0:T(8,128)S(1)} %copy-done.2, f32[9,8,128]{2,1,0:T(8,128)S(1)} %backward.1.own_ref, ...), custom_call_target="tpu_custom_call" | custom-call | tf_op jit(solution)/shard_map/update/pallas_call | solution.py:927
Async XLA Ops:
  1.4 9.7 %collective-permute-start.1 = (f32[59,128]{1,0:T(8,128)S(1)}, f32[59,128]{1,0:T(8,128)S(1)}, u32[]{:S(2)}, u32[]{:S(2)}) collective-permute-start(f32[59,128]{1,0:T(8,128)S(1)} %get-tuple-element.28), channel_id=1, source_target_pairs={{8,16},{16,8},{9,17},{17,9},{10,18},{18,10},{11,19},{19,11},{12,20... | collective-permute-start | bytes 90632 | tf_op jit(solution)/shard_map/ppermute | solution.py:789
  5.9 5.2 %collective-permute-start = (f32[59,128]{1,0:T(8,128)S(1)}, f32[59,128]{1,0:T(8,128)S(1)}, u32[]{:S(2)}, u32[]{:S(2)}) collective-permute-start(f32[59,128]{1,0:T(8,128)S(1)} %get-tuple-element.29), channel_id=1, source_target_pairs={{0,8},{8,0},{16,24},{24,16},{1,9},{9,1},{17,25},{25,17},{2,10},{10... | collective-permute-start | bytes 90632 | tf_op jit(solution)/shard_map/ppermute | solution.py:788
  12.9 11.8 %copy-start.3 = (f32[3]{0:T(128)S(1)}, f32[3]{0:T(128)}, u32[]{:S(2)}) copy-start(f32[3]{0:T(128)} %background_ref.1) | copy-start | bytes 40
  39.3 11.1 %collective-permute-start.2 = (f32[16,128]{1,0:T(8,128)S(1)}, f32[16,128]{1,0:T(8,128)S(1)}, u32[]{:S(2)}, u32[]{:S(2)}) collective-permute-start(f32[16,128]{1,0:T(8,128)S(1)} %get-tuple-element.26), channel_id=1, source_target_pairs={{0,8},{8,0},{16,24},{24,16},{1,9},{9,1},{17,25},{25,17},{2,10},{10... | collective-permute-start | bytes 24584 | tf_op jit(solution)/shard_map/ppermute | solution.py:788
  43.3 7.1 %collective-permute-start.3 = (f32[16,128]{1,0:T(8,128)S(1)}, f32[16,128]{1,0:T(8,128)S(1)}, u32[]{:S(2)}, u32[]{:S(2)}) collective-permute-start(f32[16,128]{1,0:T(8,128)S(1)} %get-tuple-element.27), channel_id=1, source_target_pairs={{8,16},{16,8},{9,17},{17,9},{10,18},{18,10},{11,19},{19,11},{12,20... | collective-permute-start | bytes 24584 | tf_op jit(solution)/shard_map/ppermute | solution.py:789
  46.6 3.7 %copy-start = (f32[59,1024]{1,0:T(8,128)S(1)}, f32[59,1024]{1,0:T(8,128)}, u32[]{:S(2)}) copy-start(f32[59,1024]{1,0:T(8,128)} %params_ref.1) | copy-start | bytes 724996
  46.6 3.7 %copy-start.1 = (f32[59,1024]{1,0:T(8,128)S(1)}, f32[59,1024]{1,0:T(8,128)}, u32[]{:S(2)}) copy-start(f32[59,1024]{1,0:T(8,128)} %first_ref.1) | copy-start | bytes 724996
  46.6 3.7 %copy-start.2 = (f32[59,1024]{1,0:T(8,128)S(1)}, f32[59,1024]{1,0:T(8,128)}, u32[]{:S(2)}) copy-start(f32[59,1024]{1,0:T(8,128)} %second_ref.1) | copy-start | bytes 724996

commit v6 on v5

--- a/solution.py
+++ b/solution.py
@@ -238,6 +238,7 @@
     room = pieces + SUBL
     size = 3 * room + 2
     edges = items_ref[2 * size - 2]
+    raw = item
     edge = item < edges
     doubles = jnp.where(edge, items_ref[size - 1], items_ref[size - 2])
     base = jnp.where(edge, size, 0)
@@ -249,7 +250,7 @@
     found = [chained.astype(jnp.int32)]
     for entry in (first, second):
         found += [entry & 63, lax.shift_right_logical(entry, 6)]
-    return tuple(found)
+    return (*found, raw)
 
 
 def pipelined(items_ref, pieces, begin, end, multiply, front, back):
@@ -321,8 +322,11 @@
         colour_ref[block] = jnp.concatenate(tiles[KT // SUBL :] * 2, axis=0).astype(bf16)
 
 
-def render_items(begin, end, items_ref, table_ref, colour_ref, basis_ref, result_ref, scratch):
+def render_items(
+    begin, end, items_ref, table_ref, colour_ref, basis_ref, result_ref, saved_refs, scratch
+):
     local_refs, before_refs, left_refs = scratch
+    alpha_all_ref, local_all_ref, ends_all_ref = saved_refs
     pieces = basis_ref.shape[0]
 
     def multiply(found):
@@ -337,12 +341,14 @@
         for slot in range(2):
             alphas = jnp.exp2(powers[slot])
             keep = None
+            alpha_all_ref[found[5], slot * BLOCK : (slot + 1) * BLOCK, :] = alphas
             for row in range(ROWS):
                 alpha = alphas[row * SUBL : (row + 1) * SUBL]
                 weight = alpha if keep is None else alpha * keep
                 keep = 1.0 - alpha if keep is None else keep - weight
                 first = slot * BLOCK + row * SUBL
                 local_refs[side][first : first + SUBL, :] = weight
+                local_all_ref[found[5], first : first + SUBL, :] = weight
             before, total = prefix_product(keep)
             if slot == 1:
                 carry = jnp.where(chained, carry, 1.0)
@@ -350,6 +356,8 @@
             carry = total
             before_refs[side][slot * SUBL : (slot + 1) * SUBL, :] = before
             left_refs[side][slot : slot + 1, :] = total
+            ends_all_ref[found[5], 2 * slot * SUBL : (2 * slot + 1) * SUBL, :] = before
+            ends_all_ref[found[5], (2 * slot + 1) * SUBL : (2 * slot + 2) * SUBL, :] = keep
 
     def back(found, side):
         chained = found[0] > 0
@@ -389,6 +397,9 @@
     result_ref,
     basis_ref,
     aimed_ref,
+    alpha_all_ref,
+    local_all_ref,
+    ends_all_ref,
     items_ref,
     blocks_ref,
     live_ref,
@@ -454,7 +465,8 @@
             aimed = jnp.where(tile_lane < (channel + 1) * GROUP, value, aimed)
         aimed_ref[dom] = aimed
     edge_pairs, pairs = item_ranges(items_ref, pieces)
-    render_items(edge_pairs, pairs, items_ref, table_ref, colour_ref, basis_ref, result_ref, scratch)
+    saved = (alpha_all_ref, local_all_ref, ends_all_ref)
+    render_items(edge_pairs, pairs, items_ref, table_ref, colour_ref, basis_ref, result_ref, saved, scratch)
 
 
 def forward_edge_kernel(
@@ -463,18 +475,10 @@
     outer_ref,
     aimed_ref,
     basis_ref,
-    table_in_ref,
-    colour_in_ref,
-    result_in_ref,
-    table_ref,
-    colour_ref,
-    result_ref,
-    out_ref,
-    rows_ref,
-    stage_ref,
-    *scratch,
+    *refs,
 ):
-    del table_in_ref, colour_in_ref, result_in_ref
+    table_ref, colour_ref, result_ref, *saved, out_ref, rows_ref, stage_ref = refs[6:15]
+    scratch = refs[15:]
     doms, pieces = out_ref.shape[0], basis_ref.shape[0]
     own_blocks = table_ref.shape[0] // BLOCK - 3
     region_idx, regions = lax.axis_index("region"), lax.axis_size("region")
@@ -487,7 +491,7 @@
     present = ((sublane == 0) & (region_idx < regions - 1)) | ((sublane == 1) & (region_idx > 0))
     places = (own_blocks, own_blocks + 1)
     fill_tables(rows, present, places, stage_ref, table_ref, colour_ref)
-    render_items(0, item_ranges(items_ref, pieces)[0], items_ref, table_ref, colour_ref, basis_ref, result_ref, scratch)
+    render_items(0, item_ranges(items_ref, pieces)[0], items_ref, table_ref, colour_ref, basis_ref, result_ref, saved, scratch)
     width = PIX // doms
     lane = lax.broadcasted_iota(jnp.int32, (pieces, LANES), 1)
     tiles = aimed_ref.shape[1]
@@ -530,9 +534,10 @@
     to_pieces = jnp.where(cell_no == upright[:, :1], 1.0, 0.0).astype(bf16)
 
     def moved(matrix, values):
-        triple = jnp.concatenate([part.astype(bf16) for part in split3(values)], axis=1)
-        wide = jnp.dot(matrix, triple, preferred_element_type=f32)
-        return wide[:, :LANES] + wide[:, LANES : 2 * LANES] + wide[:, 2 * LANES :]
+        wide = jnp.dot(
+            matrix, jnp.concatenate(split2(values), axis=1), preferred_element_type=f32
+        )
+        return wide[:, :LANES] + wide[:, LANES:]
 
     data = arrived_ref[:, :pieces, :].reshape(all_pieces, LANES)
     cells = moved(to_cells, data)
@@ -572,8 +577,11 @@
     out_ref[...] = back.reshape(out_ref.shape)
 
 
-def pull_items(begin, end, items_ref, table_ref, basis_ref, grad_ref, sums_ref, scratch):
-    alpha_refs, shade_refs, local_refs, before_refs, hidden_refs = scratch
+def pull_items(
+    begin, end, items_ref, table_ref, basis_ref, grad_ref, sums_ref, saved_refs, scratch
+):
+    shade_refs, hidden_refs = scratch
+    alpha_all_ref, local_all_ref, ends_all_ref = saved_refs
     pieces = basis_ref.shape[0]
 
     def grads_of(piece):
@@ -595,32 +603,23 @@
             rhs = jnp.concatenate([first, second], axis=0).astype(bf16)
             rhs = jnp.concatenate([jnp.zeros((KE, PIX), bf16), rhs], axis=0)
             shades = jnp.dot(table_ref[block_rows(block), :], rhs, preferred_element_type=f32)
-            powers = exponents(table_ref, basis_ref, piece, block, pieces)
-            products.append((powers, shades, grads[3:4]))
+            products.append((shades, grads[3:4]))
         return products
 
     def front(found, products, side):
-        chained = found[0] > 0
-        carry, ends = None, []
-        for slot, (powers, shades, final) in enumerate(products):
-            alphas = jnp.exp2(powers)
+        chained, item = found[0] > 0, found[5]
+        ends = []
+        for slot, (shades, final) in enumerate(products):
             span = slice(slot * BLOCK, (slot + 1) * BLOCK)
-            alpha_refs[side][span, :] = alphas
             shade_refs[side][span, :] = shades
-            keep, total = None, None
+            total = None
             for row in range(ROWS):
-                alpha = alphas[row * SUBL : (row + 1) * SUBL]
-                weight = alpha if keep is None else alpha * keep
-                keep = 1.0 - alpha if keep is None else keep - weight
-                value = weight * shades[row * SUBL : (row + 1) * SUBL]
+                first = slot * BLOCK + row * SUBL
+                value = local_all_ref[item, first : first + SUBL, :] * shades[
+                    row * SUBL : (row + 1) * SUBL
+                ]
                 total = value if total is None else total + value
-                first = slot * BLOCK + row * SUBL
-                local_refs[side][first : first + SUBL, :] = weight
-            before, whole = prefix_product(keep)
-            if slot == 1:
-                before = before * jnp.where(chained, carry, 1.0)
-            carry = whole
-            before_refs[side][slot * SUBL : (slot + 1) * SUBL, :] = before
+            keep = ends_all_ref[item, (2 * slot + 1) * SUBL : (2 * slot + 2) * SUBL, :]
             ends.append((total, keep, final))
         behind = None
         for slot in (1, 0):
@@ -633,17 +632,17 @@
         along = (((1,), (1,)), ((), ()))
         for slot in range(2):
             piece, block = found[1 + 2 * slot], found[2 + 2 * slot]
-            before = before_refs[side][slot * SUBL : (slot + 1) * SUBL, :]
+            before = ends_all_ref[found[5], 2 * slot * SUBL : (2 * slot + 1) * SUBL, :]
             hidden = hidden_refs[side][slot * SUBL : (slot + 1) * SUBL, :]
             pulls, weights = [None] * ROWS, [None] * ROWS
             for row in reversed(range(ROWS)):
                 first = slot * BLOCK + row * SUBL
                 span = slice(first, first + SUBL)
-                weight = local_refs[side][span, :] * before
+                weight = local_all_ref[found[5], span, :] * before
                 gap = shade_refs[side][span, :] - hidden
                 weights[row] = weight
                 pulls[row] = weight * gap
-                hidden = hidden + alpha_refs[side][span, :] * gap
+                hidden = hidden + alpha_all_ref[found[5], span, :] * gap
             unit = basis_ref[jnp.minimum(piece, pieces - 1)][:TOP]
             _, first, second = grads_of(piece)
             g_lhs = jnp.concatenate([first, second], axis=0).astype(bf16)
@@ -685,6 +684,9 @@
     back_ref,
     table_ref,
     basis_ref,
+    alpha_all_ref,
+    local_all_ref,
+    ends_all_ref,
     grad_ref,
     sums_ref,
     inner_ref,
@@ -710,7 +712,8 @@
             grad_ref[pl.ds(first, pieces, stride=SUBL), :] = gathered
 
     early, _ = early_pairs(items_ref, pieces)
-    pull_items(0, early, items_ref, table_ref, basis_ref, grad_ref, sums_ref, scratch)
+    saved = (alpha_all_ref, local_all_ref, ends_all_ref)
+    pull_items(0, early, items_ref, table_ref, basis_ref, grad_ref, sums_ref, saved, scratch)
     even = lax.axis_index("region") % 2 == 0
     inner_ref[...] = jnp.zeros_like(inner_ref)
     outer_ref[...] = jnp.zeros_like(outer_ref)
@@ -722,11 +725,14 @@
 
 
 def backward_kernel(
-    items_ref, table_ref, basis_ref, grad_ref, edge_sums_ref, own_ref, sums_ref, *scratch
+    items_ref, table_ref, basis_ref, grad_ref, edge_sums_ref, *refs
 ):
+    saved, own_ref, sums_ref, scratch = refs[:3], refs[3], refs[4], refs[5:]
     sums_ref[...] = edge_sums_ref[...]
     early, pairs = early_pairs(items_ref, basis_ref.shape[0])
-    pull_items(early, pairs, items_ref, table_ref, basis_ref, grad_ref, sums_ref, scratch)
+    pull_items(
+        early, pairs, items_ref, table_ref, basis_ref, grad_ref, sums_ref, saved, scratch
+    )
     for term_no, value in enumerate(summed_terms(sums_ref)):
         own_ref[term_no] = value[: own_ref.shape[1]]
 
@@ -825,9 +831,13 @@
         [strip] * 2,
         [strip] * 2,
     ]
-    backward_scratch = [[plane] * 2, [plane] * 2, [plane] * 2, [strip] * 2, [strip] * 2]
+    backward_scratch = [[plane] * 2, [strip] * 2]
+    saved_shapes = tuple(
+        jax.ShapeDtypeStruct((pieces + 4, rows, PIX), f32)
+        for rows in (2 * BLOCK, 2 * BLOCK, 4 * SUBL)
+    )
     params_limit = pltpu.CompilerParams(vmem_limit_bytes=vmem_limit)
-    table, colour, result, basis, aimed, items = pl.pallas_call(
+    table, colour, result, basis, aimed, *saved, items = pl.pallas_call(
         forward_kernel,
         out_shape=(
             table_shape,
@@ -835,10 +845,11 @@
             result_shape,
             jax.ShapeDtypeStruct(basis.shape, bf16),
             jax.ShapeDtypeStruct((doms, tiles, LANES), f32),
+            *saved_shapes,
             jax.ShapeDtypeStruct((2 * (3 * (pieces + SUBL) + 2),), jnp.int32),
         ),
         in_specs=[pl.BlockSpec(memory_space=pltpu.HBM)] * 7,
-        out_specs=(vmem,) * 5 + (smem,),
+        out_specs=(vmem,) * 8 + (smem,),
         scratch_shapes=[
             pltpu.SMEM((2, pieces), jnp.int32),
             pltpu.SMEM((1, pieces), jnp.int32),
@@ -865,18 +876,19 @@
             )
         ]
     )
-    table, _, _, payload = pl.pallas_call(
+    table, _, _, *saved, payload = pl.pallas_call(
         forward_edge_kernel,
         out_shape=(
             table_shape,
             colour_shape,
             result_shape,
+            *saved_shapes,
             jax.ShapeDtypeStruct((doms, pieces + tiles, LANES), f32),
         ),
-        in_specs=[smem] + [vmem] * 7,
-        out_specs=(vmem,) * 4,
+        in_specs=[smem] + [vmem] * 10,
+        out_specs=(vmem,) * 7,
         scratch_shapes=forward_scratch,
-        input_output_aliases={5: 0, 6: 1, 7: 2},
+        input_output_aliases={5 + i: i for i in range(6)},
         compiler_params=params_limit,
         name="forward_edge",
     )(
@@ -888,6 +900,7 @@
         table,
         colour,
         result,
+        *saved,
     )
     arrived = lax.all_to_all(payload, "dom", split_axis=0, concat_axis=0, tiled=True)
     back = pl.pallas_call(
@@ -907,22 +920,22 @@
             jax.ShapeDtypeStruct((SLOTS, LANES), f32),
             jax.ShapeDtypeStruct((SLOTS, LANES), f32),
         ),
-        in_specs=[smem] + [vmem] * 3,
+        in_specs=[smem] + [vmem] * 6,
         out_specs=(vmem,) * 4,
         scratch_shapes=backward_scratch,
         compiler_params=params_limit,
         name="backward_edge",
-    )(items, returned, table, basis)
+    )(items, returned, table, basis, *saved)
     inner, outer = exchange(to_inner, to_outer)
     own = pl.pallas_call(
         backward_kernel,
         out_shape=jax.ShapeDtypeStruct((9, own_blocks, LANES), f32),
-        in_specs=[smem] + [vmem] * 4,
+        in_specs=[smem] + [vmem] * 7,
         out_specs=vmem,
         scratch_shapes=[pltpu.VMEM(sums_shape, f32)] + backward_scratch,
         compiler_params=params_limit,
         name="backward",
-    )(items, table, basis, grads, edge_sums)
+    )(items, table, basis, grads, edge_sums, *saved)
     shape = jax.ShapeDtypeStruct(params.shape, f32)
     return pl.pallas_call(
         update_kernel,

time: 52 us -> 51.3 us (0.987)
  Pallas kernels: 17.8 us -> 17.2 us
where the time goes in v6:
time: 51.3 us; the launch traced here: 51 us
  blocking collectives  20.5 us (40%)
  Pallas kernels  17.2 us (34%)
  starting transfers between devices  11.7 us (23%)
  other arithmetic  0.78 us (2%)
  between operations  0.78 us (2%)
    all_to_all x1, blocking collectives, on_device(): lax.all_to_all(payload, 'dom', split_axis=0, concat_axis=0, tiled=True)  11.8 us
    all_to_all x1, blocking collectives, on_device(): lax.all_to_all(back, 'dom', split_axis=0, concat_axis=0, tiled=True)  8.69 us
    ppermute x2, starting transfers between devices, exchange(): far = lax.ppermute(to_outer, 'region', outer)  7.63 us
    pallas_call x1, Pallas kernels, on_device(): pl.pallas_call(forward_kernel, out_shape=(table_shape, colour_shape, resu...  5.18 us
    ppermute x2, starting transfers between devices, exchange(): near = lax.ppermute(to_inner, 'region', inner)  4.09 us
    pallas_call x1, Pallas kernels, on_device(): pl.pallas_call(backward_edge_kernel, out_shape=(result_shape, jax.ShapeDt...  3.95 us
    pallas_call x1, Pallas kernels, on_device(): pl.pallas_call(backward_kernel, out_shape=jax.ShapeDtypeStruct((9, own_bl...  3.39 us
    pallas_call x1, Pallas kernels, on_device(): pl.pallas_call(forward_edge_kernel, out_shape=(table_shape, colour_shape,...  1.83 us
  transfers between devices with their start and end apart: 4, of which 0 were waited for; matrix products, arithmetic and copies ran while one was open for 0% of the time, Pallas kernels for 17%

profile of v6, /device:TPU:1, one launch (start us, length us, event | category | flops | bytes accessed | tf_op | source)
XLA Modules:
  0.0 51.0 jit_solution(12050438667400732675)
XLA Ops:
  0.6 0.8 %slice_select_fusion = (f32[59,128]{1,0:T(8,128)S(1)}, f32[59,128]{1,0:T(8,128)S(1)}) fusion(f32[59,1024]{1,0:T(8,128)} %params_ref.1, pred[]{:T(512)S(6)} %eq.5), kind=kLoop, calls=%fused_computation | loop fusion | flops 15104 | bytes 120833 | tf_op jit(solution)/shard_map/jit(_where)/select_n | solution.py:816
  1.4 4.5 %collective-permute-start.1 = (f32[59,128]{1,0:T(8,128)S(1)}, f32[59,128]{1,0:T(8,128)S(1)}, u32[]{:S(2)}, u32[]{:S(2)}) collective-permute-start(f32[59,128]{1,0:T(8,128)S(1)} %get-tuple-element.40), channel_id=1, source_target_pairs={{8,16},{16,8},{9,17},{17,9},{10,18},{18,10},{11,19},{19,11},{12,20... | collective-permute-start | bytes 90632 | tf_op jit(solution)/shard_map/ppermute | solution.py:795
  5.9 0.1 collective-permute-start
  6.0 5.2 %forward.1 = (bf16[1408,48]{1,0:T(8,128)(2,1)S(1)}, bf16[11,16,128]{2,1,0:T(8,128)(2,1)S(1)}, f32[528,128]{1,0:T(8,128)S(1)}, bf16[32,32,256]{2,1,0:T(8,128)(2,1...) custom-call(s32[2,32]{1,0:T(2,128)} %bitcast.7, ...), custom_call_target="tpu_custom_call" | custom-call | tf_op jit(solution)/shard_map/forward/pallas_call | solution.py:840
  11.2 0.0 collective-permute-done.1.outer_ref
  11.2 0.0 collective-permute-done.inner_ref
  11.2 0.0 copy-start.3
  11.2 1.8 %forward_edge.1 = (bf16[1408,48]{1,0:T(8,128)(2,1)S(1)}, bf16[11,16,128]{2,1,0:T(8,128)(2,1)S(1)}, f32[528,128]{1,0:T(8,128)S(1)}, f32[36,256,256]{2,1,0:T(8,128...) custom-call(s32[244]{0:T(256)S(1)} %get-tuple-element.22.items_ref, ...), custom_call_target="tpu_custom_call", output_to_operand_aliasing={{0}: (5, {}), {1}: (6, {}), {2}: (7, {}), {3}: (8, {}), {4}... | custom-call | tf_op jit(solution)/shard_map/forward_edge/pallas_call | solution.py:879
  13.1 11.8 %all_to_all.10.arrived_ref = f32[8,40,128]{2,1,0:T(8,128)S(1)} all-to-all(f32[8,40,128]{2,1,0:T(8,128)S(1)} %get-tuple-element.32), channel_id=1, replica_groups=mesh['region'=4,'dom'=8] {'dom'}, dimensions={0} | all-to-all | bytes 327680 | tf_op jit(solution)/shard_map/all_to_all | solution.py:905
  24.8 0.0 copy-done.3
  24.8 1.5 %composite.1 = f32[8,32,128]{2,1,0:T(8,128)S(1)} custom-call(f32[3]{0:T(128)S(1)} %copy-done.3, f32[8,40,128]{2,1,0:T(8,128)S(1)} %all_to_all.10.arrived_ref), custom_call_target="tpu_custom_call" | custom-call | tf_op jit(solution)/shard_map/composite/pallas_call | solution.py:906
  26.3 8.7 %all_to_all.11.back_ref = f32[8,32,128]{2,1,0:T(8,128)S(1)} all-to-all(f32[8,32,128]{2,1,0:T(8,128)S(1)} %composite.1), channel_id=1, replica_groups=mesh['region'=4,'dom'=8] {'dom'}, dimensions={0} | all-to-all | bytes 262144 | tf_op jit(solution)/shard_map/all_to_all | solution.py:914
  35.0 4.0 %backward_edge.1 = (f32[528,128]{1,0:T(8,128)S(1)}, f32[384,128]{1,0:T(8,128)S(1)}, f32[16,128]{1,0:T(8,128)S(1)}, f32[16,128]{1,0:T(8,128)S(1)}) custom-call(s32[244]{0:T(256)S(1)} %get-tuple-element.22.items_ref, f32[8,32,128]{2,1,0:T(8,128)S(1)} %all_to_all.11.back_ref, bf16[1408,48]{1,0:T(8,128)(2,1)S(1)} %get-tuple-element.31.table_ref, ...), custom_call_target="tpu_custom_call" | custom-call | tf_op jit(solution)/shard_map/backward_edge/pallas_call | solution.py:915
  39.0 4.0 %collective-permute-start.2 = (f32[16,128]{1,0:T(8,128)S(1)}, f32[16,128]{1,0:T(8,128)S(1)}, u32[]{:S(2)}, u32[]{:S(2)}) collective-permute-start(f32[16,128]{1,0:T(8,128)S(1)} %get-tuple-element.38), channel_id=1, source_target_pairs={{0,8},{8,0},{16,24},{24,16},{1,9},{9,1},{17,25},{25,17},{2,10},{10... | collective-permute-start | bytes 24584 | tf_op jit(solution)/shard_map/ppermute | solution.py:794
  43.0 3.1 %collective-permute-start.3 = (f32[16,128]{1,0:T(8,128)S(1)}, f32[16,128]{1,0:T(8,128)S(1)}, u32[]{:S(2)}, u32[]{:S(2)}) collective-permute-start(f32[16,128]{1,0:T(8,128)S(1)} %get-tuple-element.39), channel_id=1, source_target_pairs={{8,16},{16,8},{9,17},{17,9},{10,18},{18,10},{11,19},{19,11},{12,20... | collective-permute-start | bytes 24584 | tf_op jit(solution)/shard_map/ppermute | solution.py:795
  46.2 0.0 copy-start
  46.2 0.0 copy-start.1
  46.2 0.0 copy-start.2
  46.2 3.4 %backward.1.own_ref = f32[9,8,128]{2,1,0:T(8,128)S(1)} custom-call(s32[244]{0:T(256)S(1)} %get-tuple-element.22.items_ref, bf16[1408,48]{1,0:T(8,128)(2,1)S(1)} %get-tuple-element.31.table_ref, bf16[32,32,256]{2,1,0:T(8,128)(2,1)S(1)} %get-tuple-element.24.basis_ref, f32[528,128]{1,0:T(8,128)S(1)} %get-tuple-element.36.grad_ref, ...), custom_call_target="tpu_custom_call" | custom-call | tf_op jit(solution)/shard_map/backward/pallas_call | solution.py:930
  49.6 0.0 collective-permute-done.2.inner_ref
  49.6 0.0 collective-permute-done.3.outer_ref
  49.6 0.0 copy-done
  49.6 0.0 copy-done.1
  49.6 0.0 copy-done.2
  49.6 1.4 %update.1 = (f32[59,1024]{1,0:T(8,128)}, f32[59,1024]{1,0:T(8,128)}, f32[59,1024]{1,0:T(8,128)}, f32[59,1024]{1,0:T(8,128)}) custom-call(f32[59,1024]{1,0:T(8,128)S(1)} %copy-done, f32[59,1024]{1,0:T(8,128)S(1)} %copy-done.1, f32[59,1024]{1,0:T(8,128)S(1)} %copy-done.2, f32[9,8,128]{2,1,0:T(8,128)S(1)} %backward.1.own_ref, ...), custom_call_target="tpu_custom_call" | custom-call | tf_op jit(solution)/shard_map/update/pallas_call | solution.py:940
Async XLA Ops:
  1.4 9.8 %collective-permute-start.1 = (f32[59,128]{1,0:T(8,128)S(1)}, f32[59,128]{1,0:T(8,128)S(1)}, u32[]{:S(2)}, u32[]{:S(2)}) collective-permute-start(f32[59,128]{1,0:T(8,128)S(1)} %get-tuple-element.40), channel_id=1, source_target_pairs={{8,16},{16,8},{9,17},{17,9},{10,18},{18,10},{11,19},{19,11},{12,20... | collective-permute-start | bytes 90632 | tf_op jit(solution)/shard_map/ppermute | solution.py:795
  5.9 5.3 %collective-permute-start = (f32[59,128]{1,0:T(8,128)S(1)}, f32[59,128]{1,0:T(8,128)S(1)}, u32[]{:S(2)}, u32[]{:S(2)}) collective-permute-start(f32[59,128]{1,0:T(8,128)S(1)} %get-tuple-element.41), channel_id=1, source_target_pairs={{0,8},{8,0},{16,24},{24,16},{1,9},{9,1},{17,25},{25,17},{2,10},{10... | collective-permute-start | bytes 90632 | tf_op jit(solution)/shard_map/ppermute | solution.py:794
  11.2 13.6 %copy-start.3 = (f32[3]{0:T(128)S(1)}, f32[3]{0:T(128)}, u32[]{:S(2)}) copy-start(f32[3]{0:T(128)} %background_ref.1) | copy-start | bytes 40
  39.0 10.6 %collective-permute-start.2 = (f32[16,128]{1,0:T(8,128)S(1)}, f32[16,128]{1,0:T(8,128)S(1)}, u32[]{:S(2)}, u32[]{:S(2)}) collective-permute-start(f32[16,128]{1,0:T(8,128)S(1)} %get-tuple-element.38), channel_id=1, source_target_pairs={{0,8},{8,0},{16,24},{24,16},{1,9},{9,1},{17,25},{25,17},{2,10},{10... | collective-permute-start | bytes 24584 | tf_op jit(solution)/shard_map/ppermute | solution.py:794
  43.0 6.6 %collective-permute-start.3 = (f32[16,128]{1,0:T(8,128)S(1)}, f32[16,128]{1,0:T(8,128)S(1)}, u32[]{:S(2)}, u32[]{:S(2)}) collective-permute-start(f32[16,128]{1,0:T(8,128)S(1)} %get-tuple-element.39), channel_id=1, source_target_pairs={{8,16},{16,8},{9,17},{17,9},{10,18},{18,10},{11,19},{19,11},{12,20... | collective-permute-start | bytes 24584 | tf_op jit(solution)/shard_map/ppermute | solution.py:795
  46.2 3.4 %copy-start = (f32[59,1024]{1,0:T(8,128)S(1)}, f32[59,1024]{1,0:T(8,128)}, u32[]{:S(2)}) copy-start(f32[59,1024]{1,0:T(8,128)} %params_ref.1) | copy-start | bytes 724996
  46.2 3.4 %copy-start.1 = (f32[59,1024]{1,0:T(8,128)S(1)}, f32[59,1024]{1,0:T(8,128)}, u32[]{:S(2)}) copy-start(f32[59,1024]{1,0:T(8,128)} %first_ref.1) | copy-start | bytes 724996
  46.2 3.4 %copy-start.2 = (f32[59,1024]{1,0:T(8,128)S(1)}, f32[59,1024]{1,0:T(8,128)}, u32[]{:S(2)}) copy-start(f32[59,1024]{1,0:T(8,128)} %second_ref.1) | copy-start | bytes 724996

commit v7 on v6

--- a/solution.py
+++ b/solution.py
@@ -181,16 +181,13 @@
     return before, run[SUBL - 1 :]
 
 
-def suffix_affine(total, keep, behind):
+def suffix_sum(total, behind):
     sub = lax.broadcasted_iota(jnp.int32, total.shape, 0)
-    value, gain = total, keep
+    value = total
     for step in (1, 2, 4):
-        inside = sub < SUBL - step
-        next_value = jnp.where(inside, pltpu.roll(value, SUBL - step, 0), 0.0)
-        next_gain = jnp.where(inside, pltpu.roll(gain, SUBL - step, 0), 1.0)
-        value = value + gain * next_value
-        gain = gain * next_gain
-    whole = value + gain * behind
+        later = pltpu.roll(value, SUBL - step, 0)
+        value = value + jnp.where(sub < SUBL - step, later, 0.0)
+    whole = value + behind
     after = jnp.where(sub < SUBL - 1, pltpu.roll(whole, SUBL - 1, 0), behind)
     return after, whole[:1]
 
@@ -326,7 +323,7 @@
     begin, end, items_ref, table_ref, colour_ref, basis_ref, result_ref, saved_refs, scratch
 ):
     local_refs, before_refs, left_refs = scratch
-    alpha_all_ref, local_all_ref, ends_all_ref = saved_refs
+    alpha_all_ref, weight_all_ref, ends_all_ref = saved_refs
     pieces = basis_ref.shape[0]
 
     def multiply(found):
@@ -348,7 +345,6 @@
                 keep = 1.0 - alpha if keep is None else keep - weight
                 first = slot * BLOCK + row * SUBL
                 local_refs[side][first : first + SUBL, :] = weight
-                local_all_ref[found[5], first : first + SUBL, :] = weight
             before, total = prefix_product(keep)
             if slot == 1:
                 carry = jnp.where(chained, carry, 1.0)
@@ -356,8 +352,7 @@
             carry = total
             before_refs[side][slot * SUBL : (slot + 1) * SUBL, :] = before
             left_refs[side][slot : slot + 1, :] = total
-            ends_all_ref[found[5], 2 * slot * SUBL : (2 * slot + 1) * SUBL, :] = before
-            ends_all_ref[found[5], (2 * slot + 1) * SUBL : (2 * slot + 2) * SUBL, :] = keep
+            ends_all_ref[found[5], slot * SUBL : (slot + 1) * SUBL, :] = before * keep
 
     def back(found, side):
         chained = found[0] > 0
@@ -368,7 +363,9 @@
             weights = []
             for row in range(ROWS):
                 first = slot * BLOCK + row * SUBL
-                weights.append(local_refs[side][first : first + SUBL, :] * before)
+                weight = local_refs[side][first : first + SUBL, :] * before
+                weight_all_ref[found[5], first : first + SUBL, :] = weight
+                weights.append(weight)
             high, low = split2(jnp.concatenate(weights, axis=0))
             left = colour_ref[block]
             wide = jnp.dot(left, high, preferred_element_type=f32)
@@ -398,7 +395,7 @@
     basis_ref,
     aimed_ref,
     alpha_all_ref,
-    local_all_ref,
+    weight_all_ref,
     ends_all_ref,
     items_ref,
     blocks_ref,
@@ -465,7 +462,7 @@
             aimed = jnp.where(tile_lane < (channel + 1) * GROUP, value, aimed)
         aimed_ref[dom] = aimed
     edge_pairs, pairs = item_ranges(items_ref, pieces)
-    saved = (alpha_all_ref, local_all_ref, ends_all_ref)
+    saved = (alpha_all_ref, weight_all_ref, ends_all_ref)
     render_items(edge_pairs, pairs, items_ref, table_ref, colour_ref, basis_ref, result_ref, saved, scratch)
 
 
@@ -581,7 +578,7 @@
     begin, end, items_ref, table_ref, basis_ref, grad_ref, sums_ref, saved_refs, scratch
 ):
     shade_refs, hidden_refs = scratch
-    alpha_all_ref, local_all_ref, ends_all_ref = saved_refs
+    alpha_all_ref, weight_all_ref, ends_all_ref = saved_refs
     pieces = basis_ref.shape[0]
 
     def grads_of(piece):
@@ -615,30 +612,30 @@
             total = None
             for row in range(ROWS):
                 first = slot * BLOCK + row * SUBL
-                value = local_all_ref[item, first : first + SUBL, :] * shades[
+                value = weight_all_ref[item, first : first + SUBL, :] * shades[
                     row * SUBL : (row + 1) * SUBL
                 ]
                 total = value if total is None else total + value
-            keep = ends_all_ref[item, (2 * slot + 1) * SUBL : (2 * slot + 2) * SUBL, :]
-            ends.append((total, keep, final))
+            left = ends_all_ref[item, slot * SUBL : (slot + 1) * SUBL, :]
+            ends.append((total, left, final * left[SUBL - 1 :]))
         behind = None
         for slot in (1, 0):
-            total, keep, final = ends[slot]
+            total, left, final = ends[slot]
             behind = jnp.where(chained, behind, final) if slot == 0 else final
-            hidden, behind = suffix_affine(total, keep, behind)
+            hidden, behind = suffix_sum(total, behind)
+            hidden = hidden / left
             hidden_refs[side][slot * SUBL : (slot + 1) * SUBL, :] = hidden
 
     def back(found, side):
         along = (((1,), (1,)), ((), ()))
         for slot in range(2):
             piece, block = found[1 + 2 * slot], found[2 + 2 * slot]
-            before = ends_all_ref[found[5], 2 * slot * SUBL : (2 * slot + 1) * SUBL, :]
             hidden = hidden_refs[side][slot * SUBL : (slot + 1) * SUBL, :]
             pulls, weights = [None] * ROWS, [None] * ROWS
             for row in reversed(range(ROWS)):
                 first = slot * BLOCK + row * SUBL
                 span = slice(first, first + SUBL)
-                weight = local_all_ref[found[5], span, :] * before
+                weight = weight_all_ref[found[5], span, :]
                 gap = shade_refs[side][span, :] - hidden
                 weights[row] = weight
                 pulls[row] = weight * gap
@@ -685,7 +682,7 @@
     table_ref,
     basis_ref,
     alpha_all_ref,
-    local_all_ref,
+    weight_all_ref,
     ends_all_ref,
     grad_ref,
     sums_ref,
@@ -712,7 +709,7 @@
             grad_ref[pl.ds(first, pieces, stride=SUBL), :] = gathered
 
     early, _ = early_pairs(items_ref, pieces)
-    saved = (alpha_all_ref, local_all_ref, ends_all_ref)
+    saved = (alpha_all_ref, weight_all_ref, ends_all_ref)
     pull_items(0, early, items_ref, table_ref, basis_ref, grad_ref, sums_ref, saved, scratch)
     even = lax.axis_index("region") % 2 == 0
     inner_ref[...] = jnp.zeros_like(inner_ref)
@@ -834,7 +831,7 @@
     backward_scratch = [[plane] * 2, [strip] * 2]
     saved_shapes = tuple(
         jax.ShapeDtypeStruct((pieces + 4, rows, PIX), f32)
-        for rows in (2 * BLOCK, 2 * BLOCK, 4 * SUBL)
+        for rows in (2 * BLOCK, 2 * BLOCK, 2 * SUBL)
     )
     params_limit = pltpu.CompilerParams(vmem_limit_bytes=vmem_limit)
     table, colour, result, basis, aimed, *saved, items = pl.pallas_call(

time: 51.3 us -> 51 us (level)
  no operation moved by 1% of the time
where the time goes in v7:
time: 51 us; the launch traced here: 50.7 us
  blocking collectives  20.4 us (40%)
  Pallas kernels  17 us (33%)
  starting transfers between devices  11.7 us (23%)
  other arithmetic  0.78 us (2%)
  between operations  0.78 us (2%)
    all_to_all x1, blocking collectives, on_device(): lax.all_to_all(payload, 'dom', split_axis=0, concat_axis=0, tiled=True)  11.8 us
    all_to_all x1, blocking collectives, on_device(): lax.all_to_all(back, 'dom', split_axis=0, concat_axis=0, tiled=True)  8.69 us
    ppermute x2, starting transfers between devices, exchange(): far = lax.ppermute(to_outer, 'region', outer)  7.61 us
    pallas_call x1, Pallas kernels, on_device(): pl.pallas_call(forward_kernel, out_shape=(table_shape, colour_shape, resu...  5.12 us
    ppermute x2, starting transfers between devices, exchange(): near = lax.ppermute(to_inner, 'region', inner)  4.09 us
    pallas_call x1, Pallas kernels, on_device(): pl.pallas_call(backward_edge_kernel, out_shape=(result_shape, jax.ShapeDt...  3.89 us
    pallas_call x1, Pallas kernels, on_device(): pl.pallas_call(backward_kernel, out_shape=jax.ShapeDtypeStruct((9, own_bl...  3.35 us
    pallas_call x1, Pallas kernels, on_device(): pl.pallas_call(forward_edge_kernel, out_shape=(table_shape, colour_shape,...  1.8 us
  transfers between devices with their start and end apart: 4, of which 0 were waited for; matrix products, arithmetic and copies ran while one was open for 0% of the time, Pallas kernels for 17%

profile of v7, /device:TPU:1, one launch (start us, length us, event | category | flops | bytes accessed | tf_op | source)
XLA Modules:
  0.0 50.7 jit_solution(11030614746108447471)
XLA Ops:
  0.6 0.8 %slice_select_fusion = (f32[59,128]{1,0:T(8,128)S(1)}, f32[59,128]{1,0:T(8,128)S(1)}) fusion(f32[59,1024]{1,0:T(8,128)} %params_ref.1, pred[]{:T(512)S(6)} %eq.5), kind=kLoop, calls=%fused_computation | loop fusion | flops 15104 | bytes 120833 | tf_op jit(solution)/shard_map/jit(_where)/select_n | solution.py:813
  1.4 4.5 %collective-permute-start.1 = (f32[59,128]{1,0:T(8,128)S(1)}, f32[59,128]{1,0:T(8,128)S(1)}, u32[]{:S(2)}, u32[]{:S(2)}) collective-permute-start(f32[59,128]{1,0:T(8,128)S(1)} %get-tuple-element.40), channel_id=1, source_target_pairs={{8,16},{16,8},{9,17},{17,9},{10,18},{18,10},{11,19},{19,11},{12,20... | collective-permute-start | bytes 90632 | tf_op jit(solution)/shard_map/ppermute | solution.py:792
  5.9 0.1 collective-permute-start
  6.0 5.1 %forward.1 = (bf16[1408,48]{1,0:T(8,128)(2,1)S(1)}, bf16[11,16,128]{2,1,0:T(8,128)(2,1)S(1)}, f32[528,128]{1,0:T(8,128)S(1)}, bf16[32,32,256]{2,1,0:T(8,128)(2,1...) custom-call(s32[2,32]{1,0:T(2,128)} %bitcast.7, ...), custom_call_target="tpu_custom_call" | custom-call | tf_op jit(solution)/shard_map/forward/pallas_call | solution.py:837
  11.1 0.0 collective-permute-done.1.outer_ref
  11.1 0.0 collective-permute-done.inner_ref
  11.2 0.0 copy-start.3
  11.2 1.8 %forward_edge.1 = (bf16[1408,48]{1,0:T(8,128)(2,1)S(1)}, bf16[11,16,128]{2,1,0:T(8,128)(2,1)S(1)}, f32[528,128]{1,0:T(8,128)S(1)}, f32[36,256,256]{2,1,0:T(8,128...) custom-call(s32[244]{0:T(256)S(1)} %get-tuple-element.22.items_ref, ...), custom_call_target="tpu_custom_call", output_to_operand_aliasing={{0}: (5, {}), {1}: (6, {}), {2}: (7, {}), {3}: (8, {}), {4}... | custom-call | tf_op jit(solution)/shard_map/forward_edge/pallas_call | solution.py:876
  13.0 11.8 %all_to_all.10.arrived_ref = f32[8,40,128]{2,1,0:T(8,128)S(1)} all-to-all(f32[8,40,128]{2,1,0:T(8,128)S(1)} %get-tuple-element.32), channel_id=1, replica_groups=mesh['region'=4,'dom'=8] {'dom'}, dimensions={0} | all-to-all | bytes 327680 | tf_op jit(solution)/shard_map/all_to_all | solution.py:902
  24.7 0.0 copy-done.3
  24.7 1.5 %composite.1 = f32[8,32,128]{2,1,0:T(8,128)S(1)} custom-call(f32[3]{0:T(128)S(1)} %copy-done.3, f32[8,40,128]{2,1,0:T(8,128)S(1)} %all_to_all.10.arrived_ref), custom_call_target="tpu_custom_call" | custom-call | tf_op jit(solution)/shard_map/composite/pallas_call | solution.py:903
  26.2 8.7 %all_to_all.11.back_ref = f32[8,32,128]{2,1,0:T(8,128)S(1)} all-to-all(f32[8,32,128]{2,1,0:T(8,128)S(1)} %composite.1), channel_id=1, replica_groups=mesh['region'=4,'dom'=8] {'dom'}, dimensions={0} | all-to-all | bytes 262144 | tf_op jit(solution)/shard_map/all_to_all | solution.py:911
  34.9 3.9 %backward_edge.1 = (f32[528,128]{1,0:T(8,128)S(1)}, f32[384,128]{1,0:T(8,128)S(1)}, f32[16,128]{1,0:T(8,128)S(1)}, f32[16,128]{1,0:T(8,128)S(1)}) custom-call(s32[244]{0:T(256)S(1)} %get-tuple-element.22.items_ref, f32[8,32,128]{2,1,0:T(8,128)S(1)} %all_to_all.11.back_ref, bf16[1408,48]{1,0:T(8,128)(2,1)S(1)} %get-tuple-element.31.table_ref, ...), custom_call_target="tpu_custom_call" | custom-call | tf_op jit(solution)/shard_map/backward_edge/pallas_call | solution.py:912
  38.8 4.0 %collective-permute-start.2 = (f32[16,128]{1,0:T(8,128)S(1)}, f32[16,128]{1,0:T(8,128)S(1)}, u32[]{:S(2)}, u32[]{:S(2)}) collective-permute-start(f32[16,128]{1,0:T(8,128)S(1)} %get-tuple-element.38), channel_id=1, source_target_pairs={{0,8},{8,0},{16,24},{24,16},{1,9},{9,1},{17,25},{25,17},{2,10},{10... | collective-permute-start | bytes 24584 | tf_op jit(solution)/shard_map/ppermute | solution.py:791
  42.8 3.1 %collective-permute-start.3 = (f32[16,128]{1,0:T(8,128)S(1)}, f32[16,128]{1,0:T(8,128)S(1)}, u32[]{:S(2)}, u32[]{:S(2)}) collective-permute-start(f32[16,128]{1,0:T(8,128)S(1)} %get-tuple-element.39), channel_id=1, source_target_pairs={{8,16},{16,8},{9,17},{17,9},{10,18},{18,10},{11,19},{19,11},{12,20... | collective-permute-start | bytes 24584 | tf_op jit(solution)/shard_map/ppermute | solution.py:792
  46.0 0.0 copy-start
  46.0 0.0 copy-start.1
  46.0 0.0 copy-start.2
  46.0 3.3 %backward.1.own_ref = f32[9,8,128]{2,1,0:T(8,128)S(1)} custom-call(s32[244]{0:T(256)S(1)} %get-tuple-element.22.items_ref, bf16[1408,48]{1,0:T(8,128)(2,1)S(1)} %get-tuple-element.31.table_ref, bf16[32,32,256]{2,1,0:T(8,128)(2,1)S(1)} %get-tuple-element.24.basis_ref, f32[528,128]{1,0:T(8,128)S(1)} %get-tuple-element.36.grad_ref, ...), custom_call_target="tpu_custom_call" | custom-call | tf_op jit(solution)/shard_map/backward/pallas_call | solution.py:927
  49.3 0.0 collective-permute-done.2.inner_ref
  49.3 0.0 collective-permute-done.3.outer_ref
  49.4 0.0 copy-done
  49.4 0.0 copy-done.1
  49.4 0.0 copy-done.2
  49.4 1.4 %update.1 = (f32[59,1024]{1,0:T(8,128)}, f32[59,1024]{1,0:T(8,128)}, f32[59,1024]{1,0:T(8,128)}, f32[59,1024]{1,0:T(8,128)}) custom-call(f32[59,1024]{1,0:T(8,128)S(1)} %copy-done, f32[59,1024]{1,0:T(8,128)S(1)} %copy-done.1, f32[59,1024]{1,0:T(8,128)S(1)} %copy-done.2, f32[9,8,128]{2,1,0:T(8,128)S(1)} %backward.1.own_ref, ...), custom_call_target="tpu_custom_call" | custom-call | tf_op jit(solution)/shard_map/update/pallas_call | solution.py:937
Async XLA Ops:
  1.4 9.7 %collective-permute-start.1 = (f32[59,128]{1,0:T(8,128)S(1)}, f32[59,128]{1,0:T(8,128)S(1)}, u32[]{:S(2)}, u32[]{:S(2)}) collective-permute-start(f32[59,128]{1,0:T(8,128)S(1)} %get-tuple-element.40), channel_id=1, source_target_pairs={{8,16},{16,8},{9,17},{17,9},{10,18},{18,10},{11,19},{19,11},{12,20... | collective-permute-start | bytes 90632 | tf_op jit(solution)/shard_map/ppermute | solution.py:792
  5.9 5.2 %collective-permute-start = (f32[59,128]{1,0:T(8,128)S(1)}, f32[59,128]{1,0:T(8,128)S(1)}, u32[]{:S(2)}, u32[]{:S(2)}) collective-permute-start(f32[59,128]{1,0:T(8,128)S(1)} %get-tuple-element.41), channel_id=1, source_target_pairs={{0,8},{8,0},{16,24},{24,16},{1,9},{9,1},{17,25},{25,17},{2,10},{10... | collective-permute-start | bytes 90632 | tf_op jit(solution)/shard_map/ppermute | solution.py:791
  11.2 13.6 %copy-start.3 = (f32[3]{0:T(128)S(1)}, f32[3]{0:T(128)}, u32[]{:S(2)}) copy-start(f32[3]{0:T(128)} %background_ref.1) | copy-start | bytes 40
  38.8 10.5 %collective-permute-start.2 = (f32[16,128]{1,0:T(8,128)S(1)}, f32[16,128]{1,0:T(8,128)S(1)}, u32[]{:S(2)}, u32[]{:S(2)}) collective-permute-start(f32[16,128]{1,0:T(8,128)S(1)} %get-tuple-element.38), channel_id=1, source_target_pairs={{0,8},{8,0},{16,24},{24,16},{1,9},{9,1},{17,25},{25,17},{2,10},{10... | collective-permute-start | bytes 24584 | tf_op jit(solution)/shard_map/ppermute | solution.py:791
  42.8 6.5 %collective-permute-start.3 = (f32[16,128]{1,0:T(8,128)S(1)}, f32[16,128]{1,0:T(8,128)S(1)}, u32[]{:S(2)}, u32[]{:S(2)}) collective-permute-start(f32[16,128]{1,0:T(8,128)S(1)} %get-tuple-element.39), channel_id=1, source_target_pairs={{8,16},{16,8},{9,17},{17,9},{10,18},{18,10},{11,19},{19,11},{12,20... | collective-permute-start | bytes 24584 | tf_op jit(solution)/shard_map/ppermute | solution.py:792
  46.0 3.4 %copy-start = (f32[59,1024]{1,0:T(8,128)S(1)}, f32[59,1024]{1,0:T(8,128)}, u32[]{:S(2)}) copy-start(f32[59,1024]{1,0:T(8,128)} %params_ref.1) | copy-start | bytes 724996
  46.0 3.4 %copy-start.1 = (f32[59,1024]{1,0:T(8,128)S(1)}, f32[59,1024]{1,0:T(8,128)}, u32[]{:S(2)}) copy-start(f32[59,1024]{1,0:T(8,128)} %first_ref.1) | copy-start | bytes 724996
  46.0 3.4 %copy-start.2 = (f32[59,1024]{1,0:T(8,128)S(1)}, f32[59,1024]{1,0:T(8,128)}, u32[]{:S(2)}) copy-start(f32[59,1024]{1,0:T(8,128)} %second_ref.1) | copy-start | bytes 724996
